TPU v7x, 256 devices: a whole 4x4x8 slice. The times are simulated.
256 devices in a mesh: dom: 8 (over y, z_hi), row: 32 (over z_lo, x, core).
Axes of the slice: x: 4, y: 4, z: 8 (z_hi: 2, z_lo: 4; z = z_hi * 4 + z_lo), core: 2. Of those that a mesh axis runs over, the one named last changes fastest.
Arguments:
- memory: bfloat16 [524288, 256], P(('dom', 'row')), may hold values from -5 to 5
- node_time: int32 [524288], P(('dom', 'row')), may hold values from 0 to 999
- target: int32 [4, 131072], P(None, ('dom', 'row')), may hold values from -1 to 2047
- source: int32 [4, 131072], P(None, ('dom', 'row')), may hold values from 0 to 131071, as said below
- event_time: int32 [4, 131072], P(None, ('dom', 'row')), may hold values from 1000 to 2999
- edge_feat: bfloat16 [4, 131072, 128], P(None, ('dom', 'row')), may hold values from -5 to 5
- owner_group: int32 [4], replicated, may hold values from 0 to 7
- w_message: bfloat16 [768, 256], replicated, may hold values from -0.21875 to 0.21875
- frequency: float32 [128], replicated, may hold values from 0.001 to 0.1
- phase_shift: float32 [128], replicated, may hold values from -3.140625 to 3.140625
- w_input: bfloat16 [256, 768], replicated, may hold values from -0.375 to 0.375
- w_hidden: bfloat16 [256, 768], replicated, may hold values from -0.375 to 0.375
- bias_input: float32 [768], replicated, may hold values from -3 to 3
- bias_hidden: float32 [768], replicated, may hold values from -3 to 3
Outputs:
- new_memory: bfloat16 [524288, 256], P(('dom', 'row'))
Inputs may be any that keep to these rules, and one draw needn't show every extreme that they name: `target`: -1 marks a padded event row. `source`: values under 65536 name the event's own group, the rest the owner group of the batch; in each batch, of the events of one device at most 24 have a value v < 65536 with v // 2048 equal to one given r, and at most 8 have v >= 65536 with (v - 65536) // 2048 equal to one given r; on every device and batch some r reaches 24 and some r reaches 8.
All inputs are finite; a program needn't handle non-finite values.
Results may differ from a plain program's by a relative error of at most 0.0034.
Values may be sent and summed in bfloat16 or wider, within the bound.
No kernel may reach another device: no remote copies, remote signals or barrier semaphores. Data moves between devices by JAX's collectives and lax.ppermute only.
A program may use at most 64 MiB of HBM per device.

v0:
```python
import functools

import jax
import jax.numpy as jnp
from jax import lax
from jax.experimental import pallas as pl
from jax.experimental.pallas import tpu as pltpu
from jax.sharding import PartitionSpec as P

LANES = 128
F32 = jnp.float32
BF16 = jnp.bfloat16
I32 = jnp.int32
MIB = 1024 * 1024
VMEM_MIB = dict(plan=6, codes=6, prep=8, local=8, serve=8, update=16)


def whole():
    return pl.BlockSpec(memory_space=pltpu.VMEM)


def call(kernel, out_shape, args, flops=0, name=None, specs=None, scalars=(), aliases=None):
    moved = sum(a.size * a.dtype.itemsize for a in args)
    moved += sum(o.size * o.dtype.itemsize for o in jax.tree.leaves(out_shape))
    specs = specs or {}
    return pl.pallas_call(
        kernel,
        out_shape=out_shape,
        grid_spec=pltpu.PrefetchScalarGridSpec(
            num_scalar_prefetch=len(scalars),
            grid=(1,) if scalars else (),
            in_specs=[specs.get(i, whole()) for i in range(len(args))],
            out_specs=jax.tree.map(lambda _: whole(), out_shape),
        ),
        input_output_aliases=aliases or {},
        compiler_params=pltpu.CompilerParams(vmem_limit_bytes=VMEM_MIB[name] * MIB),
        cost_estimate=pl.CostEstimate(flops=flops, bytes_accessed=moved, transcendentals=0),
        name=name,
    )(*scalars, *args)


def dot(a, b):
    return jnp.dot(a, b, preferred_element_type=F32)


def dot_nt(a, b):
    return lax.dot_general(a, b, (((1,), (1,)), ((), ())), preferred_element_type=F32)


def lane_code_f32(index_col, rows):
    lane = lax.broadcasted_iota(I32, (rows, LANES), 1)
    hit = (index_col & (LANES - 1)) == lane
    return jnp.where(hit, (index_col >> 7).astype(F32), -1.0)


def lane_code(index_col, rows):
    return lane_code_f32(index_col, rows).astype(BF16)


def expand(code, first, count):
    one = jnp.ones((), BF16)
    zero = jnp.zeros((), BF16)
    return jnp.concatenate(
        [jnp.where(code == jnp.asarray(k, BF16), one, zero) for k in range(first, first + count)],
        axis=1,
    )


def plan_kernel(cap, ocap, node_dev, source_ref, ids_ref, pcode_ref):
    batches, events = source_ref.shape
    rows = ids_ref.shape[1]
    per = cap + ocap
    group_nodes = rows * node_dev
    upper = (
        lax.broadcasted_iota(I32, (events, events), 0)
        <= lax.broadcasted_iota(I32, (events, events), 1)
    ).astype(F32).astype(BF16)
    bucket_iota = lax.broadcasted_iota(I32, (2 * rows, events), 0)
    lane_iota = lax.broadcasted_iota(I32, (LANES, events), 0)
    high = jnp.zeros((rows, LANES), F32)
    low = jnp.zeros((rows, LANES), F32)
    places = []
    for b in range(batches):
        src = source_ref[b : b + 1, :]
        far = src >= group_nodes
        local = jnp.where(far, src - group_nodes, src)
        dest = local // node_dev
        offset = local - dest * node_dev
        bucket = jnp.where(far, dest + rows, dest)
        hit = bucket == bucket_iota
        hitf = hit.astype(F32)
        running = dot(hitf.astype(BF16), upper)
        rank = jnp.sum(hitf * running, axis=0, keepdims=True).astype(I32) - 1
        slot = jnp.where(far, rank + cap, rank)
        both = (hitf[:rows] + hitf[rows:]).astype(BF16)
        spot = (slot + b * per == lane_iota).astype(F32)
        high = high + dot_nt(both, (spot * (offset >> 6).astype(F32)).astype(BF16))
        low = low + dot_nt(both, (spot * (offset & 63).astype(F32)).astype(BF16))
        places.append(dest * per + slot)
    ids = high.astype(I32) * 64 + low.astype(I32)
    for g in range(ids_ref.shape[0]):
        ids_ref[g] = ids
    stacked = jnp.concatenate(
        [p.astype(F32) for p in places] + [jnp.zeros((LANES - batches, events), F32)], axis=0
    )
    cols = stacked.T
    for b in range(batches):
        pcode_ref[b] = lane_code(cols[:, b : b + 1].astype(I32), events)


def spread_codes(ids, first, count):
    rows = ids.shape[0]
    total = rows * count
    place = lax.broadcasted_iota(I32, (total, LANES), 0)
    lane = lax.broadcasted_iota(I32, (total, LANES), 1)
    row = place // count
    copy = (row[:, :rows] == lane[:, :rows]).astype(F32).astype(BF16)
    keep = (lane == first + place - row * count).astype(F32)
    ones = jnp.ones((LANES, LANES), BF16)

    def everywhere(part):
        taken = dot(copy, part.astype(F32).astype(BF16)) * keep
        return dot(taken.astype(BF16), ones)

    low = everywhere(ids & (LANES - 1))
    high = everywhere(ids >> 7)
    return jnp.where(low == lane.astype(F32), high, -1.0).astype(BF16)


def code_kernel(cap, per, at_ref, asked_ref, _, own_ref, far_ref):
    b = at_ref[0]
    groups, rows, _ = asked_ref.shape
    own_ref[...] = spread_codes(asked_ref[at_ref[1]], b * per, per)
    block = rows * (per - cap)
    for g in range(groups):
        far_ref[g * block : (g + 1) * block, :] = spread_codes(
            asked_ref[g], b * per + cap, per - cap
        )


def cosine(x):
    turns = jnp.floor(x * 0.15915494309189535 + 0.5)
    r = (x - turns * 6.28125) - turns * 0.0019353071795864769
    z = r * r
    value = jnp.full_like(z, 1.0 / 20922789888000.0)
    for factor in (
        -1.0 / 87178291200.0,
        1.0 / 479001600.0,
        -1.0 / 3628800.0,
        1.0 / 40320.0,
        -1.0 / 720.0,
        1.0 / 24.0,
        -0.5,
        1.0,
    ):
        value = value * z + factor
    return value


def prep_kernel(
    width,
    at_ref,
    target_ref,
    time_ref,
    node_time_ref,
    edge_ref,
    freq_ref,
    phase_ref,
    w_ref,
    _,
    base_ref,
    gcode_ref,
    scode_ref,
    same_ref,
    count_ref,
):
    b = at_ref[0]
    batches, events = target_ref.shape
    node_dev = node_time_ref.shape[1]
    enc_at = 2 * width
    edge_at = enc_at + freq_ref.shape[1]
    trow = target_ref[pl.ds(b, 1), :]
    erow = time_ref[pl.ds(b, 1), :]
    stacked = jnp.concatenate(
        [trow.astype(F32), erow.astype(F32), jnp.zeros((LANES - 2, events), F32)], axis=0
    )
    cols = stacked.T
    sub = lax.broadcasted_iota(I32, (events, events), 0)
    lane = lax.broadcasted_iota(I32, (events, events), 1)
    node_lane = lax.broadcasted_iota(I32, (events, node_dev), 1)
    tcol = cols[:, 0:1].astype(I32)
    ecol = cols[:, 1:2]
    seen = jnp.max(
        jnp.where(tcol == node_lane, node_time_ref[...].astype(F32), 0.0), axis=1, keepdims=True
    )
    for before in range(batches - 1):
        row = target_ref[before : before + 1, :]
        row = jnp.where((row < 0) | (before >= b), -2, row)
        seen = jnp.maximum(
            seen,
            jnp.max(
                jnp.where(tcol == row, time_ref[before : before + 1, :].astype(F32), 0.0),
                axis=1,
                keepdims=True,
            ),
        )
    angle = (ecol - seen) * freq_ref[...] + phase_ref[...]
    encoded = cosine(angle).astype(BF16)
    base_ref[...] = dot(encoded, w_ref[enc_at:edge_at, :]) + dot(edge_ref[0], w_ref[edge_at:, :])
    gcode_ref[...] = lane_code(tcol, events)
    same = (tcol == trow) & (trow >= 0)
    samef = same.astype(F32)
    same_ref[...] = samef.astype(BF16)
    count_ref[...] = jnp.broadcast_to(
        jnp.maximum(jnp.sum(samef, axis=1, keepdims=True), 1.0), (events, LANES)
    )
    earlier = jnp.max(jnp.where(sub < lane, samef, 0.0), axis=0, keepdims=True)
    first = jnp.where(earlier > 0.0, -1, trow)
    sub128 = lax.broadcasted_iota(I32, (LANES, events), 0)
    scode_ref[...] = jnp.where(
        (first & (LANES - 1)) == sub128, (first >> 7).astype(F32), -1.0
    ).astype(BF16)


def serve_rows(table_ref, code_ref, out_ref, step):
    blocks = table_ref.shape[0] // LANES
    table = table_ref[...]
    for start in range(0, code_ref.shape[0], step):
        picked = dot(expand(code_ref[start : start + step, :], 0, blocks), table)
        out_ref[start : start + step, :] = picked.astype(BF16)


def serve_kernel(table_ref, own_code_ref, far_code_ref, own_ref, far_ref):
    serve_rows(table_ref, own_code_ref, own_ref, 256)
    serve_rows(table_ref, far_code_ref, far_ref, 512)


def local_kernel(table_ref, gcode_ref, base_ref, w_ref, mem_ref, out_ref):
    blocks = table_ref.shape[0] // LANES
    mem = dot(expand(gcode_ref[...], 0, blocks), table_ref[...]).astype(BF16)
    mem_ref[...] = mem
    out_ref[...] = base_ref[...] + dot(mem, w_ref[: mem.shape[1], :])


def update_kernel(
    last,
    at_ref,
    table_ref,
    back_ref,
    pcode_ref,
    base_ref,
    mem_ref,
    same_ref,
    count_ref,
    scode_ref,
    w_ref,
    w_input_ref,
    w_hidden_ref,
    bias_input_ref,
    bias_hidden_ref,
    own_code_ref,
    far_code_ref,
    new_ref,
    own_out_ref,
    far_out_ref,
):
    width = table_ref.shape[1]
    mem = mem_ref[...]
    hidden = dot(mem, w_hidden_ref[...]) + bias_hidden_ref[...]
    source = dot(expand(pcode_ref[0], 0, back_ref.shape[0] // LANES), back_ref[...])
    w_source = w_ref[width : 2 * width, :]
    message = (base_ref[...] + dot(source.astype(BF16), w_source)).astype(BF16)
    total = dot(same_ref[...], message)
    averaged = (total / count_ref[:, :1]).astype(BF16)
    gates = dot(averaged, w_input_ref[...]) + bias_input_ref[...]
    reset = jax.nn.sigmoid(gates[:, :width] + hidden[:, :width])
    update = jax.nn.sigmoid(gates[:, width : 2 * width] + hidden[:, width : 2 * width])
    candidate = jnp.tanh(gates[:, 2 * width :] + reset * hidden[:, 2 * width :])
    fresh = ((1.0 - update) * candidate + update * mem.astype(F32)).astype(BF16)
    ones = jnp.ones((fresh.shape[0], LANES), BF16)
    placed = jnp.concatenate([fresh, ones], axis=1)
    scode = scode_ref[...]
    one = jnp.ones((), BF16)
    zero = jnp.zeros((), BF16)
    blocks = table_ref.shape[0] // LANES
    group = 4
    for k in range(0, blocks, group):
        spread = jnp.concatenate(
            [jnp.where(scode == jnp.asarray(k + j, BF16), one, zero) for j in range(group)], axis=0
        )
        moved = dot(spread, placed)
        rows = slice(k * LANES, (k + group) * LANES)
        new_ref[rows, :] = jnp.where(
            moved[:, width : width + 1] > 0.0, moved[:, :width], table_ref[rows, :].astype(F32)
        ).astype(BF16)

    @pl.when(at_ref[0] < last)
    def _():
        serve_rows(new_ref, own_code_ref, own_out_ref, 256)
        serve_rows(new_ref, far_code_ref, far_out_ref, 512)


def from_owner(own_rows, far_rows, owner, cap):
    rows, _, width = own_rows.shape
    ys = far_rows.shape[0] // 2

    def branch(root):
        y, z = root // 2, root % 2

        def body(own_rows, far_rows):
            me = lax.axis_index("dom")
            my_y, my_z = me >> 1, me & 1

            def spread(which):
                part = far_rows[2 * y + which]
                moved = []
                for shift in range(1, ys):
                    there = (y + shift) % ys
                    pairs = [(2 * y + side, 2 * there + side) for side in range(2)]
                    block = lax.ppermute(far_rows[2 * there + which], "dom", pairs)
                    moved.append((there, block))
                for there, block in moved:
                    part = jnp.where(my_y == there, block, part)
                return part

            across = lax.ppermute(
                spread(1 - z), "dom", [(2 * i + z, 2 * i + 1 - z) for i in range(ys)]
            )
            mine = jnp.where(my_z == z, spread(z), across)
            return own_rows.at[:, cap:, :].set(mine.reshape(rows, -1, width))

        return body

    return lax.switch(owner, [branch(r) for r in range(2 * ys)], own_rows, far_rows)


def shards(
    memory,
    node_time,
    target,
    source,
    event_time,
    edge_feat,
    owner_group,
    w_message,
    frequency,
    phase_shift,
    w_input,
    w_hidden,
    bias_input,
    bias_hidden,
):
    node_dev, width = memory.shape
    batches, events = target.shape
    rows = lax.axis_size("row")
    groups = lax.axis_size("dom")
    cap = 3 * events // (2 * rows)
    ocap = events // (2 * rows)
    per = cap + ocap
    shape = jax.ShapeDtypeStruct
    code = shape((events, LANES), BF16)

    ids, pcode = call(
        functools.partial(plan_kernel, cap, ocap, node_dev),
        (shape((groups, rows, batches * per), I32), shape((batches, events, LANES), BF16)),
        (source,),
        name="plan",
    )
    asked = lax.all_to_all(
        ids.reshape(groups * rows, 1, batches * per), ("dom", "row"), 0, 0, tiled=True
    ).reshape(groups, rows, batches * per)
    me = lax.axis_index("dom").astype(I32)
    times_row = node_time.reshape(1, node_dev)
    freq_row = frequency.reshape(1, -1)
    phase_row = phase_shift.reshape(1, -1)
    input_row = bias_input.reshape(1, -1)
    hidden_row = bias_hidden.reshape(1, -1)
    anywhere = pl.BlockSpec(memory_space=pl.ANY)

    def codes(b, after):
        return call(
            functools.partial(code_kernel, cap, per),
            (
                shape((rows * per, LANES), BF16),
                shape((groups * rows * ocap, LANES), BF16),
            ),
            (asked, after),
            flops=2 * 10**9,
            name="codes",
            specs={1: anywhere},
            scalars=(jnp.stack([b, me]),),
        )

    own_shape = shape((rows * per, width), BF16)
    far_shape = shape((groups * rows * ocap, width), BF16)
    own_rows, far_rows = call(
        serve_kernel,
        (own_shape, far_shape),
        (memory,) + tuple(codes(jnp.zeros((), I32), asked)),
        flops=4 * 10**9,
        name="serve",
    )

    def batch(b, carry):
        table, own_rows, far_rows = carry
        at = b.reshape(1)
        sent = from_owner(
            own_rows.reshape(rows, per, width),
            far_rows.reshape(groups, rows * ocap, width),
            lax.dynamic_index_in_dim(owner_group, b, 0, keepdims=False),
            cap,
        )
        back = lax.all_to_all(sent, "row", 0, 0, tiled=True).reshape(rows * per, width)
        base, gcode, scode, same, count = call(
            functools.partial(prep_kernel, width),
            (
                shape((events, width), F32),
                code,
                shape((LANES, events), BF16),
                shape((events, events), BF16),
                shape((events, LANES), F32),
            ),
            (target, event_time, times_row, edge_feat, freq_row, phase_row, w_message, sent),
            flops=3 * 10**9,
            name="prep",
            specs={
                3: pl.BlockSpec((1,) + edge_feat.shape[1:], lambda i, at: (at[0], 0, 0)),
                7: anywhere,
            },
            scalars=(at,),
        )
        mem, local = call(
            local_kernel,
            (shape((events, width), BF16), shape((events, width), F32)),
            (table, gcode, base, w_message),
            flops=3 * 10**9,
            name="local",
        )
        own_code, far_code = codes(b + 1, sent)
        return call(
            functools.partial(update_kernel, batches - 1),
            (shape((node_dev, width), BF16), own_shape, far_shape),
            (
                table,
                back,
                pcode,
                local,
                mem,
                same,
                count,
                scode,
                w_message,
                w_input,
                w_hidden,
                input_row,
                hidden_row,
                own_code,
                far_code,
            ),
            flops=6 * 10**9,
            name="update",
            specs={2: pl.BlockSpec((1, events, LANES), lambda i, at: (at[0], 0, 0))},
            scalars=(at,),
        )

    return lax.fori_loop(0, batches, batch, (memory, own_rows, far_rows))[0]


def solution(mesh):
    in_specs = (
        P(("dom", "row"), None),
        P(("dom", "row")),
        P(None, ("dom", "row")),
        P(None, ("dom", "row")),
        P(None, ("dom", "row")),
        P(None, ("dom", "row"), None),
        P(),
        P(),
        P(),
        P(),
        P(),
        P(),
        P(),
        P(),
    )
    out_specs = P(("dom", "row"), None)
    return jax.shard_map(shards, mesh=mesh, in_specs=in_specs, out_specs=out_specs, check_vma=False)
```

profile of v0, /device:TPU:9, one launch (start us, length us, event | category | flops | bytes accessed | tf_op | source)
XLA Modules:
  0.0 270.2 jit_solution(8313055956675854772)
XLA Ops:
  0.0 2.3 copy.47.table_ref
  2.3 2.6 plan.1
  4.9 15.9 %all-to-all-start.1 = ((s32[256,1,128]{2,1,0:T(1,128)}), s32[256,1,128]{2,1,0:T(1,128)}, u32[]{:S(2)}, u32[]{:S(2)}) async-start(s32[256,1,128]{2,1,0:T(1,128)} %bitcast.81), calls=%async_computation.1 | async-start | bytes 262144 | tf_op jit(solution)/shard_map/all_to_all | solution.py:369
  21.6 10.3 %all-to-all-done.1 = s32[256,1,128]{2,1,0:T(1,128)} async-done(((s32[256,1,128]{2,1,0:T(1,128)}), s32[256,1,128]{2,1,0:T(1,128)}, u32[]{:S(2)}, u32[]{:S(2)}) %all-to-all-start.1) | async-done | bytes 131104 | tf_op jit(solution)/shard_map/all_to_all | solution.py:369
  31.8 2.5 codes.6
  34.4 5.7 %serve.1 = (bf16[1024,256]{1,0:T(8,128)(2,1)}, bf16[2048,256]{1,0:T(8,128)(2,1)}) custom-call(bf16[2048,256]{1,0:T(8,128)(2,1)} %copy.47.table_ref, bf16[1024,128]{1,0:T(8,128)(2,1)S(1)} %get-tuple-element.458.own_code_ref, bf16[2048,128]{1,0:T(8,128)(2,1)S(1)} %get-tuple-element.459.far_code_ref), custom_call_target="tpu_custom_call" | custom-call | flops 4000000000 | bytes 3407872 | tf_op jit(solution)/shard_map/serve/pallas_call | solution.py:26
  40.7 229.4 %while.25 = (s32[]{:T(128)}, bf16[2048,256]{1,0:T(8,128)(2,1)}, bf16[1024,256]{1,0:T(8,128)(2,1)}, bf16[2048,256]{1,0:T(8,128)(2,1)}, s32[4]{0:T(128)S(1)}, /*in...) while((s32[]{:T(128)}, bf16[2048,256]{1,0:T(8,128)(2,1)}, ...), condition=%wide.region_9.10_spmd, body=%wide.region_0.9_spmd.sunk | while | flops 14000458752 | bytes 30314440 | solution.py:466
  42.0 23.0 %conditional.2 = (bf16[32,32,256]{2,1,0:T(8,128)(2,1)}) conditional(s32[]{:T(128)} %bitcast.263, (bf16[8,256,256]{2,1,0:T(8,128)(2,1)}, bf16[32,32,256]{2,1,0:T(8,128)(2,1)}) %tuple.125, (bf16[8,256,256]{2,1,0:T(8,128)(2,1)}, bf16[32,32,256]{2,1,0:T(8,128)(2,1)}) %tuple.125, (bf16[8,256,256]{2,1,0:T(8,128)(2,1)}, ...), branch_computations={%region_1.1_spmd, %region_2.2_spmd, %region_3.3_spmd, %region_4.4_... | conditional | flops 458761 | bytes 6685059 | solution.py:334
  48.7 4.1 %collective-permute-done.53 = bf16[256,256]{1,0:T(8,128)(2,1)S(1)} collective-permute-done((bf16[256,256]{1,0:T(8,128)(2,1)S(1)}, bf16[256,256]{1,0:T(8,128)(2,1)S(1)}, u32[]{:S(2)}, u32[]{:S(2)}) %collective-permute-start.53) | collective-permute-done | bytes 131104 | tf_op jit(solution)/shard_map/while/body/eval_jaxpr/cond/branch_7_fun/ppermute | solution.py:320
  55.0 3.4 %collective-permute-done.50 = bf16[256,256]{1,0:T(8,128)(2,1)S(1)} collective-permute-done((bf16[256,256]{1,0:T(8,128)(2,1)S(1)}, bf16[256,256]{1,0:T(8,128)(2,1)S(1)}, u32[]{:S(2)}, u32[]{:S(2)}) %collective-permute-start.50) | collective-permute-done | bytes 131104 | tf_op jit(solution)/shard_map/while/body/eval_jaxpr/cond/branch_7_fun/ppermute | solution.py:320
  58.4 4.9 %collective-permute-done.55 = bf16[256,256]{1,0:T(8,128)(2,1)S(1)} collective-permute-done((bf16[256,256]{1,0:T(8,128)(2,1)S(1)}, bf16[256,256]{1,0:T(8,128)(2,1)S(1)}, u32[]{:S(2)}, u32[]{:S(2)}) %collective-permute-start.55) | collective-permute-done | bytes 131104 | tf_op jit(solution)/shard_map/while/body/eval_jaxpr/cond/branch_7_fun/ppermute | solution.py:326
  63.3 1.7 bitcast_dynamic-update-slice_fusion.7
  65.0 8.7 %all-to-all-start = ((bf16[32,32,256]{2,1,0:T(8,128)(2,1)}), bf16[32,32,256]{2,1,0:T(8,128)(2,1)S(1)}, u32[]{:S(2)}, u32[]{:S(2)}) async-start(bf16[32,32,256]{2,1,0:T(8,128)(2,1)} %get-tuple-element.755._), calls=%async_computation | async-start | bytes 1048576 | tf_op jit(solution)/shard_map/while/body/eval_jaxpr/all_to_all | solution.py:413
  75.0 2.5 codes.7
  77.5 2.7 %prep.5 = (f32[512,256]{1,0:T(8,128)S(1)}, bf16[512,128]{1,0:T(8,128)(2,1)S(1)}, bf16[128,512]{1,0:T(8,128)(2,1)S(1)}, bf16[512,512]{1,0:T(8,128)(2,1)S(1)}, f32[512,128]{1,0:T(8,128)S(1)}) custom-call(s32[1]{0:T(128)} %bitcast.262.at_ref, s32[4,512]{1,0:T(4,128)S(1)} %get-tuple-element.738.target_ref, s32[4,512]{1,0:T(4,128)} %get-tuple-element.739.time_ref, ...), custom_call_target="tpu_custom_call" | custom-call | flops 3000000000 | bytes 3040256 | tf_op jit(solution)/shard_map/while/body/eval_jaxpr/prep/pallas_call | solution.py:26
  81.0 1.9 local.5
  83.6 6.5 %all-to-all-done = bf16[32,32,256]{2,1,0:T(8,128)(2,1)S(1)} async-done(((bf16[32,32,256]{2,1,0:T(8,128)(2,1)}), bf16[32,32,256]{2,1,0:T(8,128)(2,1)S(1)}, u32[]{:S(2)}, u32[]{:S(2)}) %all-to-all-start) | async-done | bytes 524320 | tf_op jit(solution)/shard_map/while/body/eval_jaxpr/all_to_all | solution.py:413
  92.0 9.1 %update.5 = (bf16[2048,256]{1,0:T(8,128)(2,1)}, bf16[1024,256]{1,0:T(8,128)(2,1)}, bf16[2048,256]{1,0:T(8,128)(2,1)}) custom-call(s32[1]{0:T(128)} %bitcast.262.at_ref, bf16[2048,256]{1,0:T(8,128)(2,1)S(1)} %copy.49.table_ref, bf16[1024,256]{1,0:T(8,128)(2,1)S(1)} %bitcast.269, bf16[4,512,128]{2,1,0:T(8,128)(2,1)} %get-tuple-element.747.pcode_ref, ...), custom_call_target="tpu_custom_call" | custom-call | flops 6000000000 | bytes 8394752 | tf_op jit(solution)/shard_map/while/body/eval_jaxpr/update/pallas_call | solution.py:26
  102.9 18.0 %conditional.2 = (bf16[32,32,256]{2,1,0:T(8,128)(2,1)}) conditional(s32[]{:T(128)} %bitcast.263, (bf16[8,256,256]{2,1,0:T(8,128)(2,1)}, bf16[32,32,256]{2,1,0:T(8,128)(2,1)}) %tuple.125, (bf16[8,256,256]{2,1,0:T(8,128)(2,1)}, bf16[32,32,256]{2,1,0:T(8,128)(2,1)}) %tuple.125, (bf16[8,256,256]{2,1,0:T(8,128)(2,1)}, ...), branch_computations={%region_1.1_spmd, %region_2.2_spmd, %region_3.3_spmd, %region_4.4_... | conditional | flops 458761 | bytes 6685059 | solution.py:334
  109.5 4.1 %collective-permute-done.46 = bf16[256,256]{1,0:T(8,128)(2,1)S(1)} collective-permute-done((bf16[256,256]{1,0:T(8,128)(2,1)S(1)}, bf16[256,256]{1,0:T(8,128)(2,1)S(1)}, u32[]{:S(2)}, u32[]{:S(2)}) %collective-permute-start.46) | collective-permute-done | bytes 131104 | tf_op jit(solution)/shard_map/while/body/eval_jaxpr/cond/branch_6_fun/ppermute | solution.py:320
  115.9 3.3 %collective-permute-done.43 = bf16[256,256]{1,0:T(8,128)(2,1)S(1)} collective-permute-done((bf16[256,256]{1,0:T(8,128)(2,1)S(1)}, bf16[256,256]{1,0:T(8,128)(2,1)S(1)}, u32[]{:S(2)}, u32[]{:S(2)}) %collective-permute-start.43) | collective-permute-done | bytes 131104 | tf_op jit(solution)/shard_map/while/body/eval_jaxpr/cond/branch_6_fun/ppermute | solution.py:320
  119.2 1.7 bitcast_dynamic-update-slice_fusion.6
  120.9 5.5 %all-to-all-start = ((bf16[32,32,256]{2,1,0:T(8,128)(2,1)}), bf16[32,32,256]{2,1,0:T(8,128)(2,1)S(1)}, u32[]{:S(2)}, u32[]{:S(2)}) async-start(bf16[32,32,256]{2,1,0:T(8,128)(2,1)} %get-tuple-element.755._), calls=%async_computation | async-start | bytes 1048576 | tf_op jit(solution)/shard_map/while/body/eval_jaxpr/all_to_all | solution.py:413
  127.7 2.5 codes.7
  130.3 2.7 %prep.5 = (f32[512,256]{1,0:T(8,128)S(1)}, bf16[512,128]{1,0:T(8,128)(2,1)S(1)}, bf16[128,512]{1,0:T(8,128)(2,1)S(1)}, bf16[512,512]{1,0:T(8,128)(2,1)S(1)}, f32[512,128]{1,0:T(8,128)S(1)}) custom-call(s32[1]{0:T(128)} %bitcast.262.at_ref, s32[4,512]{1,0:T(4,128)S(1)} %get-tuple-element.738.target_ref, s32[4,512]{1,0:T(4,128)} %get-tuple-element.739.time_ref, ...), custom_call_target="tpu_custom_call" | custom-call | flops 3000000000 | bytes 3040256 | tf_op jit(solution)/shard_map/while/body/eval_jaxpr/prep/pallas_call | solution.py:26
  133.7 1.9 local.5
  136.3 6.5 %all-to-all-done = bf16[32,32,256]{2,1,0:T(8,128)(2,1)S(1)} async-done(((bf16[32,32,256]{2,1,0:T(8,128)(2,1)}), bf16[32,32,256]{2,1,0:T(8,128)(2,1)S(1)}, u32[]{:S(2)}, u32[]{:S(2)}) %all-to-all-start) | async-done | bytes 524320 | tf_op jit(solution)/shard_map/while/body/eval_jaxpr/all_to_all | solution.py:413
  144.7 9.1 %update.5 = (bf16[2048,256]{1,0:T(8,128)(2,1)}, bf16[1024,256]{1,0:T(8,128)(2,1)}, bf16[2048,256]{1,0:T(8,128)(2,1)}) custom-call(s32[1]{0:T(128)} %bitcast.262.at_ref, bf16[2048,256]{1,0:T(8,128)(2,1)S(1)} %copy.49.table_ref, bf16[1024,256]{1,0:T(8,128)(2,1)S(1)} %bitcast.269, bf16[4,512,128]{2,1,0:T(8,128)(2,1)} %get-tuple-element.747.pcode_ref, ...), custom_call_target="tpu_custom_call" | custom-call | flops 6000000000 | bytes 8394752 | tf_op jit(solution)/shard_map/while/body/eval_jaxpr/update/pallas_call | solution.py:26
  155.6 25.1 %conditional.2 = (bf16[32,32,256]{2,1,0:T(8,128)(2,1)}) conditional(s32[]{:T(128)} %bitcast.263, (bf16[8,256,256]{2,1,0:T(8,128)(2,1)}, bf16[32,32,256]{2,1,0:T(8,128)(2,1)}) %tuple.125, (bf16[8,256,256]{2,1,0:T(8,128)(2,1)}, bf16[32,32,256]{2,1,0:T(8,128)(2,1)}) %tuple.125, (bf16[8,256,256]{2,1,0:T(8,128)(2,1)}, ...), branch_computations={%region_1.1_spmd, %region_2.2_spmd, %region_3.3_spmd, %region_4.4_... | conditional | flops 458761 | bytes 6685059 | solution.py:334
  162.2 5.6 %collective-permute-done.31 = bf16[256,256]{1,0:T(8,128)(2,1)S(1)} collective-permute-done((bf16[256,256]{1,0:T(8,128)(2,1)S(1)}, bf16[256,256]{1,0:T(8,128)(2,1)S(1)}, u32[]{:S(2)}, u32[]{:S(2)}) %collective-permute-start.31) | collective-permute-done | bytes 131104 | tf_op jit(solution)/shard_map/while/body/eval_jaxpr/cond/branch_4_fun/ppermute | solution.py:320
  168.8 8.0 %collective-permute-start.34 = (bf16[256,256]{1,0:T(8,128)(2,1)S(1)}, bf16[256,256]{1,0:T(8,128)(2,1)S(1)}, u32[]{:S(2)}, u32[]{:S(2)}) collective-permute-start(bf16[256,256]{1,0:T(8,128)(2,1)S(1)} %fusion.21), channel_id=1, source_target_pairs={{0,32},{64,96},{128,160},{192,224},{1,33},{65,97},{129,161},{193,2... | collective-permute-start | bytes 393224 | tf_op jit(solution)/shard_map/while/body/eval_jaxpr/cond/branch_4_fun/ppermute | solution.py:326
  176.8 2.2 collective-permute-done.34
  180.7 6.5 %all-to-all-start = ((bf16[32,32,256]{2,1,0:T(8,128)(2,1)}), bf16[32,32,256]{2,1,0:T(8,128)(2,1)S(1)}, u32[]{:S(2)}, u32[]{:S(2)}) async-start(bf16[32,32,256]{2,1,0:T(8,128)(2,1)} %get-tuple-element.755._), calls=%async_computation | async-start | bytes 1048576 | tf_op jit(solution)/shard_map/while/body/eval_jaxpr/all_to_all | solution.py:413
  188.6 2.5 codes.7
  191.1 2.7 %prep.5 = (f32[512,256]{1,0:T(8,128)S(1)}, bf16[512,128]{1,0:T(8,128)(2,1)S(1)}, bf16[128,512]{1,0:T(8,128)(2,1)S(1)}, bf16[512,512]{1,0:T(8,128)(2,1)S(1)}, f32[512,128]{1,0:T(8,128)S(1)}) custom-call(s32[1]{0:T(128)} %bitcast.262.at_ref, s32[4,512]{1,0:T(4,128)S(1)} %get-tuple-element.738.target_ref, s32[4,512]{1,0:T(4,128)} %get-tuple-element.739.time_ref, ...), custom_call_target="tpu_custom_call" | custom-call | flops 3000000000 | bytes 3040256 | tf_op jit(solution)/shard_map/while/body/eval_jaxpr/prep/pallas_call | solution.py:26
  194.5 1.9 local.5
  197.1 6.5 %all-to-all-done = bf16[32,32,256]{2,1,0:T(8,128)(2,1)S(1)} async-done(((bf16[32,32,256]{2,1,0:T(8,128)(2,1)}), bf16[32,32,256]{2,1,0:T(8,128)(2,1)S(1)}, u32[]{:S(2)}, u32[]{:S(2)}) %all-to-all-start) | async-done | bytes 524320 | tf_op jit(solution)/shard_map/while/body/eval_jaxpr/all_to_all | solution.py:413
  205.6 9.1 %update.5 = (bf16[2048,256]{1,0:T(8,128)(2,1)}, bf16[1024,256]{1,0:T(8,128)(2,1)}, bf16[2048,256]{1,0:T(8,128)(2,1)}) custom-call(s32[1]{0:T(128)} %bitcast.262.at_ref, bf16[2048,256]{1,0:T(8,128)(2,1)S(1)} %copy.49.table_ref, bf16[1024,256]{1,0:T(8,128)(2,1)S(1)} %bitcast.269, bf16[4,512,128]{2,1,0:T(8,128)(2,1)} %get-tuple-element.747.pcode_ref, ...), custom_call_target="tpu_custom_call" | custom-call | flops 6000000000 | bytes 8394752 | tf_op jit(solution)/shard_map/while/body/eval_jaxpr/update/pallas_call | solution.py:26
  216.5 22.6 %conditional.2 = (bf16[32,32,256]{2,1,0:T(8,128)(2,1)}) conditional(s32[]{:T(128)} %bitcast.263, (bf16[8,256,256]{2,1,0:T(8,128)(2,1)}, bf16[32,32,256]{2,1,0:T(8,128)(2,1)}) %tuple.125, (bf16[8,256,256]{2,1,0:T(8,128)(2,1)}, bf16[32,32,256]{2,1,0:T(8,128)(2,1)}) %tuple.125, (bf16[8,256,256]{2,1,0:T(8,128)(2,1)}, ...), branch_computations={%region_1.1_spmd, %region_2.2_spmd, %region_3.3_spmd, %region_4.4_... | conditional | flops 458761 | bytes 6685059 | solution.py:334
  222.4 2.9 %collective-permute-done.5 = bf16[256,256]{1,0:T(8,128)(2,1)S(1)} collective-permute-done((bf16[256,256]{1,0:T(8,128)(2,1)S(1)}, bf16[256,256]{1,0:T(8,128)(2,1)S(1)}, u32[]{:S(2)}, u32[]{:S(2)}) %collective-permute-start.5) | collective-permute-done | bytes 131104 | tf_op jit(solution)/shard_map/while/body/eval_jaxpr/cond/branch_0_fun/ppermute | solution.py:320
  226.9 8.0 %collective-permute-start.6 = (bf16[256,256]{1,0:T(8,128)(2,1)S(1)}, bf16[256,256]{1,0:T(8,128)(2,1)S(1)}, u32[]{:S(2)}, u32[]{:S(2)}) collective-permute-start(bf16[256,256]{1,0:T(8,128)(2,1)S(1)} %fusion.1), channel_id=1, source_target_pairs={{0,32},{64,96},{128,160},{192,224},{1,33},{65,97},{129,161},{193,2... | collective-permute-start | bytes 393224 | tf_op jit(solution)/shard_map/while/body/eval_jaxpr/cond/branch_0_fun/ppermute | solution.py:326
  235.0 2.4 collective-permute-done.6
  239.1 6.4 %all-to-all-start = ((bf16[32,32,256]{2,1,0:T(8,128)(2,1)}), bf16[32,32,256]{2,1,0:T(8,128)(2,1)S(1)}, u32[]{:S(2)}, u32[]{:S(2)}) async-start(bf16[32,32,256]{2,1,0:T(8,128)(2,1)} %get-tuple-element.755._), calls=%async_computation | async-start | bytes 1048576 | tf_op jit(solution)/shard_map/while/body/eval_jaxpr/all_to_all | solution.py:413
  246.8 2.5 codes.7
  249.3 2.7 %prep.5 = (f32[512,256]{1,0:T(8,128)S(1)}, bf16[512,128]{1,0:T(8,128)(2,1)S(1)}, bf16[128,512]{1,0:T(8,128)(2,1)S(1)}, bf16[512,512]{1,0:T(8,128)(2,1)S(1)}, f32[512,128]{1,0:T(8,128)S(1)}) custom-call(s32[1]{0:T(128)} %bitcast.262.at_ref, s32[4,512]{1,0:T(4,128)S(1)} %get-tuple-element.738.target_ref, s32[4,512]{1,0:T(4,128)} %get-tuple-element.739.time_ref, ...), custom_call_target="tpu_custom_call" | custom-call | flops 3000000000 | bytes 3040256 | tf_op jit(solution)/shard_map/while/body/eval_jaxpr/prep/pallas_call | solution.py:26
  252.8 1.9 local.5
  255.4 6.5 %all-to-all-done = bf16[32,32,256]{2,1,0:T(8,128)(2,1)S(1)} async-done(((bf16[32,32,256]{2,1,0:T(8,128)(2,1)}), bf16[32,32,256]{2,1,0:T(8,128)(2,1)S(1)}, u32[]{:S(2)}, u32[]{:S(2)}) %all-to-all-start) | async-done | bytes 524320 | tf_op jit(solution)/shard_map/while/body/eval_jaxpr/all_to_all | solution.py:413
  263.8 5.7 %update.5 = (bf16[2048,256]{1,0:T(8,128)(2,1)}, bf16[1024,256]{1,0:T(8,128)(2,1)}, bf16[2048,256]{1,0:T(8,128)(2,1)}) custom-call(s32[1]{0:T(128)} %bitcast.262.at_ref, bf16[2048,256]{1,0:T(8,128)(2,1)S(1)} %copy.49.table_ref, bf16[1024,256]{1,0:T(8,128)(2,1)S(1)} %bitcast.269, bf16[4,512,128]{2,1,0:T(8,128)(2,1)} %get-tuple-element.747.pcode_ref, ...), custom_call_target="tpu_custom_call" | custom-call | flops 6000000000 | bytes 8394752 | tf_op jit(solution)/shard_map/while/body/eval_jaxpr/update/pallas_call | solution.py:26
  (140 shorter events, 60.5 us)
Async XLA Ops:
  0.0 2.3 copy-start
  4.9 27.0 %all-to-all-start.1 = ((s32[256,1,128]{2,1,0:T(1,128)}), s32[256,1,128]{2,1,0:T(1,128)}, u32[]{:S(2)}, u32[]{:S(2)}) async-start(s32[256,1,128]{2,1,0:T(1,128)} %bitcast.81), calls=%async_computation.1 | async-start | bytes 262144 | tf_op jit(solution)/shard_map/all_to_all | solution.py:369
  40.0 0.7 copy-start.10
  40.0 0.7 copy-start.12
  43.3 4.6 %collective-permute-start.54 = (bf16[256,256]{1,0:T(8,128)(2,1)S(1)}, bf16[256,256]{1,0:T(8,128)(2,1)S(1)}, u32[]{:S(2)}, u32[]{:S(2)}) collective-permute-start(bf16[256,256]{1,0:T(8,128)(2,1)S(1)} %get-tuple-element.545), channel_id=1, source_target_pairs={{192,0},{224,32},{193,1},{225,33},{194,2},{226,34},{195,3},{227,35... | collective-permute-start | bytes 393224 | tf_op jit(solution)/shard_map/while/body/eval_jaxpr/cond/branch_7_fun/ppermute | solution.py:320
  44.0 8.8 %collective-permute-start.53 = (bf16[256,256]{1,0:T(8,128)(2,1)S(1)}, bf16[256,256]{1,0:T(8,128)(2,1)S(1)}, u32[]{:S(2)}, u32[]{:S(2)}) collective-permute-start(bf16[256,256]{1,0:T(8,128)(2,1)S(1)} %get-tuple-element.546), channel_id=1, source_target_pairs={{192,64},{224,96},{193,65},{225,97},{194,66},{226,98},{195,67},{22... | collective-permute-start | bytes 393224 | tf_op jit(solution)/shard_map/while/body/eval_jaxpr/cond/branch_7_fun/ppermute | solution.py:320
  45.3 7.5 %collective-permute-start.52 = (bf16[256,256]{1,0:T(8,128)(2,1)S(1)}, bf16[256,256]{1,0:T(8,128)(2,1)S(1)}, u32[]{:S(2)}, u32[]{:S(2)}) collective-permute-start(bf16[256,256]{1,0:T(8,128)(2,1)S(1)} %get-tuple-element.547), channel_id=1, source_target_pairs={{192,128},{224,160},{193,129},{225,161},{194,130},{226,162},{195,1... | collective-permute-start | bytes 393224 | tf_op jit(solution)/shard_map/while/body/eval_jaxpr/cond/branch_7_fun/ppermute | solution.py:320
  46.0 9.0 %collective-permute-start.51 = (bf16[256,256]{1,0:T(8,128)(2,1)S(1)}, bf16[256,256]{1,0:T(8,128)(2,1)S(1)}, u32[]{:S(2)}, u32[]{:S(2)}) collective-permute-start(bf16[256,256]{1,0:T(8,128)(2,1)S(1)} %get-tuple-element.544), channel_id=1, source_target_pairs={{192,0},{224,32},{193,1},{225,33},{194,2},{226,34},{195,3},{227,35... | collective-permute-start | bytes 393224 | tf_op jit(solution)/shard_map/while/body/eval_jaxpr/cond/branch_7_fun/ppermute | solution.py:320
  46.7 11.7 %collective-permute-start.50 = (bf16[256,256]{1,0:T(8,128)(2,1)S(1)}, bf16[256,256]{1,0:T(8,128)(2,1)S(1)}, u32[]{:S(2)}, u32[]{:S(2)}) collective-permute-start(bf16[256,256]{1,0:T(8,128)(2,1)S(1)} %get-tuple-element.548), channel_id=1, source_target_pairs={{192,64},{224,96},{193,65},{225,97},{194,66},{226,98},{195,67},{22... | collective-permute-start | bytes 393224 | tf_op jit(solution)/shard_map/while/body/eval_jaxpr/cond/branch_7_fun/ppermute | solution.py:320
  48.0 10.4 %collective-permute-start.49 = (bf16[256,256]{1,0:T(8,128)(2,1)S(1)}, bf16[256,256]{1,0:T(8,128)(2,1)S(1)}, u32[]{:S(2)}, u32[]{:S(2)}) collective-permute-start(bf16[256,256]{1,0:T(8,128)(2,1)S(1)} %get-tuple-element.549), channel_id=1, source_target_pairs={{192,128},{224,160},{193,129},{225,161},{194,130},{226,162},{195,1... | collective-permute-start | bytes 393224 | tf_op jit(solution)/shard_map/while/body/eval_jaxpr/cond/branch_7_fun/ppermute | solution.py:320
  53.7 9.6 %collective-permute-start.55 = (bf16[256,256]{1,0:T(8,128)(2,1)S(1)}, bf16[256,256]{1,0:T(8,128)(2,1)S(1)}, u32[]{:S(2)}, u32[]{:S(2)}) collective-permute-start(bf16[256,256]{1,0:T(8,128)(2,1)S(1)} %fusion.36), channel_id=1, source_target_pairs={{32,0},{96,64},{160,128},{224,192},{33,1},{97,65},{161,129},{225,1... | collective-permute-start | bytes 393224 | tf_op jit(solution)/shard_map/while/body/eval_jaxpr/cond/branch_7_fun/ppermute | solution.py:326
  65.0 25.1 %all-to-all-start = ((bf16[32,32,256]{2,1,0:T(8,128)(2,1)}), bf16[32,32,256]{2,1,0:T(8,128)(2,1)S(1)}, u32[]{:S(2)}, u32[]{:S(2)}) async-start(bf16[32,32,256]{2,1,0:T(8,128)(2,1)} %get-tuple-element.755._), calls=%async_computation | async-start | bytes 1048576 | tf_op jit(solution)/shard_map/while/body/eval_jaxpr/all_to_all | solution.py:413
  82.9 0.7 copy-start.1
  90.1 1.0 copy-start.2
  91.0 0.9 copy-start.4
  104.2 4.6 %collective-permute-start.47 = (bf16[256,256]{1,0:T(8,128)(2,1)S(1)}, bf16[256,256]{1,0:T(8,128)(2,1)S(1)}, u32[]{:S(2)}, u32[]{:S(2)}) collective-permute-start(bf16[256,256]{1,0:T(8,128)(2,1)S(1)} %get-tuple-element.539), channel_id=1, source_target_pairs={{192,0},{224,32},{193,1},{225,33},{194,2},{226,34},{195,3},{227,35... | collective-permute-start | bytes 393224 | tf_op jit(solution)/shard_map/while/body/eval_jaxpr/cond/branch_6_fun/ppermute | solution.py:320
  104.9 8.8 %collective-permute-start.46 = (bf16[256,256]{1,0:T(8,128)(2,1)S(1)}, bf16[256,256]{1,0:T(8,128)(2,1)S(1)}, u32[]{:S(2)}, u32[]{:S(2)}) collective-permute-start(bf16[256,256]{1,0:T(8,128)(2,1)S(1)} %get-tuple-element.540), channel_id=1, source_target_pairs={{192,64},{224,96},{193,65},{225,97},{194,66},{226,98},{195,67},{22... | collective-permute-start | bytes 393224 | tf_op jit(solution)/shard_map/while/body/eval_jaxpr/cond/branch_6_fun/ppermute | solution.py:320
  106.2 7.5 %collective-permute-start.45 = (bf16[256,256]{1,0:T(8,128)(2,1)S(1)}, bf16[256,256]{1,0:T(8,128)(2,1)S(1)}, u32[]{:S(2)}, u32[]{:S(2)}) collective-permute-start(bf16[256,256]{1,0:T(8,128)(2,1)S(1)} %get-tuple-element.541), channel_id=1, source_target_pairs={{192,128},{224,160},{193,129},{225,161},{194,130},{226,162},{195,1... | collective-permute-start | bytes 393224 | tf_op jit(solution)/shard_map/while/body/eval_jaxpr/cond/branch_6_fun/ppermute | solution.py:320
  106.8 9.0 %collective-permute-start.44 = (bf16[256,256]{1,0:T(8,128)(2,1)S(1)}, bf16[256,256]{1,0:T(8,128)(2,1)S(1)}, u32[]{:S(2)}, u32[]{:S(2)}) collective-permute-start(bf16[256,256]{1,0:T(8,128)(2,1)S(1)} %get-tuple-element.538), channel_id=1, source_target_pairs={{192,0},{224,32},{193,1},{225,33},{194,2},{226,34},{195,3},{227,35... | collective-permute-start | bytes 393224 | tf_op jit(solution)/shard_map/while/body/eval_jaxpr/cond/branch_6_fun/ppermute | solution.py:320
  107.5 11.7 %collective-permute-start.43 = (bf16[256,256]{1,0:T(8,128)(2,1)S(1)}, bf16[256,256]{1,0:T(8,128)(2,1)S(1)}, u32[]{:S(2)}, u32[]{:S(2)}) collective-permute-start(bf16[256,256]{1,0:T(8,128)(2,1)S(1)} %get-tuple-element.542), channel_id=1, source_target_pairs={{192,64},{224,96},{193,65},{225,97},{194,66},{226,98},{195,67},{22... | collective-permute-start | bytes 393224 | tf_op jit(solution)/shard_map/while/body/eval_jaxpr/cond/branch_6_fun/ppermute | solution.py:320
  108.8 10.4 %collective-permute-start.42 = (bf16[256,256]{1,0:T(8,128)(2,1)S(1)}, bf16[256,256]{1,0:T(8,128)(2,1)S(1)}, u32[]{:S(2)}, u32[]{:S(2)}) collective-permute-start(bf16[256,256]{1,0:T(8,128)(2,1)S(1)} %get-tuple-element.543), channel_id=1, source_target_pairs={{192,128},{224,160},{193,129},{225,161},{194,130},{226,162},{195,1... | collective-permute-start | bytes 393224 | tf_op jit(solution)/shard_map/while/body/eval_jaxpr/cond/branch_6_fun/ppermute | solution.py:320
  114.6 4.7 %collective-permute-start.48 = (bf16[256,256]{1,0:T(8,128)(2,1)S(1)}, bf16[256,256]{1,0:T(8,128)(2,1)S(1)}, u32[]{:S(2)}, u32[]{:S(2)}) collective-permute-start(bf16[256,256]{1,0:T(8,128)(2,1)S(1)} %fusion.31), channel_id=1, source_target_pairs={{0,32},{64,96},{128,160},{192,224},{1,33},{65,97},{129,161},{193,2... | collective-permute-start | bytes 393224 | tf_op jit(solution)/shard_map/while/body/eval_jaxpr/cond/branch_6_fun/ppermute | solution.py:326
  120.9 21.9 %all-to-all-start = ((bf16[32,32,256]{2,1,0:T(8,128)(2,1)}), bf16[32,32,256]{2,1,0:T(8,128)(2,1)S(1)}, u32[]{:S(2)}, u32[]{:S(2)}) async-start(bf16[32,32,256]{2,1,0:T(8,128)(2,1)} %get-tuple-element.755._), calls=%async_computation | async-start | bytes 1048576 | tf_op jit(solution)/shard_map/while/body/eval_jaxpr/all_to_all | solution.py:413
  135.6 0.7 copy-start.1
  142.8 1.0 copy-start.2
  143.8 0.9 copy-start.4
  156.9 4.0 %collective-permute-start.33 = (bf16[256,256]{1,0:T(8,128)(2,1)S(1)}, bf16[256,256]{1,0:T(8,128)(2,1)S(1)}, u32[]{:S(2)}, u32[]{:S(2)}) collective-permute-start(bf16[256,256]{1,0:T(8,128)(2,1)S(1)} %get-tuple-element.527), channel_id=1, source_target_pairs={{128,192},{160,224},{129,193},{161,225},{130,194},{162,226},{131,1... | collective-permute-start | bytes 393224 | tf_op jit(solution)/shard_map/while/body/eval_jaxpr/cond/branch_4_fun/ppermute | solution.py:320
  157.6 4.7 %collective-permute-start.32 = (bf16[256,256]{1,0:T(8,128)(2,1)S(1)}, bf16[256,256]{1,0:T(8,128)(2,1)S(1)}, u32[]{:S(2)}, u32[]{:S(2)}) collective-permute-start(bf16[256,256]{1,0:T(8,128)(2,1)S(1)} %get-tuple-element.528), channel_id=1, source_target_pairs={{128,0},{160,32},{129,1},{161,33},{130,2},{162,34},{131,3},{163,35... | collective-permute-start | bytes 393224 | tf_op jit(solution)/shard_map/while/body/eval_jaxpr/cond/branch_4_fun/ppermute | solution.py:320
  158.3 9.6 %collective-permute-start.31 = (bf16[256,256]{1,0:T(8,128)(2,1)S(1)}, bf16[256,256]{1,0:T(8,128)(2,1)S(1)}, u32[]{:S(2)}, u32[]{:S(2)}) collective-permute-start(bf16[256,256]{1,0:T(8,128)(2,1)S(1)} %get-tuple-element.529), channel_id=1, source_target_pairs={{128,64},{160,96},{129,65},{161,97},{130,66},{162,98},{131,67},{16... | collective-permute-start | bytes 393224 | tf_op jit(solution)/shard_map/while/body/eval_jaxpr/cond/branch_4_fun/ppermute | solution.py:320
  159.6 17.2 %collective-permute-start.30 = (bf16[256,256]{1,0:T(8,128)(2,1)S(1)}, bf16[256,256]{1,0:T(8,128)(2,1)S(1)}, u32[]{:S(2)}, u32[]{:S(2)}) collective-permute-start(bf16[256,256]{1,0:T(8,128)(2,1)S(1)} %get-tuple-element.526), channel_id=1, source_target_pairs={{128,192},{160,224},{129,193},{161,225},{130,194},{162,226},{131,1... | collective-permute-start | bytes 393224 | tf_op jit(solution)/shard_map/while/body/eval_jaxpr/cond/branch_4_fun/ppermute | solution.py:320
  160.2 16.6 %collective-permute-start.29 = (bf16[256,256]{1,0:T(8,128)(2,1)S(1)}, bf16[256,256]{1,0:T(8,128)(2,1)S(1)}, u32[]{:S(2)}, u32[]{:S(2)}) collective-permute-start(bf16[256,256]{1,0:T(8,128)(2,1)S(1)} %get-tuple-element.530), channel_id=1, source_target_pairs={{128,0},{160,32},{129,1},{161,33},{130,2},{162,34},{131,3},{163,35... | collective-permute-start | bytes 393224 | tf_op jit(solution)/shard_map/while/body/eval_jaxpr/cond/branch_4_fun/ppermute | solution.py:320
  160.9 15.9 %collective-permute-start.28 = (bf16[256,256]{1,0:T(8,128)(2,1)S(1)}, bf16[256,256]{1,0:T(8,128)(2,1)S(1)}, u32[]{:S(2)}, u32[]{:S(2)}) collective-permute-start(bf16[256,256]{1,0:T(8,128)(2,1)S(1)} %get-tuple-element.531), channel_id=1, source_target_pairs={{128,64},{160,96},{129,65},{161,97},{130,66},{162,98},{131,67},{16... | collective-permute-start | bytes 393224 | tf_op jit(solution)/shard_map/while/body/eval_jaxpr/cond/branch_4_fun/ppermute | solution.py:320
  168.8 10.3 %collective-permute-start.34 = (bf16[256,256]{1,0:T(8,128)(2,1)S(1)}, bf16[256,256]{1,0:T(8,128)(2,1)S(1)}, u32[]{:S(2)}, u32[]{:S(2)}) collective-permute-start(bf16[256,256]{1,0:T(8,128)(2,1)S(1)} %fusion.21), channel_id=1, source_target_pairs={{0,32},{64,96},{128,160},{192,224},{1,33},{65,97},{129,161},{193,2... | collective-permute-start | bytes 393224 | tf_op jit(solution)/shard_map/while/body/eval_jaxpr/cond/branch_4_fun/ppermute | solution.py:326
  180.7 22.9 %all-to-all-start = ((bf16[32,32,256]{2,1,0:T(8,128)(2,1)}), bf16[32,32,256]{2,1,0:T(8,128)(2,1)S(1)}, u32[]{:S(2)}, u32[]{:S(2)}) async-start(bf16[32,32,256]{2,1,0:T(8,128)(2,1)} %get-tuple-element.755._), calls=%async_computation | async-start | bytes 1048576 | tf_op jit(solution)/shard_map/while/body/eval_jaxpr/all_to_all | solution.py:413
  196.4 0.7 copy-start.1
  203.7 1.0 copy-start.2
  204.6 0.9 copy-start.4
  217.7 7.6 %collective-permute-start.5 = (bf16[256,256]{1,0:T(8,128)(2,1)S(1)}, bf16[256,256]{1,0:T(8,128)(2,1)S(1)}, u32[]{:S(2)}, u32[]{:S(2)}) collective-permute-start(bf16[256,256]{1,0:T(8,128)(2,1)S(1)} %get-tuple-element.503), channel_id=1, source_target_pairs={{0,64},{32,96},{1,65},{33,97},{2,66},{34,98},{3,67},{35,99},{4,68}... | collective-permute-start | bytes 393224 | tf_op jit(solution)/shard_map/while/body/eval_jaxpr/cond/branch_0_fun/ppermute | solution.py:320
  219.0 6.9 %collective-permute-start.4 = (bf16[256,256]{1,0:T(8,128)(2,1)S(1)}, bf16[256,256]{1,0:T(8,128)(2,1)S(1)}, u32[]{:S(2)}, u32[]{:S(2)}) collective-permute-start(bf16[256,256]{1,0:T(8,128)(2,1)S(1)} %get-tuple-element.504), channel_id=1, source_target_pairs={{0,128},{32,160},{1,129},{33,161},{2,130},{34,162},{3,131},{35,163... | collective-permute-start | bytes 393224 | tf_op jit(solution)/shard_map/while/body/eval_jaxpr/cond/branch_0_fun/ppermute | solution.py:320
  219.7 6.3 %collective-permute-start.3 = (bf16[256,256]{1,0:T(8,128)(2,1)S(1)}, bf16[256,256]{1,0:T(8,128)(2,1)S(1)}, u32[]{:S(2)}, u32[]{:S(2)}) collective-permute-start(bf16[256,256]{1,0:T(8,128)(2,1)S(1)} %get-tuple-element.505), channel_id=1, source_target_pairs={{0,192},{32,224},{1,193},{33,225},{2,194},{34,226},{3,195},{35,227... | collective-permute-start | bytes 393224 | tf_op jit(solution)/shard_map/while/body/eval_jaxpr/cond/branch_0_fun/ppermute | solution.py:320
  220.4 14.6 %collective-permute-start.2 = (bf16[256,256]{1,0:T(8,128)(2,1)S(1)}, bf16[256,256]{1,0:T(8,128)(2,1)S(1)}, u32[]{:S(2)}, u32[]{:S(2)}) collective-permute-start(bf16[256,256]{1,0:T(8,128)(2,1)S(1)} %get-tuple-element.502), channel_id=1, source_target_pairs={{0,64},{32,96},{1,65},{33,97},{2,66},{34,98},{3,67},{35,99},{4,68}... | collective-permute-start | bytes 393224 | tf_op jit(solution)/shard_map/while/body/eval_jaxpr/cond/branch_0_fun/ppermute | solution.py:320
  221.7 13.3 %collective-permute-start.1 = (bf16[256,256]{1,0:T(8,128)(2,1)S(1)}, bf16[256,256]{1,0:T(8,128)(2,1)S(1)}, u32[]{:S(2)}, u32[]{:S(2)}) collective-permute-start(bf16[256,256]{1,0:T(8,128)(2,1)S(1)} %get-tuple-element.506), channel_id=1, source_target_pairs={{0,128},{32,160},{1,129},{33,161},{2,130},{34,162},{3,131},{35,163... | collective-permute-start | bytes 393224 | tf_op jit(solution)/shard_map/while/body/eval_jaxpr/cond/branch_0_fun/ppermute | solution.py:320
  225.3 9.7 %collective-permute-start = (bf16[256,256]{1,0:T(8,128)(2,1)S(1)}, bf16[256,256]{1,0:T(8,128)(2,1)S(1)}, u32[]{:S(2)}, u32[]{:S(2)}) collective-permute-start(bf16[256,256]{1,0:T(8,128)(2,1)S(1)} %get-tuple-element.507), channel_id=1, source_target_pairs={{0,192},{32,224},{1,193},{33,225},{2,194},{34,226},{3,195},{35,227... | collective-permute-start | bytes 393224 | tf_op jit(solution)/shard_map/while/body/eval_jaxpr/cond/branch_0_fun/ppermute | solution.py:320
  226.9 10.5 %collective-permute-start.6 = (bf16[256,256]{1,0:T(8,128)(2,1)S(1)}, bf16[256,256]{1,0:T(8,128)(2,1)S(1)}, u32[]{:S(2)}, u32[]{:S(2)}) collective-permute-start(bf16[256,256]{1,0:T(8,128)(2,1)S(1)} %fusion.1), channel_id=1, source_target_pairs={{0,32},{64,96},{128,160},{192,224},{1,33},{65,97},{129,161},{193,2... | collective-permute-start | bytes 393224 | tf_op jit(solution)/shard_map/while/body/eval_jaxpr/cond/branch_0_fun/ppermute | solution.py:326
  239.1 22.9 %all-to-all-start = ((bf16[32,32,256]{2,1,0:T(8,128)(2,1)}), bf16[32,32,256]{2,1,0:T(8,128)(2,1)S(1)}, u32[]{:S(2)}, u32[]{:S(2)}) async-start(bf16[32,32,256]{2,1,0:T(8,128)(2,1)} %get-tuple-element.755._), calls=%async_computation | async-start | bytes 1048576 | tf_op jit(solution)/shard_map/while/body/eval_jaxpr/all_to_all | solution.py:413
  254.7 0.7 copy-start.1
  261.9 1.0 copy-start.2
  262.9 0.9 copy-start.4
  (20 other events, 13.6 us)
where the time goes:
time: 271 us; the launch traced here: 270 us
  starting transfers between devices  82.7 us (31%)
  Pallas kernels  72.3 us (27%)
  waiting for transfers between devices  69.4 us (26%)
  local copies, waits for them, and re-layouts  31.7 us (12%)
  other arithmetic  10.8 us (4%)
  loops' own time  3.17 us (1%)
    pallas_call x19, Pallas kernels, call(): pl.pallas_call(kernel, out_shape=out_shape, grid_spec=pltpu.PrefetchScala...  72.3 us
    all_to_all x4, starting transfers between devices, batch(): lax.all_to_all(sent, 'row', 0, 0, tiled=True).reshape(rows * per, width)  27.2 us
    all_to_all x4, waiting for transfers between devices, batch(): lax.all_to_all(sent, 'row', 0, 0, tiled=True).reshape(rows * per, width)  26.1 us
    ppermute x24, waiting for transfers between devices, spread(): block = lax.ppermute(far_rows[2 * there + which], 'dom', pairs)  23.5 us
    ppermute x24, starting transfers between devices, spread(): block = lax.ppermute(far_rows[2 * there + which], 'dom', pairs)  21 us
    while x60, local copies, waits for them, and re-layouts  20.8 us
    ppermute x4, starting transfers between devices, body(): lax.ppermute(spread(1 - z), 'dom', [(2 * i + z, 2 * i + 1 - z) for i in r...  18.6 us
    all_to_all x1, starting transfers between devices, shards(): lax.all_to_all(ids.reshape(groups * rows, 1, batches * per), ('dom', 'row...  15.9 us
  transfers between devices with their start and end apart: 33, of which 14 were waited for; matrix products, arithmetic and copies ran while one was open for 3% of the time, Pallas kernels for 11%

commit v1 on v0

--- a/solution.py
+++ b/solution.py
@@ -66,7 +66,7 @@
     )
 
 
-def plan_kernel(cap, ocap, node_dev, source_ref, ids_ref, pcode_ref):
+def plan_kernel(cap, ocap, node_dev, flip_ref, source_ref, ids_ref, pcode_ref):
     batches, events = source_ref.shape
     rows = ids_ref.shape[1]
     per = cap + ocap
@@ -96,7 +96,7 @@
         spot = (slot + b * per == lane_iota).astype(F32)
         high = high + dot_nt(both, (spot * (offset >> 6).astype(F32)).astype(BF16))
         low = low + dot_nt(both, (spot * (offset & 63).astype(F32)).astype(BF16))
-        places.append(dest * per + slot)
+        places.append(jnp.where(far, dest ^ flip_ref[b], dest) * per + slot)
     ids = high.astype(I32) * 64 + low.astype(I32)
     for g in range(ids_ref.shape[0]):
         ids_ref[g] = ids
@@ -172,7 +172,6 @@
     gcode_ref,
     scode_ref,
     same_ref,
-    count_ref,
 ):
     b = at_ref[0]
     batches, events = target_ref.shape
@@ -211,9 +210,6 @@
     same = (tcol == trow) & (trow >= 0)
     samef = same.astype(F32)
     same_ref[...] = samef.astype(BF16)
-    count_ref[...] = jnp.broadcast_to(
-        jnp.maximum(jnp.sum(samef, axis=1, keepdims=True), 1.0), (events, LANES)
-    )
     earlier = jnp.max(jnp.where(sub < lane, samef, 0.0), axis=0, keepdims=True)
     first = jnp.where(earlier > 0.0, -1, trow)
     sub128 = lax.broadcasted_iota(I32, (LANES, events), 0)
@@ -222,24 +218,27 @@
     ).astype(BF16)
 
 
-def serve_rows(table_ref, code_ref, out_ref, step):
+def serve_rows(table_ref, code_ref, out_refs, step):
     blocks = table_ref.shape[0] // LANES
     table = table_ref[...]
+    rows = out_refs[0].shape[0]
     for start in range(0, code_ref.shape[0], step):
-        picked = dot(expand(code_ref[start : start + step, :], 0, blocks), table)
-        out_ref[start : start + step, :] = picked.astype(BF16)
-
-
-def serve_kernel(table_ref, own_code_ref, far_code_ref, own_ref, far_ref):
-    serve_rows(table_ref, own_code_ref, own_ref, 256)
-    serve_rows(table_ref, far_code_ref, far_ref, 512)
-
-
-def local_kernel(table_ref, gcode_ref, base_ref, w_ref, mem_ref, out_ref):
+        picked = dot(expand(code_ref[start : start + step, :], 0, blocks), table).astype(BF16)
+        for part in range(0, step, rows):
+            out_refs[(start + part) // rows][...] = picked[part : part + rows]
+
+
+def serve_kernel(table_ref, own_code_ref, far_code_ref, own_ref, *far_refs):
+    serve_rows(table_ref, own_code_ref, [own_ref.at[i : i + 256] for i in range(0, own_ref.shape[0], 256)], 256)
+    serve_rows(table_ref, far_code_ref, far_refs, 512)
+
+
+def local_kernel(table_ref, gcode_ref, base_ref, w_ref, out_ref):
     blocks = table_ref.shape[0] // LANES
-    mem = dot(expand(gcode_ref[...], 0, blocks), table_ref[...]).astype(BF16)
-    mem_ref[...] = mem
-    out_ref[...] = base_ref[...] + dot(mem, w_ref[: mem.shape[1], :])
+    width = table_ref.shape[1]
+    mem = dot(expand(gcode_ref[...], 0, blocks), table_ref[...])
+    out_ref[:, :width] = base_ref[...] + dot(mem.astype(BF16), w_ref[:width, :])
+    out_ref[:, width:] = mem
 
 
 def update_kernel(
@@ -248,10 +247,8 @@
     table_ref,
     back_ref,
     pcode_ref,
-    base_ref,
-    mem_ref,
+    local_ref,
     same_ref,
-    count_ref,
     scode_ref,
     w_ref,
     w_input_ref,
@@ -262,21 +259,23 @@
     far_code_ref,
     new_ref,
     own_out_ref,
-    far_out_ref,
+    *far_out_refs,
 ):
     width = table_ref.shape[1]
-    mem = mem_ref[...]
-    hidden = dot(mem, w_hidden_ref[...]) + bias_hidden_ref[...]
+    mem = local_ref[:, width:]
+    hidden = dot(mem.astype(BF16), w_hidden_ref[...]) + bias_hidden_ref[...]
     source = dot(expand(pcode_ref[0], 0, back_ref.shape[0] // LANES), back_ref[...])
     w_source = w_ref[width : 2 * width, :]
-    message = (base_ref[...] + dot(source.astype(BF16), w_source)).astype(BF16)
-    total = dot(same_ref[...], message)
-    averaged = (total / count_ref[:, :1]).astype(BF16)
+    message = (local_ref[:, :width] + dot(source.astype(BF16), w_source)).astype(BF16)
+    same = same_ref[...]
+    total = dot(same, message)
+    count = jnp.maximum(dot(same, jnp.ones((same.shape[0], LANES), BF16))[:, :1], 1.0)
+    averaged = (total / count).astype(BF16)
     gates = dot(averaged, w_input_ref[...]) + bias_input_ref[...]
     reset = jax.nn.sigmoid(gates[:, :width] + hidden[:, :width])
     update = jax.nn.sigmoid(gates[:, width : 2 * width] + hidden[:, width : 2 * width])
     candidate = jnp.tanh(gates[:, 2 * width :] + reset * hidden[:, 2 * width :])
-    fresh = ((1.0 - update) * candidate + update * mem.astype(F32)).astype(BF16)
+    fresh = ((1.0 - update) * candidate + update * mem).astype(BF16)
     ones = jnp.ones((fresh.shape[0], LANES), BF16)
     placed = jnp.concatenate([fresh, ones], axis=1)
     scode = scode_ref[...]
@@ -296,18 +295,17 @@
 
     @pl.when(at_ref[0] < last)
     def _():
-        serve_rows(new_ref, own_code_ref, own_out_ref, 256)
-        serve_rows(new_ref, far_code_ref, far_out_ref, 512)
-
-
-def from_owner(own_rows, far_rows, owner, cap):
+        serve_kernel(new_ref, own_code_ref, far_code_ref, own_out_ref, *far_out_refs)
+
+
+def from_owner(own_rows, far_rows, owner, cap, turn):
     rows, _, width = own_rows.shape
-    ys = far_rows.shape[0] // 2
+    ys = len(far_rows) // 2
 
     def branch(root):
         y, z = root // 2, root % 2
 
-        def body(own_rows, far_rows):
+        def body(own_rows, *far_rows):
             me = lax.axis_index("dom")
             my_y, my_z = me >> 1, me & 1
 
@@ -324,14 +322,20 @@
                 return part
 
             across = lax.ppermute(
-                spread(1 - z), "dom", [(2 * i + z, 2 * i + 1 - z) for i in range(ys)]
+                spread(1 - z),
+                ("dom", "row"),
+                [
+                    ((2 * i + z) * rows + r, (2 * i + 1 - z) * rows + (r ^ turn))
+                    for i in range(ys)
+                    for r in range(rows)
+                ],
             )
             mine = jnp.where(my_z == z, spread(z), across)
             return own_rows.at[:, cap:, :].set(mine.reshape(rows, -1, width))
 
         return body
 
-    return lax.switch(owner, [branch(r) for r in range(2 * ys)], own_rows, far_rows)
+    return lax.switch(owner, [branch(r) for r in range(2 * ys)], own_rows, *far_rows)
 
 
 def shards(
@@ -360,16 +364,19 @@
     shape = jax.ShapeDtypeStruct
     code = shape((events, LANES), BF16)
 
+    me = lax.axis_index("dom").astype(I32)
+    turn = rows - rows // 4
+    flip = jnp.where((owner_group & 1) == (me & 1), 0, turn).astype(I32)
     ids, pcode = call(
         functools.partial(plan_kernel, cap, ocap, node_dev),
         (shape((groups, rows, batches * per), I32), shape((batches, events, LANES), BF16)),
         (source,),
         name="plan",
+        scalars=(flip,),
     )
     asked = lax.all_to_all(
         ids.reshape(groups * rows, 1, batches * per), ("dom", "row"), 0, 0, tiled=True
     ).reshape(groups, rows, batches * per)
-    me = lax.axis_index("dom").astype(I32)
     times_row = node_time.reshape(1, node_dev)
     freq_row = frequency.reshape(1, -1)
     phase_row = phase_shift.reshape(1, -1)
@@ -392,33 +399,33 @@
         )
 
     own_shape = shape((rows * per, width), BF16)
-    far_shape = shape((groups * rows * ocap, width), BF16)
-    own_rows, far_rows = call(
+    far_shape = (shape((rows * ocap, width), BF16),) * groups
+    own_rows, *far_rows = call(
         serve_kernel,
-        (own_shape, far_shape),
+        (own_shape,) + far_shape,
         (memory,) + tuple(codes(jnp.zeros((), I32), asked)),
         flops=4 * 10**9,
         name="serve",
     )
 
     def batch(b, carry):
-        table, own_rows, far_rows = carry
+        table, own_rows, *far_rows = carry
         at = b.reshape(1)
         sent = from_owner(
             own_rows.reshape(rows, per, width),
-            far_rows.reshape(groups, rows * ocap, width),
+            far_rows,
             lax.dynamic_index_in_dim(owner_group, b, 0, keepdims=False),
             cap,
+            turn,
         )
         back = lax.all_to_all(sent, "row", 0, 0, tiled=True).reshape(rows * per, width)
-        base, gcode, scode, same, count = call(
+        base, gcode, scode, same = call(
             functools.partial(prep_kernel, width),
             (
                 shape((events, width), F32),
                 code,
                 shape((LANES, events), BF16),
                 shape((events, events), BF16),
-                shape((events, LANES), F32),
             ),
             (target, event_time, times_row, edge_feat, freq_row, phase_row, w_message, sent),
             flops=3 * 10**9,
@@ -429,9 +436,9 @@
             },
             scalars=(at,),
         )
-        mem, local = call(
+        local = call(
             local_kernel,
-            (shape((events, width), BF16), shape((events, width), F32)),
+            shape((events, 2 * width), F32),
             (table, gcode, base, w_message),
             flops=3 * 10**9,
             name="local",
@@ -439,15 +446,13 @@
         own_code, far_code = codes(b + 1, sent)
         return call(
             functools.partial(update_kernel, batches - 1),
-            (shape((node_dev, width), BF16), own_shape, far_shape),
+            (shape((node_dev, width), BF16), own_shape) + far_shape,
             (
                 table,
                 back,
                 pcode,
                 local,
-                mem,
                 same,
-                count,
                 scode,
                 w_message,
                 w_input,
@@ -463,7 +468,7 @@
             scalars=(at,),
         )
 
-    return lax.fori_loop(0, batches, batch, (memory, own_rows, far_rows))[0]
+    return lax.fori_loop(0, batches, batch, (memory, own_rows, *far_rows))[0]
 
 
 def solution(mesh):

time: 271 us -> 264 us (0.974); the launches traced: 270 us -> 260 us
  local copies, waits for them, and re-layouts: 31.7 us -> 21.9 us
  starting transfers between devices: 82.7 us -> 74.3 us
  waiting for transfers between devices: 69.4 us -> 77.2 us
    ppermute x4, starting transfers between devices: 18.6 us -> 10.1 us  [body(): lax.ppermute(spread(1 - z), ('dom', 'row'), [((2 * i + z) * rows + r, (2...]
    ppermute x4, waiting for transfers between devices: 9.6 us -> 17.8 us  [body(): lax.ppermute(spread(1 - z), ('dom', 'row'), [((2 * i + z) * rows + r, (2...]
    while x60 -> x52, local copies, waits for them, and re-layouts: 20.8 us -> 15 us
    ppermute x24, starting transfers between devices: 21 us -> 26.6 us  [spread(): block = lax.ppermute(far_rows[2 * there + which], 'dom', pairs)]
    all_to_all x4, starting transfers between devices: 27.2 us -> 21.7 us  [batch(): lax.all_to_all(sent, 'row', 0, 0, tiled=True).reshape(rows * per, width)]
    squeeze x4 -> x0, local copies, waits for them, and re-layouts: 5.03 us -> none  [spread(): block = lax.ppermute(far_rows[2 * there + which], 'dom', pairs)]
    ppermute x24, waiting for transfers between devices: 23.5 us -> 20.6 us  [spread(): block = lax.ppermute(far_rows[2 * there + which], 'dom', pairs)]
  transfers between devices with their start and end apart: 33 -> 33, of which waited for: 14 -> 15; matrix products, arithmetic and copies ran while one was open for 3% -> 3% of each run, Pallas kernels for 11% -> 11%
where the time goes in v1:
time: 264 us; the launch traced here: 260 us
  waiting for transfers between devices  77.2 us (29%)
  starting transfers between devices  74.3 us (28%)
  Pallas kernels  74.2 us (28%)
  local copies, waits for them, and re-layouts  21.9 us (8%)
  other arithmetic  9.13 us (3%)
  loops' own time  3.3 us (1%)
    pallas_call x19, Pallas kernels, call(): pl.pallas_call(kernel, out_shape=out_shape, grid_spec=pltpu.PrefetchScala...  74.2 us
    all_to_all x4, waiting for transfers between devices, batch(): lax.all_to_all(sent, 'row', 0, 0, tiled=True).reshape(rows * per, width)  28.5 us
    ppermute x24, starting transfers between devices, spread(): block = lax.ppermute(far_rows[2 * there + which], 'dom', pairs)  26.6 us
    all_to_all x4, starting transfers between devices, batch(): lax.all_to_all(sent, 'row', 0, 0, tiled=True).reshape(rows * per, width)  21.7 us
    ppermute x24, waiting for transfers between devices, spread(): block = lax.ppermute(far_rows[2 * there + which], 'dom', pairs)  20.6 us
    ppermute x4, waiting for transfers between devices, body(): lax.ppermute(spread(1 - z), ('dom', 'row'), [((2 * i + z) * rows + r, (2...  17.8 us
    all_to_all x1, starting transfers between devices, shards(): lax.all_to_all(ids.reshape(groups * rows, 1, batches * per), ('dom', 'row...  15.9 us
    while x52, local copies, waits for them, and re-layouts  15 us
  transfers between devices with their start and end apart: 33, of which 15 were waited for; matrix products, arithmetic and copies ran while one was open for 3% of the time, Pallas kernels for 11%

profile of v1, /device:TPU:9, one launch (start us, length us, event | category | flops | bytes accessed | tf_op | source)
XLA Modules:
  0.0 260.3 jit_solution(15123175141292519390)
XLA Ops:
  0.0 2.3 copy.68.table_ref
  3.0 3.1 %plan.1 = (s32[8,32,128]{2,1,0:T(8,128)}, bf16[4,512,128]{2,1,0:T(8,128)(2,1)}) custom-call(s32[4]{0:T(128)S(1)} %compare_select_fusion.flip_ref, s32[4,512]{1,0:T(4,128)S(1)} %copy-done), custom_call_target="tpu_custom_call" | custom-call | bytes 663552 | tf_op jit(solution)/shard_map/plan/pallas_call | solution.py:26
  6.1 15.9 %all-to-all-start.1 = ((s32[256,1,128]{2,1,0:T(1,128)}), s32[256,1,128]{2,1,0:T(1,128)}, u32[]{:S(2)}, u32[]{:S(2)}) async-start(s32[256,1,128]{2,1,0:T(1,128)} %bitcast.16), calls=%async_computation.1 | async-start | bytes 262144 | tf_op jit(solution)/shard_map/all_to_all | solution.py:377
  22.8 10.4 %all-to-all-done.1 = s32[256,1,128]{2,1,0:T(1,128)} async-done(((s32[256,1,128]{2,1,0:T(1,128)}), s32[256,1,128]{2,1,0:T(1,128)}, u32[]{:S(2)}, u32[]{:S(2)}) %all-to-all-start.1) | async-done | bytes 131104 | tf_op jit(solution)/shard_map/all_to_all | solution.py:377
  33.2 2.5 codes.6
  35.8 5.5 %serve.1 = (bf16[1024,256]{1,0:T(8,128)(2,1)}, bf16[256,256]{1,0:T(8,128)(2,1)}, bf16[256,256]{1,0:T(8,128)(2,1)}, bf16[256,256]{1,0:T(8,128)(2,1)}, bf16[256,25...) custom-call(bf16[2048,256]{1,0:T(8,128)(2,1)} %copy.68.table_ref, ...), custom_call_target="tpu_custom_call" | custom-call | flops 4000000000 | bytes 3407872 | tf_op jit(solution)/shard_map/serve/pallas_call | solution.py:26
  42.0 218.2 %while.39 = (s32[]{:T(128)}, bf16[2048,256]{1,0:T(8,128)(2,1)}, bf16[1024,256]{1,0:T(8,128)(2,1)}, bf16[256,256]{1,0:T(8,128)(2,1)}, bf16[256,256]{1,0:T(8,128)(...) while((s32[]{:T(128)}, bf16[2048,256]{1,0:T(8,128)(2,1)}, ...), condition=%wide.region_9.10_spmd, body=%wide.region_0.9_spmd.sunk | while | flops 14000458752 | bytes 28805660 | solution.py:471
  43.2 17.5 %conditional.2 = (bf16[32,32,256]{2,1,0:T(8,128)(2,1)}) conditional(s32[]{:T(128)} %bitcast.37, (bf16[256,256]{1,0:T(8,128)(2,1)}, bf16[256,256]{1,0:T(8,128)(2,1)}, bf16[256,256]{1,0:T(8,128)(2,1)}, bf16[256,256]{1,0:T(8,128)(2,1)}, bf16[256,256]{1,0:T(8,128)(2,1)}, /*index=5*/bf16[256,256]{1,0:T(8,128)(2,1)}, ...), branch_computations={%region_1.1_spmd, %region_2.2_spmd, %region_3.3_spmd, %region_4.4_... | conditional | flops 458761 | bytes 5112195 | solution.py:338
  48.6 5.5 %collective-permute-done.5 = bf16[256,256]{1,0:T(8,128)(2,1)S(1)} collective-permute-done((bf16[256,256]{1,0:T(8,128)(2,1)}, bf16[256,256]{1,0:T(8,128)(2,1)S(1)}, u32[]{:S(2)}, u32[]{:S(2)}) %collective-permute-start.5) | collective-permute-done | bytes 131104 | tf_op jit(solution)/shard_map/while/body/eval_jaxpr/cond/branch_0_fun/ppermute | solution.py:318
  54.2 2.5 collective-permute-start.6
  56.7 3.0 %collective-permute-done.2 = bf16[256,256]{1,0:T(8,128)(2,1)S(1)} collective-permute-done((bf16[256,256]{1,0:T(8,128)(2,1)}, bf16[256,256]{1,0:T(8,128)(2,1)S(1)}, u32[]{:S(2)}, u32[]{:S(2)}) %collective-permute-start.2) | collective-permute-done | bytes 131104 | tf_op jit(solution)/shard_map/while/body/eval_jaxpr/cond/branch_0_fun/ppermute | solution.py:318
  60.8 7.0 %all-to-all-start = ((bf16[32,32,256]{2,1,0:T(8,128)(2,1)}), bf16[32,32,256]{2,1,0:T(8,128)(2,1)S(1)}, u32[]{:S(2)}, u32[]{:S(2)}) async-start(bf16[32,32,256]{2,1,0:T(8,128)(2,1)} %get-tuple-element.1097._), calls=%async_computation | async-start | bytes 1048576 | tf_op jit(solution)/shard_map/while/body/eval_jaxpr/all_to_all | solution.py:421
  69.1 2.5 codes.7
  71.6 2.8 %prep.5 = (f32[512,256]{1,0:T(8,128)S(1)}, bf16[512,128]{1,0:T(8,128)(2,1)S(1)}, bf16[128,512]{1,0:T(8,128)(2,1)S(1)}, bf16[512,512]{1,0:T(8,128)(2,1)S(1)}) custom-call(s32[1]{0:T(128)} %bitcast.36.at_ref, s32[4,512]{1,0:T(4,128)S(1)} %get-tuple-element.1080.target_ref, s32[4,512]{1,0:T(4,128)S(1)} %get-tuple-element.1081.time_ref, ...), custom_call_target="tpu_custom_call" | custom-call | flops 3000000000 | bytes 2778112 | tf_op jit(solution)/shard_map/while/body/eval_jaxpr/prep/pallas_call | solution.py:26
  75.2 1.9 local.1.local_ref
  77.1 7.1 %all-to-all-done = bf16[32,32,256]{2,1,0:T(8,128)(2,1)S(1)} async-done(((bf16[32,32,256]{2,1,0:T(8,128)(2,1)}), bf16[32,32,256]{2,1,0:T(8,128)(2,1)S(1)}, u32[]{:S(2)}, u32[]{:S(2)}) %all-to-all-start) | async-done | bytes 524320 | tf_op jit(solution)/shard_map/while/body/eval_jaxpr/all_to_all | solution.py:421
  85.2 9.4 %update.5 = (bf16[2048,256]{1,0:T(8,128)(2,1)}, bf16[1024,256]{1,0:T(8,128)(2,1)}, bf16[256,256]{1,0:T(8,128)(2,1)}, bf16[256,256]{1,0:T(8,128)(2,1)}, bf16[256,...) custom-call(s32[1]{0:T(128)} %bitcast.36.at_ref, ...), custom_call_target="tpu_custom_call" | custom-call | flops 6000000000 | bytes 8394752 | tf_op jit(solution)/shard_map/while/body/eval_jaxpr/update/pallas_call | solution.py:26
  96.6 24.6 %conditional.2 = (bf16[32,32,256]{2,1,0:T(8,128)(2,1)}) conditional(s32[]{:T(128)} %bitcast.37, (bf16[256,256]{1,0:T(8,128)(2,1)}, bf16[256,256]{1,0:T(8,128)(2,1)}, bf16[256,256]{1,0:T(8,128)(2,1)}, bf16[256,256]{1,0:T(8,128)(2,1)}, bf16[256,256]{1,0:T(8,128)(2,1)}, /*index=5*/bf16[256,256]{1,0:T(8,128)(2,1)}, ...), branch_computations={%region_1.1_spmd, %region_2.2_spmd, %region_3.3_spmd, %region_4.4_... | conditional | flops 458761 | bytes 5112195 | solution.py:338
  102.0 4.8 %collective-permute-done.53 = bf16[256,256]{1,0:T(8,128)(2,1)S(1)} collective-permute-done((bf16[256,256]{1,0:T(8,128)(2,1)}, bf16[256,256]{1,0:T(8,128)(2,1)S(1)}, u32[]{:S(2)}, u32[]{:S(2)}) %collective-permute-start.53) | collective-permute-done | bytes 131104 | tf_op jit(solution)/shard_map/while/body/eval_jaxpr/cond/branch_7_fun/ppermute | solution.py:318
  109.1 3.4 %collective-permute-done.50 = bf16[256,256]{1,0:T(8,128)(2,1)S(1)} collective-permute-done((bf16[256,256]{1,0:T(8,128)(2,1)}, bf16[256,256]{1,0:T(8,128)(2,1)S(1)}, u32[]{:S(2)}, u32[]{:S(2)}) %collective-permute-start.50) | collective-permute-done | bytes 131104 | tf_op jit(solution)/shard_map/while/body/eval_jaxpr/cond/branch_7_fun/ppermute | solution.py:318
  112.5 7.1 %collective-permute-done.55 = bf16[256,256]{1,0:T(8,128)(2,1)S(1)} collective-permute-done((bf16[256,256]{1,0:T(8,128)(2,1)S(1)}, bf16[256,256]{1,0:T(8,128)(2,1)S(1)}, u32[]{:S(2)}, u32[]{:S(2)}) %collective-permute-start.55) | collective-permute-done | bytes 131104 | tf_op jit(solution)/shard_map/while/body/eval_jaxpr/cond/branch_7_fun/ppermute | solution.py:324
  119.6 1.7 bitcast_dynamic-update-slice_fusion.7
  121.3 5.0 %all-to-all-start = ((bf16[32,32,256]{2,1,0:T(8,128)(2,1)}), bf16[32,32,256]{2,1,0:T(8,128)(2,1)S(1)}, u32[]{:S(2)}, u32[]{:S(2)}) async-start(bf16[32,32,256]{2,1,0:T(8,128)(2,1)} %get-tuple-element.1097._), calls=%async_computation | async-start | bytes 1048576 | tf_op jit(solution)/shard_map/while/body/eval_jaxpr/all_to_all | solution.py:421
  127.6 2.5 codes.7
  130.1 2.8 %prep.5 = (f32[512,256]{1,0:T(8,128)S(1)}, bf16[512,128]{1,0:T(8,128)(2,1)S(1)}, bf16[128,512]{1,0:T(8,128)(2,1)S(1)}, bf16[512,512]{1,0:T(8,128)(2,1)S(1)}) custom-call(s32[1]{0:T(128)} %bitcast.36.at_ref, s32[4,512]{1,0:T(4,128)S(1)} %get-tuple-element.1080.target_ref, s32[4,512]{1,0:T(4,128)S(1)} %get-tuple-element.1081.time_ref, ...), custom_call_target="tpu_custom_call" | custom-call | flops 3000000000 | bytes 2778112 | tf_op jit(solution)/shard_map/while/body/eval_jaxpr/prep/pallas_call | solution.py:26
  133.7 1.9 local.1.local_ref
  135.6 7.1 %all-to-all-done = bf16[32,32,256]{2,1,0:T(8,128)(2,1)S(1)} async-done(((bf16[32,32,256]{2,1,0:T(8,128)(2,1)}), bf16[32,32,256]{2,1,0:T(8,128)(2,1)S(1)}, u32[]{:S(2)}, u32[]{:S(2)}) %all-to-all-start) | async-done | bytes 524320 | tf_op jit(solution)/shard_map/while/body/eval_jaxpr/all_to_all | solution.py:421
  143.7 9.4 %update.5 = (bf16[2048,256]{1,0:T(8,128)(2,1)}, bf16[1024,256]{1,0:T(8,128)(2,1)}, bf16[256,256]{1,0:T(8,128)(2,1)}, bf16[256,256]{1,0:T(8,128)(2,1)}, bf16[256,...) custom-call(s32[1]{0:T(128)} %bitcast.36.at_ref, ...), custom_call_target="tpu_custom_call" | custom-call | flops 6000000000 | bytes 8394752 | tf_op jit(solution)/shard_map/while/body/eval_jaxpr/update/pallas_call | solution.py:26
  155.1 17.9 %conditional.2 = (bf16[32,32,256]{2,1,0:T(8,128)(2,1)}) conditional(s32[]{:T(128)} %bitcast.37, (bf16[256,256]{1,0:T(8,128)(2,1)}, bf16[256,256]{1,0:T(8,128)(2,1)}, bf16[256,256]{1,0:T(8,128)(2,1)}, bf16[256,256]{1,0:T(8,128)(2,1)}, bf16[256,256]{1,0:T(8,128)(2,1)}, /*index=5*/bf16[256,256]{1,0:T(8,128)(2,1)}, ...), branch_computations={%region_1.1_spmd, %region_2.2_spmd, %region_3.3_spmd, %region_4.4_... | conditional | flops 458761 | bytes 5112195 | solution.py:338
  159.8 2.8 %collective-permute-done.31 = bf16[256,256]{1,0:T(8,128)(2,1)S(1)} collective-permute-done((bf16[256,256]{1,0:T(8,128)(2,1)}, bf16[256,256]{1,0:T(8,128)(2,1)S(1)}, u32[]{:S(2)}, u32[]{:S(2)}) %collective-permute-start.31) | collective-permute-done | bytes 131104 | tf_op jit(solution)/shard_map/while/body/eval_jaxpr/cond/branch_4_fun/ppermute | solution.py:318
  166.5 4.8 %collective-permute-done.34 = bf16[256,256]{1,0:T(8,128)(2,1)S(1)} collective-permute-done((bf16[256,256]{1,0:T(8,128)(2,1)S(1)}, bf16[256,256]{1,0:T(8,128)(2,1)S(1)}, u32[]{:S(2)}, u32[]{:S(2)}) %collective-permute-start.34) | collective-permute-done | bytes 131104 | tf_op jit(solution)/shard_map/while/body/eval_jaxpr/cond/branch_4_fun/ppermute | solution.py:324
  171.4 1.7 bitcast_dynamic-update-slice_fusion.4
  173.0 4.2 %all-to-all-start = ((bf16[32,32,256]{2,1,0:T(8,128)(2,1)}), bf16[32,32,256]{2,1,0:T(8,128)(2,1)S(1)}, u32[]{:S(2)}, u32[]{:S(2)}) async-start(bf16[32,32,256]{2,1,0:T(8,128)(2,1)} %get-tuple-element.1097._), calls=%async_computation | async-start | bytes 1048576 | tf_op jit(solution)/shard_map/while/body/eval_jaxpr/all_to_all | solution.py:421
  178.6 2.5 codes.7
  181.1 2.8 %prep.5 = (f32[512,256]{1,0:T(8,128)S(1)}, bf16[512,128]{1,0:T(8,128)(2,1)S(1)}, bf16[128,512]{1,0:T(8,128)(2,1)S(1)}, bf16[512,512]{1,0:T(8,128)(2,1)S(1)}) custom-call(s32[1]{0:T(128)} %bitcast.36.at_ref, s32[4,512]{1,0:T(4,128)S(1)} %get-tuple-element.1080.target_ref, s32[4,512]{1,0:T(4,128)S(1)} %get-tuple-element.1081.time_ref, ...), custom_call_target="tpu_custom_call" | custom-call | flops 3000000000 | bytes 2778112 | tf_op jit(solution)/shard_map/while/body/eval_jaxpr/prep/pallas_call | solution.py:26
  184.7 1.9 local.1.local_ref
  186.6 7.2 %all-to-all-done = bf16[32,32,256]{2,1,0:T(8,128)(2,1)S(1)} async-done(((bf16[32,32,256]{2,1,0:T(8,128)(2,1)}), bf16[32,32,256]{2,1,0:T(8,128)(2,1)S(1)}, u32[]{:S(2)}, u32[]{:S(2)}) %all-to-all-start) | async-done | bytes 524320 | tf_op jit(solution)/shard_map/while/body/eval_jaxpr/all_to_all | solution.py:421
  194.8 9.4 %update.5 = (bf16[2048,256]{1,0:T(8,128)(2,1)}, bf16[1024,256]{1,0:T(8,128)(2,1)}, bf16[256,256]{1,0:T(8,128)(2,1)}, bf16[256,256]{1,0:T(8,128)(2,1)}, bf16[256,...) custom-call(s32[1]{0:T(128)} %bitcast.36.at_ref, ...), custom_call_target="tpu_custom_call" | custom-call | flops 6000000000 | bytes 8394752 | tf_op jit(solution)/shard_map/while/body/eval_jaxpr/update/pallas_call | solution.py:26
  206.2 24.3 %conditional.2 = (bf16[32,32,256]{2,1,0:T(8,128)(2,1)}) conditional(s32[]{:T(128)} %bitcast.37, (bf16[256,256]{1,0:T(8,128)(2,1)}, bf16[256,256]{1,0:T(8,128)(2,1)}, bf16[256,256]{1,0:T(8,128)(2,1)}, bf16[256,256]{1,0:T(8,128)(2,1)}, bf16[256,256]{1,0:T(8,128)(2,1)}, /*index=5*/bf16[256,256]{1,0:T(8,128)(2,1)}, ...), branch_computations={%region_1.1_spmd, %region_2.2_spmd, %region_3.3_spmd, %region_4.4_... | conditional | flops 458761 | bytes 5112195 | solution.py:338
  206.3 4.3 %collective-permute-start.17 = (bf16[256,256]{1,0:T(8,128)(2,1)}, bf16[256,256]{1,0:T(8,128)(2,1)S(1)}, u32[]{:S(2)}, u32[]{:S(2)}) collective-permute-start(bf16[256,256]{1,0:T(8,128)(2,1)} %get-tuple-element.649), channel_id=1, source_target_pairs={{64,0},{96,32},{65,1},{97,33},{66,2},{98,34},{67,3},{99,35},{68,4}... | collective-permute-start | bytes 393224 | tf_op jit(solution)/shard_map/while/body/eval_jaxpr/cond/branch_2_fun/ppermute | solution.py:318
  218.1 5.0 %collective-permute-start.20 = (bf16[256,256]{1,0:T(8,128)(2,1)S(1)}, bf16[256,256]{1,0:T(8,128)(2,1)S(1)}, u32[]{:S(2)}, u32[]{:S(2)}) collective-permute-start(bf16[256,256]{1,0:T(8,128)(2,1)S(1)} %select_select_fusion.2), channel_id=1, source_target_pairs={{0,56},{1,57},{2,58},{3,59},{4,60},{5,61},{6,62},{7,63},{8,48},{9,... | collective-permute-start | bytes 393224 | tf_op jit(solution)/shard_map/while/body/eval_jaxpr/cond/branch_2_fun/ppermute | solution.py:324
  223.2 5.6 %collective-permute-done.20 = bf16[256,256]{1,0:T(8,128)(2,1)S(1)} collective-permute-done((bf16[256,256]{1,0:T(8,128)(2,1)S(1)}, bf16[256,256]{1,0:T(8,128)(2,1)S(1)}, u32[]{:S(2)}, u32[]{:S(2)}) %collective-permute-start.20) | collective-permute-done | bytes 131104 | tf_op jit(solution)/shard_map/while/body/eval_jaxpr/cond/branch_2_fun/ppermute | solution.py:324
  230.5 5.5 %all-to-all-start = ((bf16[32,32,256]{2,1,0:T(8,128)(2,1)}), bf16[32,32,256]{2,1,0:T(8,128)(2,1)S(1)}, u32[]{:S(2)}, u32[]{:S(2)}) async-start(bf16[32,32,256]{2,1,0:T(8,128)(2,1)} %get-tuple-element.1097._), calls=%async_computation | async-start | bytes 1048576 | tf_op jit(solution)/shard_map/while/body/eval_jaxpr/all_to_all | solution.py:421
  237.3 2.5 codes.7
  239.8 2.8 %prep.5 = (f32[512,256]{1,0:T(8,128)S(1)}, bf16[512,128]{1,0:T(8,128)(2,1)S(1)}, bf16[128,512]{1,0:T(8,128)(2,1)S(1)}, bf16[512,512]{1,0:T(8,128)(2,1)S(1)}) custom-call(s32[1]{0:T(128)} %bitcast.36.at_ref, s32[4,512]{1,0:T(4,128)S(1)} %get-tuple-element.1080.target_ref, s32[4,512]{1,0:T(4,128)S(1)} %get-tuple-element.1081.time_ref, ...), custom_call_target="tpu_custom_call" | custom-call | flops 3000000000 | bytes 2778112 | tf_op jit(solution)/shard_map/while/body/eval_jaxpr/prep/pallas_call | solution.py:26
  243.4 1.9 local.1.local_ref
  245.3 7.1 %all-to-all-done = bf16[32,32,256]{2,1,0:T(8,128)(2,1)S(1)} async-done(((bf16[32,32,256]{2,1,0:T(8,128)(2,1)}), bf16[32,32,256]{2,1,0:T(8,128)(2,1)S(1)}, u32[]{:S(2)}, u32[]{:S(2)}) %all-to-all-start) | async-done | bytes 524320 | tf_op jit(solution)/shard_map/while/body/eval_jaxpr/all_to_all | solution.py:421
  253.4 6.0 %update.5 = (bf16[2048,256]{1,0:T(8,128)(2,1)}, bf16[1024,256]{1,0:T(8,128)(2,1)}, bf16[256,256]{1,0:T(8,128)(2,1)}, bf16[256,256]{1,0:T(8,128)(2,1)}, bf16[256,...) custom-call(s32[1]{0:T(128)} %bitcast.36.at_ref, ...), custom_call_target="tpu_custom_call" | custom-call | flops 6000000000 | bytes 8394752 | tf_op jit(solution)/shard_map/while/body/eval_jaxpr/update/pallas_call | solution.py:26
  (131 shorter events, 51.5 us)
Async XLA Ops:
  6.1 15.9 %copy-start.3 = (f32[768]{0:T(1024)S(1)}, f32[768]{0:T(1024)}, u32[]{:S(2)}) copy-start(f32[768]{0:T(1024)} %param.52) | copy-start | bytes 9220
  6.1 27.1 %all-to-all-start.1 = ((s32[256,1,128]{2,1,0:T(1,128)}), s32[256,1,128]{2,1,0:T(1,128)}, u32[]{:S(2)}, u32[]{:S(2)}) async-start(s32[256,1,128]{2,1,0:T(1,128)} %bitcast.16), calls=%async_computation.1 | async-start | bytes 262144 | tf_op jit(solution)/shard_map/all_to_all | solution.py:377
  35.7 5.5 %copy-start.8 = (s32[2048]{0:T(1024)S(1)}, s32[2048]{0:T(1024)}, u32[]{:S(2)}) copy-start(s32[2048]{0:T(1024)} %param.41) | copy-start | bytes 24580
  41.2 0.7 copy-start.5
  41.2 0.7 copy-start.12
  43.2 4.0 %collective-permute-start.3 = (bf16[256,256]{1,0:T(8,128)(2,1)}, bf16[256,256]{1,0:T(8,128)(2,1)S(1)}, u32[]{:S(2)}, u32[]{:S(2)}) collective-permute-start(bf16[256,256]{1,0:T(8,128)(2,1)} %get-tuple-element.631), channel_id=1, source_target_pairs={{0,192},{32,224},{1,193},{33,225},{2,194},{34,226},{3,195},{35,227... | collective-permute-start | bytes 393224 | tf_op jit(solution)/shard_map/while/body/eval_jaxpr/cond/branch_0_fun/ppermute | solution.py:318
  43.9 4.7 %collective-permute-start.4 = (bf16[256,256]{1,0:T(8,128)(2,1)}, bf16[256,256]{1,0:T(8,128)(2,1)S(1)}, u32[]{:S(2)}, u32[]{:S(2)}) collective-permute-start(bf16[256,256]{1,0:T(8,128)(2,1)} %get-tuple-element.632), channel_id=1, source_target_pairs={{0,128},{32,160},{1,129},{33,161},{2,130},{34,162},{3,131},{35,163... | collective-permute-start | bytes 393224 | tf_op jit(solution)/shard_map/while/body/eval_jaxpr/cond/branch_0_fun/ppermute | solution.py:318
  44.6 9.5 %collective-permute-start.5 = (bf16[256,256]{1,0:T(8,128)(2,1)}, bf16[256,256]{1,0:T(8,128)(2,1)S(1)}, u32[]{:S(2)}, u32[]{:S(2)}) collective-permute-start(bf16[256,256]{1,0:T(8,128)(2,1)} %get-tuple-element.633), channel_id=1, source_target_pairs={{0,64},{32,96},{1,65},{33,97},{2,66},{34,98},{3,67},{35,99},{4,68}... | collective-permute-start | bytes 393224 | tf_op jit(solution)/shard_map/while/body/eval_jaxpr/cond/branch_0_fun/ppermute | solution.py:318
  45.9 10.8 %collective-permute-start = (bf16[256,256]{1,0:T(8,128)(2,1)}, bf16[256,256]{1,0:T(8,128)(2,1)S(1)}, u32[]{:S(2)}, u32[]{:S(2)}) collective-permute-start(bf16[256,256]{1,0:T(8,128)(2,1)} %get-tuple-element.627), channel_id=1, source_target_pairs={{0,192},{32,224},{1,193},{33,225},{2,194},{34,226},{3,195},{35,227... | collective-permute-start | bytes 393224 | tf_op jit(solution)/shard_map/while/body/eval_jaxpr/cond/branch_0_fun/ppermute | solution.py:318
  46.6 10.1 %collective-permute-start.1 = (bf16[256,256]{1,0:T(8,128)(2,1)}, bf16[256,256]{1,0:T(8,128)(2,1)S(1)}, u32[]{:S(2)}, u32[]{:S(2)}) collective-permute-start(bf16[256,256]{1,0:T(8,128)(2,1)} %get-tuple-element.628), channel_id=1, source_target_pairs={{0,128},{32,160},{1,129},{33,161},{2,130},{34,162},{3,131},{35,163... | collective-permute-start | bytes 393224 | tf_op jit(solution)/shard_map/while/body/eval_jaxpr/cond/branch_0_fun/ppermute | solution.py:318
  47.3 12.5 %collective-permute-start.2 = (bf16[256,256]{1,0:T(8,128)(2,1)}, bf16[256,256]{1,0:T(8,128)(2,1)S(1)}, u32[]{:S(2)}, u32[]{:S(2)}) collective-permute-start(bf16[256,256]{1,0:T(8,128)(2,1)} %get-tuple-element.629), channel_id=1, source_target_pairs={{0,64},{32,96},{1,65},{33,97},{2,66},{34,98},{3,67},{35,99},{4,68}... | collective-permute-start | bytes 393224 | tf_op jit(solution)/shard_map/while/body/eval_jaxpr/cond/branch_0_fun/ppermute | solution.py:318
  54.2 5.8 %collective-permute-start.6 = (bf16[256,256]{1,0:T(8,128)(2,1)S(1)}, bf16[256,256]{1,0:T(8,128)(2,1)S(1)}, u32[]{:S(2)}, u32[]{:S(2)}) collective-permute-start(bf16[256,256]{1,0:T(8,128)(2,1)S(1)} %select_select_fusion), channel_id=1, source_target_pairs={{0,56},{1,57},{2,58},{3,59},{4,60},{5,61},{6,62},{7,63},{8,48},{9,... | collective-permute-start | bytes 393224 | tf_op jit(solution)/shard_map/while/body/eval_jaxpr/cond/branch_0_fun/ppermute | solution.py:324
  60.8 23.4 %all-to-all-start = ((bf16[32,32,256]{2,1,0:T(8,128)(2,1)}), bf16[32,32,256]{2,1,0:T(8,128)(2,1)S(1)}, u32[]{:S(2)}, u32[]{:S(2)}) async-start(bf16[32,32,256]{2,1,0:T(8,128)(2,1)} %get-tuple-element.1097._), calls=%async_computation | async-start | bytes 1048576 | tf_op jit(solution)/shard_map/while/body/eval_jaxpr/all_to_all | solution.py:421
  74.4 0.8 copy-start.1
  84.2 1.0 copy-start.2
  94.6 0.7 copy-start.7
  96.7 4.6 %collective-permute-start.52 = (bf16[256,256]{1,0:T(8,128)(2,1)}, bf16[256,256]{1,0:T(8,128)(2,1)S(1)}, u32[]{:S(2)}, u32[]{:S(2)}) collective-permute-start(bf16[256,256]{1,0:T(8,128)(2,1)} %get-tuple-element.694), channel_id=1, source_target_pairs={{192,128},{224,160},{193,129},{225,161},{194,130},{226,162},{195,1... | collective-permute-start | bytes 393224 | tf_op jit(solution)/shard_map/while/body/eval_jaxpr/cond/branch_7_fun/ppermute | solution.py:318
  97.4 9.5 %collective-permute-start.53 = (bf16[256,256]{1,0:T(8,128)(2,1)}, bf16[256,256]{1,0:T(8,128)(2,1)S(1)}, u32[]{:S(2)}, u32[]{:S(2)}) collective-permute-start(bf16[256,256]{1,0:T(8,128)(2,1)} %get-tuple-element.695), channel_id=1, source_target_pairs={{192,64},{224,96},{193,65},{225,97},{194,66},{226,98},{195,67},{22... | collective-permute-start | bytes 393224 | tf_op jit(solution)/shard_map/while/body/eval_jaxpr/cond/branch_7_fun/ppermute | solution.py:318
  98.7 8.2 %collective-permute-start.54 = (bf16[256,256]{1,0:T(8,128)(2,1)}, bf16[256,256]{1,0:T(8,128)(2,1)S(1)}, u32[]{:S(2)}, u32[]{:S(2)}) collective-permute-start(bf16[256,256]{1,0:T(8,128)(2,1)} %get-tuple-element.696), channel_id=1, source_target_pairs={{192,0},{224,32},{193,1},{225,33},{194,2},{226,34},{195,3},{227,35... | collective-permute-start | bytes 393224 | tf_op jit(solution)/shard_map/while/body/eval_jaxpr/cond/branch_7_fun/ppermute | solution.py:318
  99.3 9.8 %collective-permute-start.49 = (bf16[256,256]{1,0:T(8,128)(2,1)}, bf16[256,256]{1,0:T(8,128)(2,1)S(1)}, u32[]{:S(2)}, u32[]{:S(2)}) collective-permute-start(bf16[256,256]{1,0:T(8,128)(2,1)} %get-tuple-element.690), channel_id=1, source_target_pairs={{192,128},{224,160},{193,129},{225,161},{194,130},{226,162},{195,1... | collective-permute-start | bytes 393224 | tf_op jit(solution)/shard_map/while/body/eval_jaxpr/cond/branch_7_fun/ppermute | solution.py:318
  100.0 12.4 %collective-permute-start.50 = (bf16[256,256]{1,0:T(8,128)(2,1)}, bf16[256,256]{1,0:T(8,128)(2,1)S(1)}, u32[]{:S(2)}, u32[]{:S(2)}) collective-permute-start(bf16[256,256]{1,0:T(8,128)(2,1)} %get-tuple-element.691), channel_id=1, source_target_pairs={{192,64},{224,96},{193,65},{225,97},{194,66},{226,98},{195,67},{22... | collective-permute-start | bytes 393224 | tf_op jit(solution)/shard_map/while/body/eval_jaxpr/cond/branch_7_fun/ppermute | solution.py:318
  101.3 11.1 %collective-permute-start.51 = (bf16[256,256]{1,0:T(8,128)(2,1)}, bf16[256,256]{1,0:T(8,128)(2,1)S(1)}, u32[]{:S(2)}, u32[]{:S(2)}) collective-permute-start(bf16[256,256]{1,0:T(8,128)(2,1)} %get-tuple-element.692), channel_id=1, source_target_pairs={{192,0},{224,32},{193,1},{225,33},{194,2},{226,34},{195,3},{227,35... | collective-permute-start | bytes 393224 | tf_op jit(solution)/shard_map/while/body/eval_jaxpr/cond/branch_7_fun/ppermute | solution.py:318
  107.8 11.8 %collective-permute-start.55 = (bf16[256,256]{1,0:T(8,128)(2,1)S(1)}, bf16[256,256]{1,0:T(8,128)(2,1)S(1)}, u32[]{:S(2)}, u32[]{:S(2)}) collective-permute-start(bf16[256,256]{1,0:T(8,128)(2,1)S(1)} %select_select_fusion.7), channel_id=1, source_target_pairs={{32,24},{33,25},{34,26},{35,27},{36,28},{37,29},{38,30},{39,31},{4... | collective-permute-start | bytes 393224 | tf_op jit(solution)/shard_map/while/body/eval_jaxpr/cond/branch_7_fun/ppermute | solution.py:324
  121.3 21.4 %all-to-all-start = ((bf16[32,32,256]{2,1,0:T(8,128)(2,1)}), bf16[32,32,256]{2,1,0:T(8,128)(2,1)S(1)}, u32[]{:S(2)}, u32[]{:S(2)}) async-start(bf16[32,32,256]{2,1,0:T(8,128)(2,1)} %get-tuple-element.1097._), calls=%async_computation | async-start | bytes 1048576 | tf_op jit(solution)/shard_map/while/body/eval_jaxpr/all_to_all | solution.py:421
  132.9 0.8 copy-start.1
  142.7 1.0 copy-start.2
  153.1 0.7 copy-start.7
  155.2 7.5 %collective-permute-start.31 = (bf16[256,256]{1,0:T(8,128)(2,1)}, bf16[256,256]{1,0:T(8,128)(2,1)S(1)}, u32[]{:S(2)}, u32[]{:S(2)}) collective-permute-start(bf16[256,256]{1,0:T(8,128)(2,1)} %get-tuple-element.667), channel_id=1, source_target_pairs={{128,64},{160,96},{129,65},{161,97},{130,66},{162,98},{131,67},{16... | collective-permute-start | bytes 393224 | tf_op jit(solution)/shard_map/while/body/eval_jaxpr/cond/branch_4_fun/ppermute | solution.py:318
  156.5 6.8 %collective-permute-start.32 = (bf16[256,256]{1,0:T(8,128)(2,1)}, bf16[256,256]{1,0:T(8,128)(2,1)S(1)}, u32[]{:S(2)}, u32[]{:S(2)}) collective-permute-start(bf16[256,256]{1,0:T(8,128)(2,1)} %get-tuple-element.668), channel_id=1, source_target_pairs={{128,0},{160,32},{129,1},{161,33},{130,2},{162,34},{131,3},{163,35... | collective-permute-start | bytes 393224 | tf_op jit(solution)/shard_map/while/body/eval_jaxpr/cond/branch_4_fun/ppermute | solution.py:318
  157.1 6.2 %collective-permute-start.33 = (bf16[256,256]{1,0:T(8,128)(2,1)}, bf16[256,256]{1,0:T(8,128)(2,1)S(1)}, u32[]{:S(2)}, u32[]{:S(2)}) collective-permute-start(bf16[256,256]{1,0:T(8,128)(2,1)} %get-tuple-element.669), channel_id=1, source_target_pairs={{128,192},{160,224},{129,193},{161,225},{130,194},{162,226},{131,1... | collective-permute-start | bytes 393224 | tf_op jit(solution)/shard_map/while/body/eval_jaxpr/cond/branch_4_fun/ppermute | solution.py:318
  157.8 8.7 %collective-permute-start.28 = (bf16[256,256]{1,0:T(8,128)(2,1)}, bf16[256,256]{1,0:T(8,128)(2,1)S(1)}, u32[]{:S(2)}, u32[]{:S(2)}) collective-permute-start(bf16[256,256]{1,0:T(8,128)(2,1)} %get-tuple-element.663), channel_id=1, source_target_pairs={{128,64},{160,96},{129,65},{161,97},{130,66},{162,98},{131,67},{16... | collective-permute-start | bytes 393224 | tf_op jit(solution)/shard_map/while/body/eval_jaxpr/cond/branch_4_fun/ppermute | solution.py:318
  159.1 7.4 %collective-permute-start.29 = (bf16[256,256]{1,0:T(8,128)(2,1)}, bf16[256,256]{1,0:T(8,128)(2,1)S(1)}, u32[]{:S(2)}, u32[]{:S(2)}) collective-permute-start(bf16[256,256]{1,0:T(8,128)(2,1)} %get-tuple-element.664), channel_id=1, source_target_pairs={{128,0},{160,32},{129,1},{161,33},{130,2},{162,34},{131,3},{163,35... | collective-permute-start | bytes 393224 | tf_op jit(solution)/shard_map/while/body/eval_jaxpr/cond/branch_4_fun/ppermute | solution.py:318
  162.6 3.9 %collective-permute-start.30 = (bf16[256,256]{1,0:T(8,128)(2,1)}, bf16[256,256]{1,0:T(8,128)(2,1)S(1)}, u32[]{:S(2)}, u32[]{:S(2)}) collective-permute-start(bf16[256,256]{1,0:T(8,128)(2,1)} %get-tuple-element.665), channel_id=1, source_target_pairs={{128,192},{160,224},{129,193},{161,225},{130,194},{162,226},{131,1... | collective-permute-start | bytes 393224 | tf_op jit(solution)/shard_map/while/body/eval_jaxpr/cond/branch_4_fun/ppermute | solution.py:318
  164.2 7.1 %collective-permute-start.34 = (bf16[256,256]{1,0:T(8,128)(2,1)S(1)}, bf16[256,256]{1,0:T(8,128)(2,1)S(1)}, u32[]{:S(2)}, u32[]{:S(2)}) collective-permute-start(bf16[256,256]{1,0:T(8,128)(2,1)S(1)} %select_select_fusion.4), channel_id=1, source_target_pairs={{0,56},{1,57},{2,58},{3,59},{4,60},{5,61},{6,62},{7,63},{8,48},{9,... | collective-permute-start | bytes 393224 | tf_op jit(solution)/shard_map/while/body/eval_jaxpr/cond/branch_4_fun/ppermute | solution.py:324
  173.0 20.8 %all-to-all-start = ((bf16[32,32,256]{2,1,0:T(8,128)(2,1)}), bf16[32,32,256]{2,1,0:T(8,128)(2,1)S(1)}, u32[]{:S(2)}, u32[]{:S(2)}) async-start(bf16[32,32,256]{2,1,0:T(8,128)(2,1)} %get-tuple-element.1097._), calls=%async_computation | async-start | bytes 1048576 | tf_op jit(solution)/shard_map/while/body/eval_jaxpr/all_to_all | solution.py:421
  183.9 0.8 copy-start.1
  193.8 1.0 copy-start.2
  204.3 0.7 copy-start.7
  206.3 9.6 %collective-permute-start.17 = (bf16[256,256]{1,0:T(8,128)(2,1)}, bf16[256,256]{1,0:T(8,128)(2,1)S(1)}, u32[]{:S(2)}, u32[]{:S(2)}) collective-permute-start(bf16[256,256]{1,0:T(8,128)(2,1)} %get-tuple-element.649), channel_id=1, source_target_pairs={{64,0},{96,32},{65,1},{97,33},{66,2},{98,34},{67,3},{99,35},{68,4}... | collective-permute-start | bytes 393224 | tf_op jit(solution)/shard_map/while/body/eval_jaxpr/cond/branch_2_fun/ppermute | solution.py:318
  210.6 6.5 %collective-permute-start.18 = (bf16[256,256]{1,0:T(8,128)(2,1)}, bf16[256,256]{1,0:T(8,128)(2,1)S(1)}, u32[]{:S(2)}, u32[]{:S(2)}) collective-permute-start(bf16[256,256]{1,0:T(8,128)(2,1)} %get-tuple-element.650), channel_id=1, source_target_pairs={{64,192},{96,224},{65,193},{97,225},{66,194},{98,226},{67,195},{99... | collective-permute-start | bytes 393224 | tf_op jit(solution)/shard_map/while/body/eval_jaxpr/cond/branch_2_fun/ppermute | solution.py:318
  211.9 5.3 %collective-permute-start.19 = (bf16[256,256]{1,0:T(8,128)(2,1)}, bf16[256,256]{1,0:T(8,128)(2,1)S(1)}, u32[]{:S(2)}, u32[]{:S(2)}) collective-permute-start(bf16[256,256]{1,0:T(8,128)(2,1)} %get-tuple-element.651), channel_id=1, source_target_pairs={{64,128},{96,160},{65,129},{97,161},{66,130},{98,162},{67,131},{99... | collective-permute-start | bytes 393224 | tf_op jit(solution)/shard_map/while/body/eval_jaxpr/cond/branch_2_fun/ppermute | solution.py:318
  213.2 10.0 %collective-permute-start.14 = (bf16[256,256]{1,0:T(8,128)(2,1)}, bf16[256,256]{1,0:T(8,128)(2,1)S(1)}, u32[]{:S(2)}, u32[]{:S(2)}) collective-permute-start(bf16[256,256]{1,0:T(8,128)(2,1)} %get-tuple-element.645), channel_id=1, source_target_pairs={{64,0},{96,32},{65,1},{97,33},{66,2},{98,34},{67,3},{99,35},{68,4}... | collective-permute-start | bytes 393224 | tf_op jit(solution)/shard_map/while/body/eval_jaxpr/cond/branch_2_fun/ppermute | solution.py:318
  214.5 8.7 %collective-permute-start.15 = (bf16[256,256]{1,0:T(8,128)(2,1)}, bf16[256,256]{1,0:T(8,128)(2,1)S(1)}, u32[]{:S(2)}, u32[]{:S(2)}) collective-permute-start(bf16[256,256]{1,0:T(8,128)(2,1)} %get-tuple-element.646), channel_id=1, source_target_pairs={{64,192},{96,224},{65,193},{97,225},{66,194},{98,226},{67,195},{99... | collective-permute-start | bytes 393224 | tf_op jit(solution)/shard_map/while/body/eval_jaxpr/cond/branch_2_fun/ppermute | solution.py:318
  215.9 7.3 %collective-permute-start.16 = (bf16[256,256]{1,0:T(8,128)(2,1)}, bf16[256,256]{1,0:T(8,128)(2,1)S(1)}, u32[]{:S(2)}, u32[]{:S(2)}) collective-permute-start(bf16[256,256]{1,0:T(8,128)(2,1)} %get-tuple-element.647), channel_id=1, source_target_pairs={{64,128},{96,160},{65,129},{97,161},{66,130},{98,162},{67,131},{99... | collective-permute-start | bytes 393224 | tf_op jit(solution)/shard_map/while/body/eval_jaxpr/cond/branch_2_fun/ppermute | solution.py:318
  218.1 10.7 %collective-permute-start.20 = (bf16[256,256]{1,0:T(8,128)(2,1)S(1)}, bf16[256,256]{1,0:T(8,128)(2,1)S(1)}, u32[]{:S(2)}, u32[]{:S(2)}) collective-permute-start(bf16[256,256]{1,0:T(8,128)(2,1)S(1)} %select_select_fusion.2), channel_id=1, source_target_pairs={{0,56},{1,57},{2,58},{3,59},{4,60},{5,61},{6,62},{7,63},{8,48},{9,... | collective-permute-start | bytes 393224 | tf_op jit(solution)/shard_map/while/body/eval_jaxpr/cond/branch_2_fun/ppermute | solution.py:324
  230.5 21.9 %all-to-all-start = ((bf16[32,32,256]{2,1,0:T(8,128)(2,1)}), bf16[32,32,256]{2,1,0:T(8,128)(2,1)S(1)}, u32[]{:S(2)}, u32[]{:S(2)}) async-start(bf16[32,32,256]{2,1,0:T(8,128)(2,1)} %get-tuple-element.1097._), calls=%async_computation | async-start | bytes 1048576 | tf_op jit(solution)/shard_map/while/body/eval_jaxpr/all_to_all | solution.py:421
  242.6 0.8 copy-start.1
  252.4 1.0 copy-start.2
  (17 other events, 11.9 us)

commit v2 on v1

--- a/solution.py
+++ b/solution.py
@@ -12,14 +12,14 @@
 BF16 = jnp.bfloat16
 I32 = jnp.int32
 MIB = 1024 * 1024
-VMEM_MIB = dict(plan=6, codes=6, prep=8, local=8, serve=8, update=16)
+VMEM_MIB = dict(plan=6, stage=6, codes=6, prep=12, serve=8, update=16)
 
 
 def whole():
     return pl.BlockSpec(memory_space=pltpu.VMEM)
 
 
-def call(kernel, out_shape, args, flops=0, name=None, specs=None, scalars=(), aliases=None):
+def call(kernel, out_shape, args, flops=0, name=None, specs=None, scalars=()):
     moved = sum(a.size * a.dtype.itemsize for a in args)
     moved += sum(o.size * o.dtype.itemsize for o in jax.tree.leaves(out_shape))
     specs = specs or {}
@@ -32,7 +32,6 @@
             in_specs=[specs.get(i, whole()) for i in range(len(args))],
             out_specs=jax.tree.map(lambda _: whole(), out_shape),
         ),
-        input_output_aliases=aliases or {},
         compiler_params=pltpu.CompilerParams(vmem_limit_bytes=VMEM_MIB[name] * MIB),
         cost_estimate=pl.CostEstimate(flops=flops, bytes_accessed=moved, transcendentals=0),
         name=name,
@@ -66,10 +65,17 @@
     )
 
 
+def stage_kernel(_, *refs):
+    count = len(refs) // 2
+    for given, kept in zip(refs[:count], refs[count:]):
+        kept[...] = given[...]
+
+
 def plan_kernel(cap, ocap, node_dev, flip_ref, source_ref, ids_ref, pcode_ref):
     batches, events = source_ref.shape
     rows = ids_ref.shape[1]
     per = cap + ocap
+    own_total = rows * cap
     group_nodes = rows * node_dev
     upper = (
         lax.broadcasted_iota(I32, (events, events), 0)
@@ -96,7 +102,9 @@
         spot = (slot + b * per == lane_iota).astype(F32)
         high = high + dot_nt(both, (spot * (offset >> 6).astype(F32)).astype(BF16))
         low = low + dot_nt(both, (spot * (offset & 63).astype(F32)).astype(BF16))
-        places.append(jnp.where(far, dest ^ flip_ref[b], dest) * per + slot)
+        places.append(
+            jnp.where(far, own_total + (dest ^ flip_ref[b]) * ocap + rank, dest * cap + rank)
+        )
     ids = high.astype(I32) * 64 + low.astype(I32)
     for g in range(ids_ref.shape[0]):
         ids_ref[g] = ids
@@ -130,7 +138,7 @@
 def code_kernel(cap, per, at_ref, asked_ref, _, own_ref, far_ref):
     b = at_ref[0]
     groups, rows, _ = asked_ref.shape
-    own_ref[...] = spread_codes(asked_ref[at_ref[1]], b * per, per)
+    own_ref[...] = spread_codes(asked_ref[at_ref[1]], b * per, cap)
     block = rows * (per - cap)
     for g in range(groups):
         far_ref[g * block : (g + 1) * block, :] = spread_codes(
@@ -160,6 +168,7 @@
 def prep_kernel(
     width,
     at_ref,
+    table_ref,
     target_ref,
     time_ref,
     node_time_ref,
@@ -168,8 +177,7 @@
     phase_ref,
     w_ref,
     _,
-    base_ref,
-    gcode_ref,
+    local_ref,
     scode_ref,
     same_ref,
 ):
@@ -205,8 +213,13 @@
         )
     angle = (ecol - seen) * freq_ref[...] + phase_ref[...]
     encoded = cosine(angle).astype(BF16)
-    base_ref[...] = dot(encoded, w_ref[enc_at:edge_at, :]) + dot(edge_ref[0], w_ref[edge_at:, :])
-    gcode_ref[...] = lane_code(tcol, events)
+    mem = dot(expand(lane_code(tcol, events), 0, node_dev // LANES), table_ref[...])
+    local_ref[:, :width] = (
+        dot(encoded, w_ref[enc_at:edge_at, :])
+        + dot(edge_ref[0], w_ref[edge_at:, :])
+        + dot(mem.astype(BF16), w_ref[:width, :])
+    )
+    local_ref[:, width:] = mem
     same = (tcol == trow) & (trow >= 0)
     samef = same.astype(F32)
     same_ref[...] = samef.astype(BF16)
@@ -233,19 +246,12 @@
     serve_rows(table_ref, far_code_ref, far_refs, 512)
 
 
-def local_kernel(table_ref, gcode_ref, base_ref, w_ref, out_ref):
-    blocks = table_ref.shape[0] // LANES
-    width = table_ref.shape[1]
-    mem = dot(expand(gcode_ref[...], 0, blocks), table_ref[...])
-    out_ref[:, :width] = base_ref[...] + dot(mem.astype(BF16), w_ref[:width, :])
-    out_ref[:, width:] = mem
-
-
 def update_kernel(
     last,
     at_ref,
     table_ref,
-    back_ref,
+    own_back_ref,
+    far_back_ref,
     pcode_ref,
     local_ref,
     same_ref,
@@ -264,7 +270,12 @@
     width = table_ref.shape[1]
     mem = local_ref[:, width:]
     hidden = dot(mem.astype(BF16), w_hidden_ref[...]) + bias_hidden_ref[...]
-    source = dot(expand(pcode_ref[0], 0, back_ref.shape[0] // LANES), back_ref[...])
+    own_blocks = own_back_ref.shape[0] // LANES
+    far_blocks = far_back_ref.shape[0] // LANES
+    pcode = pcode_ref[0]
+    source = dot(expand(pcode, 0, own_blocks), own_back_ref[...]) + dot(
+        expand(pcode, own_blocks, far_blocks), far_back_ref[...]
+    )
     w_source = w_ref[width : 2 * width, :]
     message = (local_ref[:, :width] + dot(source.astype(BF16), w_source)).astype(BF16)
     same = same_ref[...]
@@ -298,8 +309,8 @@
         serve_kernel(new_ref, own_code_ref, far_code_ref, own_out_ref, *far_out_refs)
 
 
-def from_owner(own_rows, far_rows, owner, cap, turn):
-    rows, _, width = own_rows.shape
+def fetch(own_rows, far_rows, owner, turn):
+    rows = own_rows.shape[0]
     ys = len(far_rows) // 2
 
     def branch(root):
@@ -330,8 +341,10 @@
                     for r in range(rows)
                 ],
             )
-            mine = jnp.where(my_z == z, spread(z), across)
-            return own_rows.at[:, cap:, :].set(mine.reshape(rows, -1, width))
+            along = spread(z)
+            own_back = lax.all_to_all(own_rows, "row", 0, 0, tiled=True)
+            seat = my_z + (own_back[0, 0, 0].astype(F32) * 0.0).astype(I32)
+            return own_back, jnp.where(seat == z, along, across)
 
         return body
 
@@ -362,33 +375,44 @@
     ocap = events // (2 * rows)
     per = cap + ocap
     shape = jax.ShapeDtypeStruct
-    code = shape((events, LANES), BF16)
-
     me = lax.axis_index("dom").astype(I32)
     turn = rows - rows // 4
     flip = jnp.where((owner_group & 1) == (me & 1), 0, turn).astype(I32)
+    row_vectors = (
+        node_time.reshape(1, node_dev),
+        frequency.reshape(1, -1),
+        phase_shift.reshape(1, -1),
+        bias_input.reshape(1, -1),
+        bias_hidden.reshape(1, -1),
+    )
+    anywhere = pl.BlockSpec(memory_space=pl.ANY)
     ids, pcode = call(
         functools.partial(plan_kernel, cap, ocap, node_dev),
-        (shape((groups, rows, batches * per), I32), shape((batches, events, LANES), BF16)),
+        (
+            shape((groups, rows, batches * per), I32),
+            shape((batches, events, LANES), BF16),
+        ),
         (source,),
         name="plan",
         scalars=(flip,),
     )
+    given = (memory,) + row_vectors
+    table, times_row, freq_row, phase_row, input_row, hidden_row = call(
+        stage_kernel,
+        tuple(shape(v.shape, v.dtype) for v in given),
+        (ids,) + given,
+        flops=2 * 10**9,
+        name="stage",
+        specs={0: anywhere},
+    )
     asked = lax.all_to_all(
         ids.reshape(groups * rows, 1, batches * per), ("dom", "row"), 0, 0, tiled=True
     ).reshape(groups, rows, batches * per)
-    times_row = node_time.reshape(1, node_dev)
-    freq_row = frequency.reshape(1, -1)
-    phase_row = phase_shift.reshape(1, -1)
-    input_row = bias_input.reshape(1, -1)
-    hidden_row = bias_hidden.reshape(1, -1)
-    anywhere = pl.BlockSpec(memory_space=pl.ANY)
-
     def codes(b, after):
         return call(
             functools.partial(code_kernel, cap, per),
             (
-                shape((rows * per, LANES), BF16),
+                shape((rows * cap, LANES), BF16),
                 shape((groups * rows * ocap, LANES), BF16),
             ),
             (asked, after),
@@ -398,12 +422,12 @@
             scalars=(jnp.stack([b, me]),),
         )
 
-    own_shape = shape((rows * per, width), BF16)
+    own_shape = shape((rows * cap, width), BF16)
     far_shape = (shape((rows * ocap, width), BF16),) * groups
     own_rows, *far_rows = call(
         serve_kernel,
         (own_shape,) + far_shape,
-        (memory,) + tuple(codes(jnp.zeros((), I32), asked)),
+        (table,) + tuple(codes(jnp.zeros((), I32), asked)),
         flops=4 * 10**9,
         name="serve",
     )
@@ -411,45 +435,37 @@
     def batch(b, carry):
         table, own_rows, *far_rows = carry
         at = b.reshape(1)
-        sent = from_owner(
-            own_rows.reshape(rows, per, width),
+        own_back, mine = fetch(
+            own_rows.reshape(rows, cap, width),
             far_rows,
             lax.dynamic_index_in_dim(owner_group, b, 0, keepdims=False),
-            cap,
             turn,
         )
-        back = lax.all_to_all(sent, "row", 0, 0, tiled=True).reshape(rows * per, width)
-        base, gcode, scode, same = call(
+        far_back = lax.all_to_all(mine.reshape(rows, ocap, width), "row", 0, 0, tiled=True)
+        local, scode, same = call(
             functools.partial(prep_kernel, width),
             (
-                shape((events, width), F32),
-                code,
+                shape((events, 2 * width), F32),
                 shape((LANES, events), BF16),
                 shape((events, events), BF16),
             ),
-            (target, event_time, times_row, edge_feat, freq_row, phase_row, w_message, sent),
-            flops=3 * 10**9,
+            (table, target, event_time, times_row, edge_feat, freq_row, phase_row, w_message, mine),
+            flops=5 * 10**9,
             name="prep",
             specs={
-                3: pl.BlockSpec((1,) + edge_feat.shape[1:], lambda i, at: (at[0], 0, 0)),
-                7: anywhere,
+                4: pl.BlockSpec((1,) + edge_feat.shape[1:], lambda i, at: (at[0], 0, 0)),
+                8: anywhere,
             },
             scalars=(at,),
         )
-        local = call(
-            local_kernel,
-            shape((events, 2 * width), F32),
-            (table, gcode, base, w_message),
-            flops=3 * 10**9,
-            name="local",
-        )
-        own_code, far_code = codes(b + 1, sent)
+        own_code, far_code = codes(b + 1, mine)
         return call(
             functools.partial(update_kernel, batches - 1),
             (shape((node_dev, width), BF16), own_shape) + far_shape,
             (
                 table,
-                back,
+                own_back.reshape(rows * cap, width),
+                far_back.reshape(rows * ocap, width),
                 pcode,
                 local,
                 same,
@@ -464,11 +480,11 @@
             ),
             flops=6 * 10**9,
             name="update",
-            specs={2: pl.BlockSpec((1, events, LANES), lambda i, at: (at[0], 0, 0))},
+            specs={3: pl.BlockSpec((1, events, LANES), lambda i, at: (at[0], 0, 0))},
             scalars=(at,),
         )
 
-    return lax.fori_loop(0, batches, batch, (memory, own_rows, *far_rows))[0]
+    return lax.fori_loop(0, batches, batch, (table, own_rows, *far_rows))[0]
 
 
 def solution(mesh):

time: 264 us -> 267 us (1.011)
  starting transfers between devices: 74.3 us -> 116 us
  waiting for transfers between devices: 77.2 us -> 41.7 us
  Pallas kernels: 74.2 us -> 68.8 us
  loops' own time: 3.3 us -> 6 us
    all_to_all x4 -> x8, starting transfers between devices: 21.7 us -> 70.6 us  [the longest x4 44.8 us: batch(): lax.all_to_all(mine.reshape(rows, ocap, width), 'row', 0, 0, tiled=True)]
    all_to_all x4 -> x8, waiting for transfers between devices: 28.5 us -> 10.4 us  [the longest x4 7.38 us: body(): own_back = lax.all_to_all(own_rows, 'row', 0, 0, tiled=True)]
    ppermute x4, waiting for transfers between devices: 17.8 us -> 6.21 us  [body(): lax.ppermute(spread(1 - z), ('dom', 'row'), [((2 * i + z) * rows + r, (2...]
    scatter x4 -> x0, other arithmetic: 5.84 us -> none  [body(): return own_rows.at[:, cap:, :].set(mine.reshape(rows, -1, width))]
    select_n x0 -> x4, other arithmetic: none -> 5.46 us  [body(): return (own_back, jnp.where(seat == z, along, across))]
    pallas_call x19 -> x16, Pallas kernels: 74.2 us -> 68.8 us  [call(): pl.pallas_call(kernel, out_shape=out_shape, grid_spec=pltpu.PrefetchScala...]
    ppermute x4, starting transfers between devices: 10.1 us -> 5.17 us  [body(): lax.ppermute(spread(1 - z), ('dom', 'row'), [((2 * i + z) * rows + r, (2...]
    slice x0 -> x4, local copies, waits for them, and re-layouts: none -> 4.84 us  [body(): seat = my_z + (own_back[0, 0, 0].astype(F32) * 0.0).astype(I32)]
  transfers between devices with their start and end apart: 33 -> 37, of which waited for: 15 -> 16; matrix products, arithmetic and copies ran while one was open for 3% -> 5% of each run, Pallas kernels for 11% -> 9%
where the time goes in v2:
time: 267 us; the launch traced here: 264 us
  starting transfers between devices  116 us (43%)
  Pallas kernels  68.8 us (26%)
  waiting for transfers between devices  41.7 us (16%)
  local copies, waits for them, and re-layouts  22.5 us (8%)
  other arithmetic  8.67 us (3%)
  loops' own time  6 us (2%)
    pallas_call x16, Pallas kernels, call(): pl.pallas_call(kernel, out_shape=out_shape, grid_spec=pltpu.PrefetchScala...  68.8 us
    all_to_all x4, starting transfers between devices, batch(): lax.all_to_all(mine.reshape(rows, ocap, width), 'row', 0, 0, tiled=True)  44.8 us
    all_to_all x4, starting transfers between devices, body(): own_back = lax.all_to_all(own_rows, 'row', 0, 0, tiled=True)  25.8 us
    ppermute x24, starting transfers between devices, spread(): block = lax.ppermute(far_rows[2 * there + which], 'dom', pairs)  24.4 us
    ppermute x24, waiting for transfers between devices, spread(): block = lax.ppermute(far_rows[2 * there + which], 'dom', pairs)  16.9 us
    all_to_all x1, starting transfers between devices, shards(): lax.all_to_all(ids.reshape(groups * rows, 1, batches * per), ('dom', 'row...  15.9 us
    while x20, local copies, waits for them, and re-layouts  11.1 us
    all_to_all x1, waiting for transfers between devices, shards(): lax.all_to_all(ids.reshape(groups * rows, 1, batches * per), ('dom', 'row...  8.14 us
  transfers between devices with their start and end apart: 37, of which 16 were waited for; matrix products, arithmetic and copies ran while one was open for 5% of the time, Pallas kernels for 9%

profile of v2, /device:TPU:9, one launch (start us, length us, event | category | flops | bytes accessed | tf_op | source)
XLA Modules:
  0.0 263.9 jit_solution(1507189969219179416)
XLA Ops:
  1.4 3.1 %plan.1 = (s32[8,32,128]{2,1,0:T(8,128)}, bf16[4,512,128]{2,1,0:T(8,128)(2,1)}) custom-call(s32[4]{0:T(128)S(1)} %compare_select_fusion.flip_ref, s32[4,512]{1,0:T(4,128)S(1)} %copy-done), custom_call_target="tpu_custom_call" | custom-call | bytes 663552 | tf_op jit(solution)/shard_map/plan/pallas_call | solution.py:26
  4.5 15.9 %all-to-all-start.9 = ((s32[256,1,128]{2,1,0:T(1,128)}), s32[256,1,128]{2,1,0:T(1,128)}, u32[]{:S(2)}, u32[]{:S(2)}) async-start(s32[256,1,128]{2,1,0:T(1,128)} %bitcast.28), calls=%async_computation.9 | async-start | bytes 262144 | tf_op jit(solution)/shard_map/all_to_all | solution.py:408
  23.4 8.1 %all-to-all-done.9 = s32[256,1,128]{2,1,0:T(1,128)} async-done(((s32[256,1,128]{2,1,0:T(1,128)}), s32[256,1,128]{2,1,0:T(1,128)}, u32[]{:S(2)}, u32[]{:S(2)}) %all-to-all-start.9) | async-done | bytes 131104 | tf_op jit(solution)/shard_map/all_to_all | solution.py:408
  31.6 2.5 codes.6
  34.1 5.2 %serve.1 = (bf16[768,256]{1,0:T(8,128)(2,1)}, bf16[256,256]{1,0:T(8,128)(2,1)}, bf16[256,256]{1,0:T(8,128)(2,1)}, bf16[256,256]{1,0:T(8,128)(2,1)}, bf16[256,256...) custom-call(bf16[2048,256]{1,0:T(8,128)(2,1)} %get-tuple-element.938, ...), custom_call_target="tpu_custom_call" | custom-call | flops 4000000000 | bytes 3211264 | tf_op jit(solution)/shard_map/serve/pallas_call | solution.py:26
  40.0 223.8 %while.31 = (s32[]{:T(128)}, bf16[2048,256]{1,0:T(8,128)(2,1)}, bf16[768,256]{1,0:T(8,128)(2,1)}, bf16[256,256]{1,0:T(8,128)(2,1)}, bf16[256,256]{1,0:T(8,128)(2...) while((s32[]{:T(128)}, bf16[2048,256]{1,0:T(8,128)(2,1)}, ...), condition=%wide.region_9.10_spmd, body=%wide.region_0.9_spmd.sunk | while | flops 13000458240 | bytes 22839700 | solution.py:487
  41.4 23.8 %conditional.2 = (bf16[256,256]{1,0:T(8,128)(2,1)}, bf16[768,256]{1,0:T(8,128)(2,1)}) conditional(s32[]{:T(128)} %bitcast.39, (bf16[32,24,256]{2,1,0:T(8,128)(2,1)}, bf16[256,256]{1,0:T(8,128)(2,1)}, bf16[256,256]{1,0:T(8,128)(2,1)}, bf16[256,256]{1,0:T(8,128)(2,1)}, bf16[256,256]{1,0:T(8,128)(2,1)}, ...), branch_computations={%region_1.1_spmd, %region_2.2_spmd, %region_3.3_spmd, %region_4.4_... | conditional | flops 458764 | bytes 6291917 | solution.py:351
  41.4 4.7 %all-to-all-start.7 = ((bf16[32,24,256]{2,1,0:T(8,128)(2,1)}), bf16[32,24,256]{2,1,0:T(8,128)(2,1)}, u32[]{:S(2)}, u32[]{:S(2)}) async-start(bf16[32,24,256]{2,1,0:T(8,128)(2,1)} %get-tuple-element.585), calls=%async_computation.7 | async-start | bytes 786432 | tf_op jit(solution)/shard_map/while/body/eval_jaxpr/cond/branch_7_fun/all_to_all | solution.py:345
  51.4 4.2 %collective-permute-done.53 = bf16[256,256]{1,0:T(8,128)(2,1)S(1)} collective-permute-done((bf16[256,256]{1,0:T(8,128)(2,1)}, bf16[256,256]{1,0:T(8,128)(2,1)S(1)}, u32[]{:S(2)}, u32[]{:S(2)}) %collective-permute-start.53) | collective-permute-done | bytes 131104 | tf_op jit(solution)/shard_map/while/body/eval_jaxpr/cond/branch_7_fun/ppermute | solution.py:329
  57.9 2.1 all-to-all-done.7
  61.9 1.6 collective-permute-done.55
  63.5 1.6 select_select_fusion.15
  65.1 12.4 %all-to-all-start.8 = ((bf16[32,8,256]{2,1,0:T(8,128)(2,1)}), bf16[32,8,256]{2,1,0:T(8,128)(2,1)S(1)}, u32[]{:S(2)}, u32[]{:S(2)}) async-start(bf16[32,8,256]{2,1,0:T(8,128)(2,1)} %bitcast.41), calls=%async_computation.8 | async-start | bytes 262144 | tf_op jit(solution)/shard_map/while/body/eval_jaxpr/all_to_all | solution.py:444
  78.8 3.3 %prep.5 = (f32[512,512]{1,0:T(8,128)S(1)}, bf16[128,512]{1,0:T(8,128)(2,1)S(1)}, bf16[512,512]{1,0:T(8,128)(2,1)S(1)}) custom-call(s32[1]{0:T(128)} %bitcast.38.at_ref, bf16[2048,256]{1,0:T(8,128)(2,1)S(1)} %copy.68.table_ref, s32[4,512]{1,0:T(4,128)S(1)} %get-tuple-element.1007.target_ref, s32[4,512]{1,0:T(4,128)S(1)} %get-tuple-element.1008.time_ref, ...), custom_call_target="tpu_custom_call" | custom-call | flops 5000000000 | bytes 3826688 | tf_op jit(solution)/shard_map/while/body/eval_jaxpr/prep/pallas_call | solution.py:26
  82.9 2.5 codes.7
  87.0 9.2 %update.5 = (bf16[2048,256]{1,0:T(8,128)(2,1)}, bf16[768,256]{1,0:T(8,128)(2,1)}, bf16[256,256]{1,0:T(8,128)(2,1)}, bf16[256,256]{1,0:T(8,128)(2,1)}, bf16[256,2...) custom-call(s32[1]{0:T(128)} %bitcast.38.at_ref, ...), custom_call_target="tpu_custom_call" | custom-call | flops 6000000000 | bytes 8198144 | tf_op jit(solution)/shard_map/while/body/eval_jaxpr/update/pallas_call | solution.py:26
  97.6 25.0 %conditional.2 = (bf16[256,256]{1,0:T(8,128)(2,1)}, bf16[768,256]{1,0:T(8,128)(2,1)}) conditional(s32[]{:T(128)} %bitcast.39, (bf16[32,24,256]{2,1,0:T(8,128)(2,1)}, bf16[256,256]{1,0:T(8,128)(2,1)}, bf16[256,256]{1,0:T(8,128)(2,1)}, bf16[256,256]{1,0:T(8,128)(2,1)}, bf16[256,256]{1,0:T(8,128)(2,1)}, ...), branch_computations={%region_1.1_spmd, %region_2.2_spmd, %region_3.3_spmd, %region_4.4_... | conditional | flops 458764 | bytes 6291917 | solution.py:351
  97.6 7.0 %all-to-all-start = ((bf16[32,24,256]{2,1,0:T(8,128)(2,1)}), bf16[32,24,256]{2,1,0:T(8,128)(2,1)}, u32[]{:S(2)}, u32[]{:S(2)}) async-start(bf16[32,24,256]{2,1,0:T(8,128)(2,1)} %get-tuple-element.522), calls=%async_computation | async-start | bytes 786432 | tf_op jit(solution)/shard_map/while/body/eval_jaxpr/cond/branch_0_fun/all_to_all | solution.py:345
  110.0 6.4 %collective-permute-done.5 = bf16[256,256]{1,0:T(8,128)(2,1)S(1)} collective-permute-done((bf16[256,256]{1,0:T(8,128)(2,1)}, bf16[256,256]{1,0:T(8,128)(2,1)S(1)}, u32[]{:S(2)}, u32[]{:S(2)}) %collective-permute-start.5) | collective-permute-done | bytes 131104 | tf_op jit(solution)/shard_map/while/body/eval_jaxpr/cond/branch_0_fun/ppermute | solution.py:329
  116.4 1.3 collective-permute-start.6
  120.3 1.6 collective-permute-done.2
  122.6 9.5 %all-to-all-start.8 = ((bf16[32,8,256]{2,1,0:T(8,128)(2,1)}), bf16[32,8,256]{2,1,0:T(8,128)(2,1)S(1)}, u32[]{:S(2)}, u32[]{:S(2)}) async-start(bf16[32,8,256]{2,1,0:T(8,128)(2,1)} %bitcast.41), calls=%async_computation.8 | async-start | bytes 262144 | tf_op jit(solution)/shard_map/while/body/eval_jaxpr/all_to_all | solution.py:444
  133.3 3.3 %prep.5 = (f32[512,512]{1,0:T(8,128)S(1)}, bf16[128,512]{1,0:T(8,128)(2,1)S(1)}, bf16[512,512]{1,0:T(8,128)(2,1)S(1)}) custom-call(s32[1]{0:T(128)} %bitcast.38.at_ref, bf16[2048,256]{1,0:T(8,128)(2,1)S(1)} %copy.68.table_ref, s32[4,512]{1,0:T(4,128)S(1)} %get-tuple-element.1007.target_ref, s32[4,512]{1,0:T(4,128)S(1)} %get-tuple-element.1008.time_ref, ...), custom_call_target="tpu_custom_call" | custom-call | flops 5000000000 | bytes 3826688 | tf_op jit(solution)/shard_map/while/body/eval_jaxpr/prep/pallas_call | solution.py:26
  137.3 2.5 codes.7
  141.5 9.2 %update.5 = (bf16[2048,256]{1,0:T(8,128)(2,1)}, bf16[768,256]{1,0:T(8,128)(2,1)}, bf16[256,256]{1,0:T(8,128)(2,1)}, bf16[256,256]{1,0:T(8,128)(2,1)}, bf16[256,2...) custom-call(s32[1]{0:T(128)} %bitcast.38.at_ref, ...), custom_call_target="tpu_custom_call" | custom-call | flops 6000000000 | bytes 8198144 | tf_op jit(solution)/shard_map/while/body/eval_jaxpr/update/pallas_call | solution.py:26
  152.0 27.5 %conditional.2 = (bf16[256,256]{1,0:T(8,128)(2,1)}, bf16[768,256]{1,0:T(8,128)(2,1)}) conditional(s32[]{:T(128)} %bitcast.39, (bf16[32,24,256]{2,1,0:T(8,128)(2,1)}, bf16[256,256]{1,0:T(8,128)(2,1)}, bf16[256,256]{1,0:T(8,128)(2,1)}, bf16[256,256]{1,0:T(8,128)(2,1)}, bf16[256,256]{1,0:T(8,128)(2,1)}, ...), branch_computations={%region_1.1_spmd, %region_2.2_spmd, %region_3.3_spmd, %region_4.4_... | conditional | flops 458764 | bytes 6291917 | solution.py:351
  152.1 7.0 %all-to-all-start.7 = ((bf16[32,24,256]{2,1,0:T(8,128)(2,1)}), bf16[32,24,256]{2,1,0:T(8,128)(2,1)}, u32[]{:S(2)}, u32[]{:S(2)}) async-start(bf16[32,24,256]{2,1,0:T(8,128)(2,1)} %get-tuple-element.585), calls=%async_computation.7 | async-start | bytes 786432 | tf_op jit(solution)/shard_map/while/body/eval_jaxpr/cond/branch_7_fun/all_to_all | solution.py:345
  164.5 4.6 %collective-permute-done.53 = bf16[256,256]{1,0:T(8,128)(2,1)S(1)} collective-permute-done((bf16[256,256]{1,0:T(8,128)(2,1)}, bf16[256,256]{1,0:T(8,128)(2,1)S(1)}, u32[]{:S(2)}, u32[]{:S(2)}) %collective-permute-start.53) | collective-permute-done | bytes 131104 | tf_op jit(solution)/shard_map/while/body/eval_jaxpr/cond/branch_7_fun/ppermute | solution.py:329
  171.4 1.6 all-to-all-done.7
  174.8 3.1 %collective-permute-done.55 = bf16[256,256]{1,0:T(8,128)(2,1)S(1)} collective-permute-done((bf16[256,256]{1,0:T(8,128)(2,1)S(1)}, bf16[256,256]{1,0:T(8,128)(2,1)S(1)}, u32[]{:S(2)}, u32[]{:S(2)}) %collective-permute-start.55) | collective-permute-done | bytes 131104 | tf_op jit(solution)/shard_map/while/body/eval_jaxpr/cond/branch_7_fun/ppermute | solution.py:335
  177.9 1.6 select_select_fusion.15
  179.5 11.3 %all-to-all-start.8 = ((bf16[32,8,256]{2,1,0:T(8,128)(2,1)}), bf16[32,8,256]{2,1,0:T(8,128)(2,1)S(1)}, u32[]{:S(2)}, u32[]{:S(2)}) async-start(bf16[32,8,256]{2,1,0:T(8,128)(2,1)} %bitcast.41), calls=%async_computation.8 | async-start | bytes 262144 | tf_op jit(solution)/shard_map/while/body/eval_jaxpr/all_to_all | solution.py:444
  192.1 3.3 %prep.5 = (f32[512,512]{1,0:T(8,128)S(1)}, bf16[128,512]{1,0:T(8,128)(2,1)S(1)}, bf16[512,512]{1,0:T(8,128)(2,1)S(1)}) custom-call(s32[1]{0:T(128)} %bitcast.38.at_ref, bf16[2048,256]{1,0:T(8,128)(2,1)S(1)} %copy.68.table_ref, s32[4,512]{1,0:T(4,128)S(1)} %get-tuple-element.1007.target_ref, s32[4,512]{1,0:T(4,128)S(1)} %get-tuple-element.1008.time_ref, ...), custom_call_target="tpu_custom_call" | custom-call | flops 5000000000 | bytes 3826688 | tf_op jit(solution)/shard_map/while/body/eval_jaxpr/prep/pallas_call | solution.py:26
  196.1 2.5 codes.7
  200.3 9.2 %update.5 = (bf16[2048,256]{1,0:T(8,128)(2,1)}, bf16[768,256]{1,0:T(8,128)(2,1)}, bf16[256,256]{1,0:T(8,128)(2,1)}, bf16[256,256]{1,0:T(8,128)(2,1)}, bf16[256,2...) custom-call(s32[1]{0:T(128)} %bitcast.38.at_ref, ...), custom_call_target="tpu_custom_call" | custom-call | flops 6000000000 | bytes 8198144 | tf_op jit(solution)/shard_map/while/body/eval_jaxpr/update/pallas_call | solution.py:26
  210.8 25.9 %conditional.2 = (bf16[256,256]{1,0:T(8,128)(2,1)}, bf16[768,256]{1,0:T(8,128)(2,1)}) conditional(s32[]{:T(128)} %bitcast.39, (bf16[32,24,256]{2,1,0:T(8,128)(2,1)}, bf16[256,256]{1,0:T(8,128)(2,1)}, bf16[256,256]{1,0:T(8,128)(2,1)}, bf16[256,256]{1,0:T(8,128)(2,1)}, bf16[256,256]{1,0:T(8,128)(2,1)}, ...), branch_computations={%region_1.1_spmd, %region_2.2_spmd, %region_3.3_spmd, %region_4.4_... | conditional | flops 458764 | bytes 6291917 | solution.py:351
  210.9 7.0 %all-to-all-start.3 = ((bf16[32,24,256]{2,1,0:T(8,128)(2,1)}), bf16[32,24,256]{2,1,0:T(8,128)(2,1)}, u32[]{:S(2)}, u32[]{:S(2)}) async-start(bf16[32,24,256]{2,1,0:T(8,128)(2,1)} %get-tuple-element.549), calls=%async_computation.3 | async-start | bytes 786432 | tf_op jit(solution)/shard_map/while/body/eval_jaxpr/cond/branch_3_fun/all_to_all | solution.py:345
  217.9 1.3 collective-permute-start.24
  219.3 2.1 collective-permute-start.25
  221.4 1.3 collective-permute-start.26
  222.7 1.3 collective-permute-start.21
  228.9 2.9 %all-to-all-done.3 = bf16[32,24,256]{2,1,0:T(8,128)(2,1)} async-done(((bf16[32,24,256]{2,1,0:T(8,128)(2,1)}), bf16[32,24,256]{2,1,0:T(8,128)(2,1)}, u32[]{:S(2)}, u32[]{:S(2)}) %all-to-all-start.3) | async-done | bytes 393248 | tf_op jit(solution)/shard_map/while/body/eval_jaxpr/cond/branch_3_fun/all_to_all | solution.py:345
  233.6 1.5 collective-permute-done.27
  235.2 1.6 select_select_fusion.7
  236.7 11.6 %all-to-all-start.8 = ((bf16[32,8,256]{2,1,0:T(8,128)(2,1)}), bf16[32,8,256]{2,1,0:T(8,128)(2,1)S(1)}, u32[]{:S(2)}, u32[]{:S(2)}) async-start(bf16[32,8,256]{2,1,0:T(8,128)(2,1)} %bitcast.41), calls=%async_computation.8 | async-start | bytes 262144 | tf_op jit(solution)/shard_map/while/body/eval_jaxpr/all_to_all | solution.py:444
  249.6 3.3 %prep.5 = (f32[512,512]{1,0:T(8,128)S(1)}, bf16[128,512]{1,0:T(8,128)(2,1)S(1)}, bf16[512,512]{1,0:T(8,128)(2,1)S(1)}) custom-call(s32[1]{0:T(128)} %bitcast.38.at_ref, bf16[2048,256]{1,0:T(8,128)(2,1)S(1)} %copy.68.table_ref, s32[4,512]{1,0:T(4,128)S(1)} %get-tuple-element.1007.target_ref, s32[4,512]{1,0:T(4,128)S(1)} %get-tuple-element.1008.time_ref, ...), custom_call_target="tpu_custom_call" | custom-call | flops 5000000000 | bytes 3826688 | tf_op jit(solution)/shard_map/while/body/eval_jaxpr/prep/pallas_call | solution.py:26
  253.7 2.5 codes.7
  257.8 6.1 %update.5 = (bf16[2048,256]{1,0:T(8,128)(2,1)}, bf16[768,256]{1,0:T(8,128)(2,1)}, bf16[256,256]{1,0:T(8,128)(2,1)}, bf16[256,256]{1,0:T(8,128)(2,1)}, bf16[256,2...) custom-call(s32[1]{0:T(128)} %bitcast.38.at_ref, ...), custom_call_target="tpu_custom_call" | custom-call | flops 6000000000 | bytes 8198144 | tf_op jit(solution)/shard_map/while/body/eval_jaxpr/update/pallas_call | solution.py:26
  (111 shorter events, 53.6 us)
Async XLA Ops:
  0.0 0.7 copy-start.7
  0.0 0.7 copy-start.8
  0.7 0.7 copy-start
  4.5 27.1 %all-to-all-start.9 = ((s32[256,1,128]{2,1,0:T(1,128)}), s32[256,1,128]{2,1,0:T(1,128)}, u32[]{:S(2)}, u32[]{:S(2)}) async-start(s32[256,1,128]{2,1,0:T(1,128)} %bitcast.28), calls=%async_computation.9 | async-start | bytes 262144 | tf_op jit(solution)/shard_map/all_to_all | solution.py:408
  20.4 0.7 copy-start.2
  21.2 1.2 copy-start.1
  39.3 0.7 copy-start.10
  39.3 0.7 copy-start.9
  41.4 18.7 %all-to-all-start.7 = ((bf16[32,24,256]{2,1,0:T(8,128)(2,1)}), bf16[32,24,256]{2,1,0:T(8,128)(2,1)}, u32[]{:S(2)}, u32[]{:S(2)}) async-start(bf16[32,24,256]{2,1,0:T(8,128)(2,1)} %get-tuple-element.585), calls=%async_computation.7 | async-start | bytes 786432 | tf_op jit(solution)/shard_map/while/body/eval_jaxpr/cond/branch_7_fun/all_to_all | solution.py:345
  46.1 4.6 %collective-permute-start.52 = (bf16[256,256]{1,0:T(8,128)(2,1)}, bf16[256,256]{1,0:T(8,128)(2,1)S(1)}, u32[]{:S(2)}, u32[]{:S(2)}) collective-permute-start(bf16[256,256]{1,0:T(8,128)(2,1)} %get-tuple-element.590), channel_id=1, source_target_pairs={{192,128},{224,160},{193,129},{225,161},{194,130},{226,162},{195,1... | collective-permute-start | bytes 393224 | tf_op jit(solution)/shard_map/while/body/eval_jaxpr/cond/branch_7_fun/ppermute | solution.py:329
  46.8 8.9 %collective-permute-start.53 = (bf16[256,256]{1,0:T(8,128)(2,1)}, bf16[256,256]{1,0:T(8,128)(2,1)S(1)}, u32[]{:S(2)}, u32[]{:S(2)}) collective-permute-start(bf16[256,256]{1,0:T(8,128)(2,1)} %get-tuple-element.591), channel_id=1, source_target_pairs={{192,64},{224,96},{193,65},{225,97},{194,66},{226,98},{195,67},{22... | collective-permute-start | bytes 393224 | tf_op jit(solution)/shard_map/while/body/eval_jaxpr/cond/branch_7_fun/ppermute | solution.py:329
  48.1 7.6 %collective-permute-start.54 = (bf16[256,256]{1,0:T(8,128)(2,1)}, bf16[256,256]{1,0:T(8,128)(2,1)S(1)}, u32[]{:S(2)}, u32[]{:S(2)}) collective-permute-start(bf16[256,256]{1,0:T(8,128)(2,1)} %get-tuple-element.592), channel_id=1, source_target_pairs={{192,0},{224,32},{193,1},{225,33},{194,2},{226,34},{195,3},{227,35... | collective-permute-start | bytes 393224 | tf_op jit(solution)/shard_map/while/body/eval_jaxpr/cond/branch_7_fun/ppermute | solution.py:329
  48.8 13.1 %collective-permute-start.49 = (bf16[256,256]{1,0:T(8,128)(2,1)}, bf16[256,256]{1,0:T(8,128)(2,1)S(1)}, u32[]{:S(2)}, u32[]{:S(2)}) collective-permute-start(bf16[256,256]{1,0:T(8,128)(2,1)} %get-tuple-element.586), channel_id=1, source_target_pairs={{192,128},{224,160},{193,129},{225,161},{194,130},{226,162},{195,1... | collective-permute-start | bytes 393224 | tf_op jit(solution)/shard_map/while/body/eval_jaxpr/cond/branch_7_fun/ppermute | solution.py:329
  49.4 12.5 %collective-permute-start.50 = (bf16[256,256]{1,0:T(8,128)(2,1)}, bf16[256,256]{1,0:T(8,128)(2,1)S(1)}, u32[]{:S(2)}, u32[]{:S(2)}) collective-permute-start(bf16[256,256]{1,0:T(8,128)(2,1)} %get-tuple-element.587), channel_id=1, source_target_pairs={{192,64},{224,96},{193,65},{225,97},{194,66},{226,98},{195,67},{22... | collective-permute-start | bytes 393224 | tf_op jit(solution)/shard_map/while/body/eval_jaxpr/cond/branch_7_fun/ppermute | solution.py:329
  50.8 11.2 %collective-permute-start.51 = (bf16[256,256]{1,0:T(8,128)(2,1)}, bf16[256,256]{1,0:T(8,128)(2,1)S(1)}, u32[]{:S(2)}, u32[]{:S(2)}) collective-permute-start(bf16[256,256]{1,0:T(8,128)(2,1)} %get-tuple-element.588), channel_id=1, source_target_pairs={{192,0},{224,32},{193,1},{225,33},{194,2},{226,34},{195,3},{227,35... | collective-permute-start | bytes 393224 | tf_op jit(solution)/shard_map/while/body/eval_jaxpr/cond/branch_7_fun/ppermute | solution.py:329
  56.6 6.9 %collective-permute-start.55 = (bf16[256,256]{1,0:T(8,128)(2,1)S(1)}, bf16[256,256]{1,0:T(8,128)(2,1)S(1)}, u32[]{:S(2)}, u32[]{:S(2)}) collective-permute-start(bf16[256,256]{1,0:T(8,128)(2,1)S(1)} %select_select_fusion.14), channel_id=1, source_target_pairs={{32,24},{33,25},{34,26},{35,27},{36,28},{37,29},{38,30},{39,31},{4... | collective-permute-start | bytes 393224 | tf_op jit(solution)/shard_map/while/body/eval_jaxpr/cond/branch_7_fun/ppermute | solution.py:335
  65.1 21.0 %all-to-all-start.8 = ((bf16[32,8,256]{2,1,0:T(8,128)(2,1)}), bf16[32,8,256]{2,1,0:T(8,128)(2,1)S(1)}, u32[]{:S(2)}, u32[]{:S(2)}) async-start(bf16[32,8,256]{2,1,0:T(8,128)(2,1)} %bitcast.41), calls=%async_computation.8 | async-start | bytes 262144 | tf_op jit(solution)/shard_map/while/body/eval_jaxpr/all_to_all | solution.py:444
  86.1 0.9 copy-start.6
  97.6 20.9 %all-to-all-start = ((bf16[32,24,256]{2,1,0:T(8,128)(2,1)}), bf16[32,24,256]{2,1,0:T(8,128)(2,1)}, u32[]{:S(2)}, u32[]{:S(2)}) async-start(bf16[32,24,256]{2,1,0:T(8,128)(2,1)} %get-tuple-element.522), calls=%async_computation | async-start | bytes 786432 | tf_op jit(solution)/shard_map/while/body/eval_jaxpr/cond/branch_0_fun/all_to_all | solution.py:345
  104.6 4.0 %collective-permute-start.3 = (bf16[256,256]{1,0:T(8,128)(2,1)}, bf16[256,256]{1,0:T(8,128)(2,1)S(1)}, u32[]{:S(2)}, u32[]{:S(2)}) collective-permute-start(bf16[256,256]{1,0:T(8,128)(2,1)} %get-tuple-element.527), channel_id=1, source_target_pairs={{0,192},{32,224},{1,193},{33,225},{2,194},{34,226},{3,195},{35,227... | collective-permute-start | bytes 393224 | tf_op jit(solution)/shard_map/while/body/eval_jaxpr/cond/branch_0_fun/ppermute | solution.py:329
  105.3 4.7 %collective-permute-start.4 = (bf16[256,256]{1,0:T(8,128)(2,1)}, bf16[256,256]{1,0:T(8,128)(2,1)S(1)}, u32[]{:S(2)}, u32[]{:S(2)}) collective-permute-start(bf16[256,256]{1,0:T(8,128)(2,1)} %get-tuple-element.528), channel_id=1, source_target_pairs={{0,128},{32,160},{1,129},{33,161},{2,130},{34,162},{3,131},{35,163... | collective-permute-start | bytes 393224 | tf_op jit(solution)/shard_map/while/body/eval_jaxpr/cond/branch_0_fun/ppermute | solution.py:329
  106.0 10.4 %collective-permute-start.5 = (bf16[256,256]{1,0:T(8,128)(2,1)}, bf16[256,256]{1,0:T(8,128)(2,1)S(1)}, u32[]{:S(2)}, u32[]{:S(2)}) collective-permute-start(bf16[256,256]{1,0:T(8,128)(2,1)} %get-tuple-element.529), channel_id=1, source_target_pairs={{0,64},{32,96},{1,65},{33,97},{2,66},{34,98},{3,67},{35,99},{4,68}... | collective-permute-start | bytes 393224 | tf_op jit(solution)/shard_map/while/body/eval_jaxpr/cond/branch_0_fun/ppermute | solution.py:329
  107.3 13.0 %collective-permute-start = (bf16[256,256]{1,0:T(8,128)(2,1)}, bf16[256,256]{1,0:T(8,128)(2,1)S(1)}, u32[]{:S(2)}, u32[]{:S(2)}) collective-permute-start(bf16[256,256]{1,0:T(8,128)(2,1)} %get-tuple-element.523), channel_id=1, source_target_pairs={{0,192},{32,224},{1,193},{33,225},{2,194},{34,226},{3,195},{35,227... | collective-permute-start | bytes 393224 | tf_op jit(solution)/shard_map/while/body/eval_jaxpr/cond/branch_0_fun/ppermute | solution.py:329
  108.0 12.4 %collective-permute-start.1 = (bf16[256,256]{1,0:T(8,128)(2,1)}, bf16[256,256]{1,0:T(8,128)(2,1)S(1)}, u32[]{:S(2)}, u32[]{:S(2)}) collective-permute-start(bf16[256,256]{1,0:T(8,128)(2,1)} %get-tuple-element.524), channel_id=1, source_target_pairs={{0,128},{32,160},{1,129},{33,161},{2,130},{34,162},{3,131},{35,163... | collective-permute-start | bytes 393224 | tf_op jit(solution)/shard_map/while/body/eval_jaxpr/cond/branch_0_fun/ppermute | solution.py:329
  108.7 13.2 %collective-permute-start.2 = (bf16[256,256]{1,0:T(8,128)(2,1)}, bf16[256,256]{1,0:T(8,128)(2,1)S(1)}, u32[]{:S(2)}, u32[]{:S(2)}) collective-permute-start(bf16[256,256]{1,0:T(8,128)(2,1)} %get-tuple-element.525), channel_id=1, source_target_pairs={{0,64},{32,96},{1,65},{33,97},{2,66},{34,98},{3,67},{35,99},{4,68}... | collective-permute-start | bytes 393224 | tf_op jit(solution)/shard_map/while/body/eval_jaxpr/cond/branch_0_fun/ppermute | solution.py:329
  116.4 5.5 %collective-permute-start.6 = (bf16[256,256]{1,0:T(8,128)(2,1)S(1)}, bf16[256,256]{1,0:T(8,128)(2,1)S(1)}, u32[]{:S(2)}, u32[]{:S(2)}) collective-permute-start(bf16[256,256]{1,0:T(8,128)(2,1)S(1)} %select_select_fusion), channel_id=1, source_target_pairs={{0,56},{1,57},{2,58},{3,59},{4,60},{5,61},{6,62},{7,63},{8,48},{9,... | collective-permute-start | bytes 393224 | tf_op jit(solution)/shard_map/while/body/eval_jaxpr/cond/branch_0_fun/ppermute | solution.py:335
  122.6 18.0 %all-to-all-start.8 = ((bf16[32,8,256]{2,1,0:T(8,128)(2,1)}), bf16[32,8,256]{2,1,0:T(8,128)(2,1)S(1)}, u32[]{:S(2)}, u32[]{:S(2)}) async-start(bf16[32,8,256]{2,1,0:T(8,128)(2,1)} %bitcast.41), calls=%async_computation.8 | async-start | bytes 262144 | tf_op jit(solution)/shard_map/while/body/eval_jaxpr/all_to_all | solution.py:444
  140.6 0.9 copy-start.6
  152.1 20.9 %all-to-all-start.7 = ((bf16[32,24,256]{2,1,0:T(8,128)(2,1)}), bf16[32,24,256]{2,1,0:T(8,128)(2,1)}, u32[]{:S(2)}, u32[]{:S(2)}) async-start(bf16[32,24,256]{2,1,0:T(8,128)(2,1)} %get-tuple-element.585), calls=%async_computation.7 | async-start | bytes 786432 | tf_op jit(solution)/shard_map/while/body/eval_jaxpr/cond/branch_7_fun/all_to_all | solution.py:345
  159.1 4.6 %collective-permute-start.52 = (bf16[256,256]{1,0:T(8,128)(2,1)}, bf16[256,256]{1,0:T(8,128)(2,1)S(1)}, u32[]{:S(2)}, u32[]{:S(2)}) collective-permute-start(bf16[256,256]{1,0:T(8,128)(2,1)} %get-tuple-element.590), channel_id=1, source_target_pairs={{192,128},{224,160},{193,129},{225,161},{194,130},{226,162},{195,1... | collective-permute-start | bytes 393224 | tf_op jit(solution)/shard_map/while/body/eval_jaxpr/cond/branch_7_fun/ppermute | solution.py:329
  159.8 9.3 %collective-permute-start.53 = (bf16[256,256]{1,0:T(8,128)(2,1)}, bf16[256,256]{1,0:T(8,128)(2,1)S(1)}, u32[]{:S(2)}, u32[]{:S(2)}) collective-permute-start(bf16[256,256]{1,0:T(8,128)(2,1)} %get-tuple-element.591), channel_id=1, source_target_pairs={{192,64},{224,96},{193,65},{225,97},{194,66},{226,98},{195,67},{22... | collective-permute-start | bytes 393224 | tf_op jit(solution)/shard_map/while/body/eval_jaxpr/cond/branch_7_fun/ppermute | solution.py:329
  161.1 8.0 %collective-permute-start.54 = (bf16[256,256]{1,0:T(8,128)(2,1)}, bf16[256,256]{1,0:T(8,128)(2,1)S(1)}, u32[]{:S(2)}, u32[]{:S(2)}) collective-permute-start(bf16[256,256]{1,0:T(8,128)(2,1)} %get-tuple-element.592), channel_id=1, source_target_pairs={{192,0},{224,32},{193,1},{225,33},{194,2},{226,34},{195,3},{227,35... | collective-permute-start | bytes 393224 | tf_op jit(solution)/shard_map/while/body/eval_jaxpr/cond/branch_7_fun/ppermute | solution.py:329
  161.8 13.0 %collective-permute-start.49 = (bf16[256,256]{1,0:T(8,128)(2,1)}, bf16[256,256]{1,0:T(8,128)(2,1)S(1)}, u32[]{:S(2)}, u32[]{:S(2)}) collective-permute-start(bf16[256,256]{1,0:T(8,128)(2,1)} %get-tuple-element.586), channel_id=1, source_target_pairs={{192,128},{224,160},{193,129},{225,161},{194,130},{226,162},{195,1... | collective-permute-start | bytes 393224 | tf_op jit(solution)/shard_map/while/body/eval_jaxpr/cond/branch_7_fun/ppermute | solution.py:329
  162.5 12.4 %collective-permute-start.50 = (bf16[256,256]{1,0:T(8,128)(2,1)}, bf16[256,256]{1,0:T(8,128)(2,1)S(1)}, u32[]{:S(2)}, u32[]{:S(2)}) collective-permute-start(bf16[256,256]{1,0:T(8,128)(2,1)} %get-tuple-element.587), channel_id=1, source_target_pairs={{192,64},{224,96},{193,65},{225,97},{194,66},{226,98},{195,67},{22... | collective-permute-start | bytes 393224 | tf_op jit(solution)/shard_map/while/body/eval_jaxpr/cond/branch_7_fun/ppermute | solution.py:329
  163.8 11.0 %collective-permute-start.51 = (bf16[256,256]{1,0:T(8,128)(2,1)}, bf16[256,256]{1,0:T(8,128)(2,1)S(1)}, u32[]{:S(2)}, u32[]{:S(2)}) collective-permute-start(bf16[256,256]{1,0:T(8,128)(2,1)} %get-tuple-element.588), channel_id=1, source_target_pairs={{192,0},{224,32},{193,1},{225,33},{194,2},{226,34},{195,3},{227,35... | collective-permute-start | bytes 393224 | tf_op jit(solution)/shard_map/while/body/eval_jaxpr/cond/branch_7_fun/ppermute | solution.py:329
  170.1 7.9 %collective-permute-start.55 = (bf16[256,256]{1,0:T(8,128)(2,1)S(1)}, bf16[256,256]{1,0:T(8,128)(2,1)S(1)}, u32[]{:S(2)}, u32[]{:S(2)}) collective-permute-start(bf16[256,256]{1,0:T(8,128)(2,1)S(1)} %select_select_fusion.14), channel_id=1, source_target_pairs={{32,24},{33,25},{34,26},{35,27},{36,28},{37,29},{38,30},{39,31},{4... | collective-permute-start | bytes 393224 | tf_op jit(solution)/shard_map/while/body/eval_jaxpr/cond/branch_7_fun/ppermute | solution.py:335
  179.5 19.9 %all-to-all-start.8 = ((bf16[32,8,256]{2,1,0:T(8,128)(2,1)}), bf16[32,8,256]{2,1,0:T(8,128)(2,1)S(1)}, u32[]{:S(2)}, u32[]{:S(2)}) async-start(bf16[32,8,256]{2,1,0:T(8,128)(2,1)} %bitcast.41), calls=%async_computation.8 | async-start | bytes 262144 | tf_op jit(solution)/shard_map/while/body/eval_jaxpr/all_to_all | solution.py:444
  199.4 0.9 copy-start.6
  210.9 20.9 %all-to-all-start.3 = ((bf16[32,24,256]{2,1,0:T(8,128)(2,1)}), bf16[32,24,256]{2,1,0:T(8,128)(2,1)}, u32[]{:S(2)}, u32[]{:S(2)}) async-start(bf16[32,24,256]{2,1,0:T(8,128)(2,1)} %get-tuple-element.549), calls=%async_computation.3 | async-start | bytes 786432 | tf_op jit(solution)/shard_map/while/body/eval_jaxpr/cond/branch_3_fun/all_to_all | solution.py:345
  217.9 7.4 %collective-permute-start.24 = (bf16[256,256]{1,0:T(8,128)(2,1)}, bf16[256,256]{1,0:T(8,128)(2,1)S(1)}, u32[]{:S(2)}, u32[]{:S(2)}) collective-permute-start(bf16[256,256]{1,0:T(8,128)(2,1)} %get-tuple-element.554), channel_id=1, source_target_pairs={{64,0},{96,32},{65,1},{97,33},{66,2},{98,34},{67,3},{99,35},{68,4}... | collective-permute-start | bytes 393224 | tf_op jit(solution)/shard_map/while/body/eval_jaxpr/cond/branch_3_fun/ppermute | solution.py:329
  219.3 7.4 %collective-permute-start.25 = (bf16[256,256]{1,0:T(8,128)(2,1)}, bf16[256,256]{1,0:T(8,128)(2,1)S(1)}, u32[]{:S(2)}, u32[]{:S(2)}) collective-permute-start(bf16[256,256]{1,0:T(8,128)(2,1)} %get-tuple-element.555), channel_id=1, source_target_pairs={{64,192},{96,224},{65,193},{97,225},{66,194},{98,226},{67,195},{99... | collective-permute-start | bytes 393224 | tf_op jit(solution)/shard_map/while/body/eval_jaxpr/cond/branch_3_fun/ppermute | solution.py:329
  221.4 5.3 %collective-permute-start.26 = (bf16[256,256]{1,0:T(8,128)(2,1)}, bf16[256,256]{1,0:T(8,128)(2,1)S(1)}, u32[]{:S(2)}, u32[]{:S(2)}) collective-permute-start(bf16[256,256]{1,0:T(8,128)(2,1)} %get-tuple-element.556), channel_id=1, source_target_pairs={{64,128},{96,160},{65,129},{97,161},{66,130},{98,162},{67,131},{99... | collective-permute-start | bytes 393224 | tf_op jit(solution)/shard_map/while/body/eval_jaxpr/cond/branch_3_fun/ppermute | solution.py:329
  222.7 10.9 %collective-permute-start.21 = (bf16[256,256]{1,0:T(8,128)(2,1)}, bf16[256,256]{1,0:T(8,128)(2,1)S(1)}, u32[]{:S(2)}, u32[]{:S(2)}) collective-permute-start(bf16[256,256]{1,0:T(8,128)(2,1)} %get-tuple-element.550), channel_id=1, source_target_pairs={{64,0},{96,32},{65,1},{97,33},{66,2},{98,34},{67,3},{99,35},{68,4}... | collective-permute-start | bytes 393224 | tf_op jit(solution)/shard_map/while/body/eval_jaxpr/cond/branch_3_fun/ppermute | solution.py:329
  224.0 9.6 %collective-permute-start.22 = (bf16[256,256]{1,0:T(8,128)(2,1)}, bf16[256,256]{1,0:T(8,128)(2,1)S(1)}, u32[]{:S(2)}, u32[]{:S(2)}) collective-permute-start(bf16[256,256]{1,0:T(8,128)(2,1)} %get-tuple-element.551), channel_id=1, source_target_pairs={{64,192},{96,224},{65,193},{97,225},{66,194},{98,226},{67,195},{99... | collective-permute-start | bytes 393224 | tf_op jit(solution)/shard_map/while/body/eval_jaxpr/cond/branch_3_fun/ppermute | solution.py:329
  225.3 8.3 %collective-permute-start.23 = (bf16[256,256]{1,0:T(8,128)(2,1)}, bf16[256,256]{1,0:T(8,128)(2,1)S(1)}, u32[]{:S(2)}, u32[]{:S(2)}) collective-permute-start(bf16[256,256]{1,0:T(8,128)(2,1)} %get-tuple-element.552), channel_id=1, source_target_pairs={{64,128},{96,160},{65,129},{97,161},{66,130},{98,162},{67,131},{99... | collective-permute-start | bytes 393224 | tf_op jit(solution)/shard_map/while/body/eval_jaxpr/cond/branch_3_fun/ppermute | solution.py:329
  227.6 7.6 %collective-permute-start.27 = (bf16[256,256]{1,0:T(8,128)(2,1)S(1)}, bf16[256,256]{1,0:T(8,128)(2,1)S(1)}, u32[]{:S(2)}, u32[]{:S(2)}) collective-permute-start(bf16[256,256]{1,0:T(8,128)(2,1)S(1)} %select_select_fusion.6), channel_id=1, source_target_pairs={{32,24},{33,25},{34,26},{35,27},{36,28},{37,29},{38,30},{39,31},{4... | collective-permute-start | bytes 393224 | tf_op jit(solution)/shard_map/while/body/eval_jaxpr/cond/branch_3_fun/ppermute | solution.py:335
  236.7 20.2 %all-to-all-start.8 = ((bf16[32,8,256]{2,1,0:T(8,128)(2,1)}), bf16[32,8,256]{2,1,0:T(8,128)(2,1)S(1)}, u32[]{:S(2)}, u32[]{:S(2)}) async-start(bf16[32,8,256]{2,1,0:T(8,128)(2,1)} %bitcast.41), calls=%async_computation.8 | async-start | bytes 262144 | tf_op jit(solution)/shard_map/while/body/eval_jaxpr/all_to_all | solution.py:444
  256.9 0.9 copy-start.6
  (7 other events, 4.6 us)

commit v3 on v2

--- a/solution.py
+++ b/solution.py
@@ -12,14 +12,14 @@
 BF16 = jnp.bfloat16
 I32 = jnp.int32
 MIB = 1024 * 1024
-VMEM_MIB = dict(plan=6, stage=6, codes=6, prep=12, serve=8, update=16)
+VMEM_MIB = dict(plan=6, stage=6, codes=6, prep=16, serve=8, update=16)
 
 
 def whole():
     return pl.BlockSpec(memory_space=pltpu.VMEM)
 
 
-def call(kernel, out_shape, args, flops=0, name=None, specs=None, scalars=()):
+def call(kernel, out_shape, args, flops=0, name=None, specs=None, scalars=(), aliases=None):
     moved = sum(a.size * a.dtype.itemsize for a in args)
     moved += sum(o.size * o.dtype.itemsize for o in jax.tree.leaves(out_shape))
     specs = specs or {}
@@ -32,6 +32,7 @@
             in_specs=[specs.get(i, whole()) for i in range(len(args))],
             out_specs=jax.tree.map(lambda _: whole(), out_shape),
         ),
+        input_output_aliases=aliases or {},
         compiler_params=pltpu.CompilerParams(vmem_limit_bytes=VMEM_MIB[name] * MIB),
         cost_estimate=pl.CostEstimate(flops=flops, bytes_accessed=moved, transcendentals=0),
         name=name,
@@ -75,7 +76,6 @@
     batches, events = source_ref.shape
     rows = ids_ref.shape[1]
     per = cap + ocap
-    own_total = rows * cap
     group_nodes = rows * node_dev
     upper = (
         lax.broadcasted_iota(I32, (events, events), 0)
@@ -102,9 +102,7 @@
         spot = (slot + b * per == lane_iota).astype(F32)
         high = high + dot_nt(both, (spot * (offset >> 6).astype(F32)).astype(BF16))
         low = low + dot_nt(both, (spot * (offset & 63).astype(F32)).astype(BF16))
-        places.append(
-            jnp.where(far, own_total + (dest ^ flip_ref[b]) * ocap + rank, dest * cap + rank)
-        )
+        places.append(jnp.where(far, dest ^ flip_ref[b], dest) * per + slot)
     ids = high.astype(I32) * 64 + low.astype(I32)
     for g in range(ids_ref.shape[0]):
         ids_ref[g] = ids
@@ -135,15 +133,18 @@
     return jnp.where(low == lane.astype(F32), high, -1.0).astype(BF16)
 
 
-def code_kernel(cap, per, at_ref, asked_ref, _, own_ref, far_ref):
-    b = at_ref[0]
+def write_codes(b, me, cap, per, asked_ref, own_ref, far_ref):
     groups, rows, _ = asked_ref.shape
-    own_ref[...] = spread_codes(asked_ref[at_ref[1]], b * per, cap)
+    own_ref[...] = spread_codes(asked_ref[me], b * per, per)
     block = rows * (per - cap)
     for g in range(groups):
         far_ref[g * block : (g + 1) * block, :] = spread_codes(
             asked_ref[g], b * per + cap, per - cap
         )
+
+
+def code_kernel(cap, per, at_ref, asked_ref, own_ref, far_ref):
+    write_codes(at_ref[0], at_ref[1], cap, per, asked_ref, own_ref, far_ref)
 
 
 def cosine(x):
@@ -167,6 +168,8 @@
 
 def prep_kernel(
     width,
+    cap,
+    per,
     at_ref,
     table_ref,
     target_ref,
@@ -176,12 +179,16 @@
     freq_ref,
     phase_ref,
     w_ref,
+    asked_ref,
     _,
     local_ref,
     scode_ref,
     same_ref,
+    own_code_ref,
+    far_code_ref,
 ):
     b = at_ref[0]
+    write_codes(b + 1, at_ref[1], cap, per, asked_ref, own_code_ref, far_code_ref)
     batches, events = target_ref.shape
     node_dev = node_time_ref.shape[1]
     enc_at = 2 * width
@@ -241,8 +248,12 @@
             out_refs[(start + part) // rows][...] = picked[part : part + rows]
 
 
-def serve_kernel(table_ref, own_code_ref, far_code_ref, own_ref, *far_refs):
-    serve_rows(table_ref, own_code_ref, [own_ref.at[i : i + 256] for i in range(0, own_ref.shape[0], 256)], 256)
+def serve_own_kernel(table_ref, own_code_ref, own_ref):
+    halves = [own_ref.at[i : i + 512] for i in range(0, own_ref.shape[0], 512)]
+    serve_rows(table_ref, own_code_ref, halves, 512)
+
+
+def serve_far_kernel(table_ref, far_code_ref, *far_refs):
     serve_rows(table_ref, far_code_ref, far_refs, 512)
 
 
@@ -250,8 +261,7 @@
     last,
     at_ref,
     table_ref,
-    own_back_ref,
-    far_back_ref,
+    back_ref,
     pcode_ref,
     local_ref,
     same_ref,
@@ -261,21 +271,14 @@
     w_hidden_ref,
     bias_input_ref,
     bias_hidden_ref,
-    own_code_ref,
     far_code_ref,
     new_ref,
-    own_out_ref,
     *far_out_refs,
 ):
     width = table_ref.shape[1]
     mem = local_ref[:, width:]
     hidden = dot(mem.astype(BF16), w_hidden_ref[...]) + bias_hidden_ref[...]
-    own_blocks = own_back_ref.shape[0] // LANES
-    far_blocks = far_back_ref.shape[0] // LANES
-    pcode = pcode_ref[0]
-    source = dot(expand(pcode, 0, own_blocks), own_back_ref[...]) + dot(
-        expand(pcode, own_blocks, far_blocks), far_back_ref[...]
-    )
+    source = dot(expand(pcode_ref[0], 0, back_ref.shape[0] // LANES), back_ref[...])
     w_source = w_ref[width : 2 * width, :]
     message = (local_ref[:, :width] + dot(source.astype(BF16), w_source)).astype(BF16)
     same = same_ref[...]
@@ -306,17 +309,17 @@
 
     @pl.when(at_ref[0] < last)
     def _():
-        serve_kernel(new_ref, own_code_ref, far_code_ref, own_out_ref, *far_out_refs)
-
-
-def fetch(own_rows, far_rows, owner, turn):
-    rows = own_rows.shape[0]
+        serve_far_kernel(new_ref, far_code_ref, *far_out_refs)
+
+
+def collect(table, own_code, far_rows, owner, turn, rows):
+    width = table.shape[1]
     ys = len(far_rows) // 2
 
     def branch(root):
         y, z = root // 2, root % 2
 
-        def body(own_rows, *far_rows):
+        def body(table, own_code, *far_rows):
             me = lax.axis_index("dom")
             my_y, my_z = me >> 1, me & 1
 
@@ -332,6 +335,13 @@
                     part = jnp.where(my_y == there, block, part)
                 return part
 
+            own_rows = call(
+                serve_own_kernel,
+                jax.ShapeDtypeStruct((own_code.shape[0], width), BF16),
+                (table, own_code),
+                flops=2 * 10**9,
+                name="serve",
+            ).reshape(rows, -1, width)
             across = lax.ppermute(
                 spread(1 - z),
                 ("dom", "row"),
@@ -341,14 +351,12 @@
                     for r in range(rows)
                 ],
             )
-            along = spread(z)
-            own_back = lax.all_to_all(own_rows, "row", 0, 0, tiled=True)
-            seat = my_z + (own_back[0, 0, 0].astype(F32) * 0.0).astype(I32)
-            return own_back, jnp.where(seat == z, along, across)
+            mine = jnp.where(my_z == z, spread(z), across).reshape(rows, -1, width)
+            return own_rows.at[:, own_rows.shape[1] - mine.shape[1] :, :].set(mine)
 
         return body
 
-    return lax.switch(owner, [branch(r) for r in range(2 * ys)], own_rows, *far_rows)
+    return lax.switch(owner, [branch(r) for r in range(2 * ys)], table, own_code, *far_rows)
 
 
 def shards(
@@ -382,9 +390,9 @@
         node_time.reshape(1, node_dev),
         frequency.reshape(1, -1),
         phase_shift.reshape(1, -1),
-        bias_input.reshape(1, -1),
-        bias_hidden.reshape(1, -1),
-    )
+    )
+    input_row = bias_input.reshape(1, -1)
+    hidden_row = bias_hidden.reshape(1, -1)
     anywhere = pl.BlockSpec(memory_space=pl.ANY)
     ids, pcode = call(
         functools.partial(plan_kernel, cap, ocap, node_dev),
@@ -397,7 +405,7 @@
         scalars=(flip,),
     )
     given = (memory,) + row_vectors
-    table, times_row, freq_row, phase_row, input_row, hidden_row = call(
+    table, times_row, freq_row, phase_row = call(
         stage_kernel,
         tuple(shape(v.shape, v.dtype) for v in given),
         (ids,) + given,
@@ -408,64 +416,58 @@
     asked = lax.all_to_all(
         ids.reshape(groups * rows, 1, batches * per), ("dom", "row"), 0, 0, tiled=True
     ).reshape(groups, rows, batches * per)
-    def codes(b, after):
-        return call(
-            functools.partial(code_kernel, cap, per),
-            (
-                shape((rows * cap, LANES), BF16),
-                shape((groups * rows * ocap, LANES), BF16),
-            ),
-            (asked, after),
-            flops=2 * 10**9,
-            name="codes",
-            specs={1: anywhere},
-            scalars=(jnp.stack([b, me]),),
-        )
-
-    own_shape = shape((rows * cap, width), BF16)
+    code_shapes = (
+        shape((rows * per, LANES), BF16),
+        shape((groups * rows * ocap, LANES), BF16),
+    )
+    own_code, far_code = call(
+        functools.partial(code_kernel, cap, per),
+        code_shapes,
+        (asked,),
+        flops=2 * 10**9,
+        name="codes",
+        scalars=(jnp.stack([jnp.zeros((), I32), me]),),
+    )
     far_shape = (shape((rows * ocap, width), BF16),) * groups
-    own_rows, *far_rows = call(
-        serve_kernel,
-        (own_shape,) + far_shape,
-        (table,) + tuple(codes(jnp.zeros((), I32), asked)),
-        flops=4 * 10**9,
-        name="serve",
+    far_rows = call(
+        serve_far_kernel, far_shape, (memory, far_code), flops=4 * 10**9, name="serve"
     )
 
     def batch(b, carry):
-        table, own_rows, *far_rows = carry
-        at = b.reshape(1)
-        own_back, mine = fetch(
-            own_rows.reshape(rows, cap, width),
+        table, own_code, *far_rows = carry
+        at = jnp.stack([b, me])
+        sent = collect(
+            table,
+            own_code,
             far_rows,
             lax.dynamic_index_in_dim(owner_group, b, 0, keepdims=False),
             turn,
+            rows,
         )
-        far_back = lax.all_to_all(mine.reshape(rows, ocap, width), "row", 0, 0, tiled=True)
-        local, scode, same = call(
-            functools.partial(prep_kernel, width),
+        back = lax.all_to_all(sent, "row", 0, 0, tiled=True).reshape(rows * per, width)
+        local, scode, same, next_own, next_far = call(
+            functools.partial(prep_kernel, width, cap, per),
             (
                 shape((events, 2 * width), F32),
                 shape((LANES, events), BF16),
                 shape((events, events), BF16),
-            ),
-            (table, target, event_time, times_row, edge_feat, freq_row, phase_row, w_message, mine),
+            )
+            + code_shapes,
+            (table, target, event_time, times_row, edge_feat, freq_row, phase_row, w_message, asked, sent),
             flops=5 * 10**9,
             name="prep",
             specs={
                 4: pl.BlockSpec((1,) + edge_feat.shape[1:], lambda i, at: (at[0], 0, 0)),
-                8: anywhere,
+                9: anywhere,
             },
             scalars=(at,),
         )
-        own_code, far_code = codes(b + 1, mine)
-        return call(
+        result = call(
             functools.partial(update_kernel, batches - 1),
-            (shape((node_dev, width), BF16), own_shape) + far_shape,
+            (shape((node_dev, width), BF16),) + far_shape,
             (
                 table,
-                own_back.reshape(rows * cap, width),
-                far_back.reshape(rows * ocap, width),
+                back,
                 pcode,
                 local,
                 same,
@@ -475,16 +477,17 @@
                 w_hidden,
                 input_row,
                 hidden_row,
-                own_code,
-                far_code,
+                next_far,
             ),
             flops=6 * 10**9,
             name="update",
-            specs={3: pl.BlockSpec((1, events, LANES), lambda i, at: (at[0], 0, 0))},
+            specs={2: pl.BlockSpec((1, events, LANES), lambda i, at: (at[0], 0, 0))},
             scalars=(at,),
+            aliases={1: 0},
         )
-
-    return lax.fori_loop(0, batches, batch, (table, own_rows, *far_rows))[0]
+        return (result[0], next_own) + tuple(result[1:])
+
+    return lax.fori_loop(0, batches, batch, (table, own_code, *far_rows))[0]
 
 
 def solution(mesh):

time: 267 us -> 250 us (0.936)
  starting transfers between devices: 116 us -> 63.2 us
  waiting for transfers between devices: 41.7 us -> 92 us
  local copies, waits for them, and re-layouts: 22.5 us -> 8.42 us
  Pallas kernels: 68.8 us -> 74.9 us
  loops' own time: 6 us -> 2.93 us
    all_to_all x8 -> x4, starting transfers between devices: 70.6 us -> 21.1 us  [batch(): lax.all_to_all(sent, 'row', 0, 0, tiled=True).reshape(rows * per, width)]
    all_to_all x8 -> x4, waiting for transfers between devices: 10.4 us -> 43.6 us  [batch(): lax.all_to_all(sent, 'row', 0, 0, tiled=True).reshape(rows * per, width)]
    ppermute x4, waiting for transfers between devices: 6.21 us -> 18.3 us  [body(): lax.ppermute(spread(1 - z), ('dom', 'row'), [((2 * i + z) * rows + r, (2...]
    while x20 -> x48, local copies, waits for them, and re-layouts: 11.1 us -> 2.82 us
    pallas_call x16, Pallas kernels: 68.8 us -> 74.9 us  [call(): pl.pallas_call(kernel, out_shape=out_shape, grid_spec=pltpu.PrefetchScala...]
    select_n x4 -> x0, other arithmetic: 5.46 us -> none  [body(): return (own_back, jnp.where(seat == z, along, across))]
    ppermute x24, waiting for transfers between devices: 16.9 us -> 22 us  [spread(): block = lax.ppermute(far_rows[2 * there + which], 'dom', pairs)]
    scatter x0 -> x4, other arithmetic: none -> 4.92 us  [body(): return own_rows.at[:, own_rows.shape[1] - mine.shape[1]:, :].set(mine)]
  transfers between devices with their start and end apart: 37 -> 33, of which waited for: 16 -> 15; matrix products, arithmetic and copies ran while one was open for 5% -> 1% of each run, Pallas kernels for 9% -> 13%
where the time goes in v3:
time: 250 us; the launch traced here: 249 us
  waiting for transfers between devices  92 us (37%)
  Pallas kernels  74.9 us (30%)
  starting transfers between devices  63.2 us (25%)
  local copies, waits for them, and re-layouts  8.42 us (3%)
  other arithmetic  7.26 us (3%)
  loops' own time  2.93 us (1%)
    pallas_call x16, Pallas kernels, call(): pl.pallas_call(kernel, out_shape=out_shape, grid_spec=pltpu.PrefetchScala...  74.9 us
    all_to_all x4, waiting for transfers between devices, batch(): lax.all_to_all(sent, 'row', 0, 0, tiled=True).reshape(rows * per, width)  43.6 us
    ppermute x24, waiting for transfers between devices, spread(): block = lax.ppermute(far_rows[2 * there + which], 'dom', pairs)  22 us
    all_to_all x4, starting transfers between devices, batch(): lax.all_to_all(sent, 'row', 0, 0, tiled=True).reshape(rows * per, width)  21.1 us
    ppermute x24, starting transfers between devices, spread(): block = lax.ppermute(far_rows[2 * there + which], 'dom', pairs)  21 us
    ppermute x4, waiting for transfers between devices, body(): lax.ppermute(spread(1 - z), ('dom', 'row'), [((2 * i + z) * rows + r, (2...  18.3 us
    all_to_all x1, starting transfers between devices, shards(): lax.all_to_all(ids.reshape(groups * rows, 1, batches * per), ('dom', 'row...  15.9 us
    all_to_all x1, waiting for transfers between devices, shards(): lax.all_to_all(ids.reshape(groups * rows, 1, batches * per), ('dom', 'row...  8.14 us
  transfers between devices with their start and end apart: 33, of which 15 were waited for; matrix products, arithmetic and copies ran while one was open for 1% of the time, Pallas kernels for 13%

profile of v3, /device:TPU:9, one launch (start us, length us, event | category | flops | bytes accessed | tf_op | source)
XLA Modules:
  0.0 248.8 jit_solution(16931888593726567077)
XLA Ops:
  1.4 3.1 %plan.1 = (s32[8,32,128]{2,1,0:T(8,128)}, bf16[4,512,128]{2,1,0:T(8,128)(2,1)}) custom-call(s32[4]{0:T(128)S(1)} %compare_select_fusion.flip_ref, s32[4,512]{1,0:T(4,128)S(1)} %copy-done), custom_call_target="tpu_custom_call" | custom-call | bytes 663552 | tf_op jit(solution)/shard_map/plan/pallas_call | solution.py:26
  4.5 15.9 %all-to-all-start.1 = ((s32[256,1,128]{2,1,0:T(1,128)}), s32[256,1,128]{2,1,0:T(1,128)}, u32[]{:S(2)}, u32[]{:S(2)}) async-start(s32[256,1,128]{2,1,0:T(1,128)} %bitcast.25), calls=%async_computation.1 | async-start | bytes 262144 | tf_op jit(solution)/shard_map/all_to_all | solution.py:416
  23.5 8.1 %all-to-all-done.1 = s32[256,1,128]{2,1,0:T(1,128)} async-done(((s32[256,1,128]{2,1,0:T(1,128)}), s32[256,1,128]{2,1,0:T(1,128)}, u32[]{:S(2)}, u32[]{:S(2)}) %all-to-all-start.1) | async-done | bytes 131104 | tf_op jit(solution)/shard_map/all_to_all | solution.py:416
  31.6 2.7 %codes.1 = (bf16[1024,128]{1,0:T(8,128)(2,1)}, bf16[2048,128]{1,0:T(8,128)(2,1)S(1)}) custom-call(s32[2]{0:T(128)S(1)} %pad_add_fusion.1.at_ref, s32[8,32,128]{2,1,0:T(8,128)} %bitcast.26.asked_ref), custom_call_target="tpu_custom_call" | custom-call | flops 2000000000 | bytes 917504 | tf_op jit(solution)/shard_map/codes/pallas_call | solution.py:26
  34.3 3.0 %serve.17 = (bf16[256,256]{1,0:T(8,128)(2,1)S(1)}, bf16[256,256]{1,0:T(8,128)(2,1)S(1)}, bf16[256,256]{1,0:T(8,128)(2,1)S(1)}, bf16[256,256]{1,0:T(8,128)(2,1)S(...) custom-call(bf16[2048,256]{1,0:T(8,128)(2,1)S(1)} %copy-done.2, ...), custom_call_target="tpu_custom_call" | custom-call | flops 4000000000 | bytes 2621440 | tf_op jit(solution)/shard_map/serve/pallas_call | solution.py:26
  37.3 211.5 %while.39 = (s32[]{:T(128)}, bf16[2048,256]{1,0:T(8,128)(2,1)}, bf16[1024,128]{1,0:T(8,128)(2,1)}, bf16[256,256]{1,0:T(8,128)(2,1)S(1)}, bf16[256,256]{1,0:T(8,1...) while((s32[]{:T(128)}, bf16[2048,256]{1,0:T(8,128)(2,1)}, ...), condition=%wide.region_9.10_spmd, body=%wide.region_0.9_spmd.sunk | while | flops 13000458240 | bytes 23466492 | solution.py:490
  38.5 18.7 %conditional.2 = (bf16[32,32,256]{2,1,0:T(8,128)(2,1)}) conditional(s32[]{:T(128)} %bitcast.42, (bf16[2048,256]{1,0:T(8,128)(2,1)}, bf16[1024,128]{1,0:T(8,128)(2,1)}, bf16[256,256]{1,0:T(8,128)(2,1)}, bf16[256,256]{1,0:T(8,128)(2,1)S(1)}, bf16[256,256]{1,0:T(8,128)(2,1)S(1)}, ...), branch_computations={%region_1.1_spmd, %region_2.2_spmd, %region_3.3_spmd, %region_4.4_... | conditional | flops 2000458752 | bytes 6947203 | solution.py:359
  38.5 1.3 collective-permute-start.38
  41.2 1.3 collective-permute-start.35
  43.1 2.0 collective-permute-done.38
  45.9 1.3 collective-permute-start.41
  47.1 3.3 %serve.14 = bf16[1024,256]{1,0:T(8,128)(2,1)} custom-call(bf16[2048,256]{1,0:T(8,128)(2,1)} %get-tuple-element.692.table_ref, bf16[1024,128]{1,0:T(8,128)(2,1)} %get-tuple-element.693.own_code_ref), custom_call_target="tpu_custom_call" | custom-call | flops 2000000000 | bytes 1835008 | tf_op jit(solution)/shard_map/while/body/eval_jaxpr/cond/branch_5_fun/serve/pallas_call | solution.py:26
  50.5 5.9 %collective-permute-done.41 = bf16[256,256]{1,0:T(8,128)(2,1)S(1)} collective-permute-done((bf16[256,256]{1,0:T(8,128)(2,1)S(1)}, bf16[256,256]{1,0:T(8,128)(2,1)S(1)}, u32[]{:S(2)}, u32[]{:S(2)}) %collective-permute-start.41) | collective-permute-done | bytes 131104 | tf_op jit(solution)/shard_map/while/body/eval_jaxpr/cond/branch_5_fun/ppermute | solution.py:345
  57.2 4.9 %all-to-all-start = ((bf16[32,32,256]{2,1,0:T(8,128)(2,1)}), bf16[32,32,256]{2,1,0:T(8,128)(2,1)S(1)}, u32[]{:S(2)}, u32[]{:S(2)}) async-start(bf16[32,32,256]{2,1,0:T(8,128)(2,1)} %get-tuple-element.1121._), calls=%async_computation | async-start | bytes 1048576 | tf_op jit(solution)/shard_map/while/body/eval_jaxpr/all_to_all | solution.py:447
  62.9 4.7 %prep.5 = (f32[512,512]{1,0:T(8,128)S(1)}, bf16[128,512]{1,0:T(8,128)(2,1)S(1)}, bf16[512,512]{1,0:T(8,128)(2,1)S(1)}, bf16[1024,128]{1,0:T(8,128)(2,1)}, bf16[2048,128]{1,0:T(8,128)(2,1)S(1)}) custom-call(s32[2]{0:T(128)S(1)} %pad_add_fusion.3.at_ref, bf16[2048,256]{1,0:T(8,128)(2,1)} %get-tuple-element.1064.table_ref, s32[4,512]{1,0:T(4,128)S(1)} %copy-done.9, ...), custom_call_target="tpu_custom_call" | custom-call | flops 5000000000 | bytes 5137408 | tf_op jit(solution)/shard_map/while/body/eval_jaxpr/prep/pallas_call | solution.py:26
  67.7 11.0 %all-to-all-done = bf16[32,32,256]{2,1,0:T(8,128)(2,1)S(1)} async-done(((bf16[32,32,256]{2,1,0:T(8,128)(2,1)}), bf16[32,32,256]{2,1,0:T(8,128)(2,1)S(1)}, u32[]{:S(2)}, u32[]{:S(2)}) %all-to-all-start) | async-done | bytes 524320 | tf_op jit(solution)/shard_map/while/body/eval_jaxpr/all_to_all | solution.py:447
  78.6 8.8 %update.5 = (bf16[2048,256]{1,0:T(8,128)(2,1)}, bf16[256,256]{1,0:T(8,128)(2,1)S(1)}, bf16[256,256]{1,0:T(8,128)(2,1)S(1)}, bf16[256,256]{1,0:T(8,128)(2,1)S(1)}...) custom-call(s32[2]{0:T(128)S(1)} %pad_add_fusion.3.at_ref, ...), custom_call_target="tpu_custom_call", output_to_operand_aliasing={{0}: (1, {})} | custom-call | flops 6000000000 | bytes 7608320 | tf_op jit(solution)/shard_map/while/body/eval_jaxpr/update/pallas_call | solution.py:26
  88.6 23.9 %conditional.2 = (bf16[32,32,256]{2,1,0:T(8,128)(2,1)}) conditional(s32[]{:T(128)} %bitcast.42, (bf16[2048,256]{1,0:T(8,128)(2,1)}, bf16[1024,128]{1,0:T(8,128)(2,1)}, bf16[256,256]{1,0:T(8,128)(2,1)}, bf16[256,256]{1,0:T(8,128)(2,1)S(1)}, bf16[256,256]{1,0:T(8,128)(2,1)S(1)}, ...), branch_computations={%region_1.1_spmd, %region_2.2_spmd, %region_3.3_spmd, %region_4.4_... | conditional | flops 2000458752 | bytes 6947203 | solution.py:359
  90.0 1.3 collective-permute-start.5
  92.7 1.3 collective-permute-start.2
  94.0 10.7 %collective-permute-done.5 = bf16[256,256]{1,0:T(8,128)(2,1)S(1)} collective-permute-done((bf16[256,256]{1,0:T(8,128)(2,1)S(1)}, bf16[256,256]{1,0:T(8,128)(2,1)S(1)}, u32[]{:S(2)}, u32[]{:S(2)}) %collective-permute-start.5) | collective-permute-done | bytes 131104 | tf_op jit(solution)/shard_map/while/body/eval_jaxpr/cond/branch_0_fun/ppermute | solution.py:332
  104.7 1.3 collective-permute-start.6
  106.0 3.3 %serve.9 = bf16[1024,256]{1,0:T(8,128)(2,1)} custom-call(bf16[2048,256]{1,0:T(8,128)(2,1)} %get-tuple-element.642.table_ref, bf16[1024,128]{1,0:T(8,128)(2,1)} %get-tuple-element.643.own_code_ref), custom_call_target="tpu_custom_call" | custom-call | flops 2000000000 | bytes 1835008 | tf_op jit(solution)/shard_map/while/body/eval_jaxpr/cond/branch_0_fun/serve/pallas_call | solution.py:26
  110.3 1.4 collective-permute-done.6
  112.5 4.7 %all-to-all-start = ((bf16[32,32,256]{2,1,0:T(8,128)(2,1)}), bf16[32,32,256]{2,1,0:T(8,128)(2,1)S(1)}, u32[]{:S(2)}, u32[]{:S(2)}) async-start(bf16[32,32,256]{2,1,0:T(8,128)(2,1)} %get-tuple-element.1121._), calls=%async_computation | async-start | bytes 1048576 | tf_op jit(solution)/shard_map/while/body/eval_jaxpr/all_to_all | solution.py:447
  117.9 4.7 %prep.5 = (f32[512,512]{1,0:T(8,128)S(1)}, bf16[128,512]{1,0:T(8,128)(2,1)S(1)}, bf16[512,512]{1,0:T(8,128)(2,1)S(1)}, bf16[1024,128]{1,0:T(8,128)(2,1)}, bf16[2048,128]{1,0:T(8,128)(2,1)S(1)}) custom-call(s32[2]{0:T(128)S(1)} %pad_add_fusion.3.at_ref, bf16[2048,256]{1,0:T(8,128)(2,1)} %get-tuple-element.1064.table_ref, s32[4,512]{1,0:T(4,128)S(1)} %copy-done.9, ...), custom_call_target="tpu_custom_call" | custom-call | flops 5000000000 | bytes 5137408 | tf_op jit(solution)/shard_map/while/body/eval_jaxpr/prep/pallas_call | solution.py:26
  122.7 10.9 %all-to-all-done = bf16[32,32,256]{2,1,0:T(8,128)(2,1)S(1)} async-done(((bf16[32,32,256]{2,1,0:T(8,128)(2,1)}), bf16[32,32,256]{2,1,0:T(8,128)(2,1)S(1)}, u32[]{:S(2)}, u32[]{:S(2)}) %all-to-all-start) | async-done | bytes 524320 | tf_op jit(solution)/shard_map/while/body/eval_jaxpr/all_to_all | solution.py:447
  133.5 8.8 %update.5 = (bf16[2048,256]{1,0:T(8,128)(2,1)}, bf16[256,256]{1,0:T(8,128)(2,1)S(1)}, bf16[256,256]{1,0:T(8,128)(2,1)S(1)}, bf16[256,256]{1,0:T(8,128)(2,1)S(1)}...) custom-call(s32[2]{0:T(128)S(1)} %pad_add_fusion.3.at_ref, ...), custom_call_target="tpu_custom_call", output_to_operand_aliasing={{0}: (1, {})} | custom-call | flops 6000000000 | bytes 7608320 | tf_op jit(solution)/shard_map/while/body/eval_jaxpr/update/pallas_call | solution.py:26
  143.5 22.3 %conditional.2 = (bf16[32,32,256]{2,1,0:T(8,128)(2,1)}) conditional(s32[]{:T(128)} %bitcast.42, (bf16[2048,256]{1,0:T(8,128)(2,1)}, bf16[1024,128]{1,0:T(8,128)(2,1)}, bf16[256,256]{1,0:T(8,128)(2,1)}, bf16[256,256]{1,0:T(8,128)(2,1)S(1)}, bf16[256,256]{1,0:T(8,128)(2,1)S(1)}, ...), branch_computations={%region_1.1_spmd, %region_2.2_spmd, %region_3.3_spmd, %region_4.4_... | conditional | flops 2000458752 | bytes 6947203 | solution.py:359
  144.2 1.3 collective-permute-start.53
  146.9 1.3 collective-permute-start.50
  148.9 4.1 %collective-permute-done.53 = bf16[256,256]{1,0:T(8,128)(2,1)S(1)} collective-permute-done((bf16[256,256]{1,0:T(8,128)(2,1)S(1)}, bf16[256,256]{1,0:T(8,128)(2,1)S(1)}, u32[]{:S(2)}, u32[]{:S(2)}) %collective-permute-start.53) | collective-permute-done | bytes 131104 | tf_op jit(solution)/shard_map/while/body/eval_jaxpr/cond/branch_7_fun/ppermute | solution.py:332
  155.2 3.3 %serve.16 = bf16[1024,256]{1,0:T(8,128)(2,1)} custom-call(bf16[2048,256]{1,0:T(8,128)(2,1)} %get-tuple-element.712.table_ref, bf16[1024,128]{1,0:T(8,128)(2,1)} %get-tuple-element.713.own_code_ref), custom_call_target="tpu_custom_call" | custom-call | flops 2000000000 | bytes 1835008 | tf_op jit(solution)/shard_map/while/body/eval_jaxpr/cond/branch_7_fun/serve/pallas_call | solution.py:26
  158.6 5.5 %collective-permute-done.55 = bf16[256,256]{1,0:T(8,128)(2,1)S(1)} collective-permute-done((bf16[256,256]{1,0:T(8,128)(2,1)S(1)}, bf16[256,256]{1,0:T(8,128)(2,1)S(1)}, u32[]{:S(2)}, u32[]{:S(2)}) %collective-permute-start.55) | collective-permute-done | bytes 131104 | tf_op jit(solution)/shard_map/while/body/eval_jaxpr/cond/branch_7_fun/ppermute | solution.py:345
  164.1 1.7 bitcast_dynamic-update-slice_fusion.7
  165.8 5.8 %all-to-all-start = ((bf16[32,32,256]{2,1,0:T(8,128)(2,1)}), bf16[32,32,256]{2,1,0:T(8,128)(2,1)S(1)}, u32[]{:S(2)}, u32[]{:S(2)}) async-start(bf16[32,32,256]{2,1,0:T(8,128)(2,1)} %get-tuple-element.1121._), calls=%async_computation | async-start | bytes 1048576 | tf_op jit(solution)/shard_map/while/body/eval_jaxpr/all_to_all | solution.py:447
  172.4 4.7 %prep.5 = (f32[512,512]{1,0:T(8,128)S(1)}, bf16[128,512]{1,0:T(8,128)(2,1)S(1)}, bf16[512,512]{1,0:T(8,128)(2,1)S(1)}, bf16[1024,128]{1,0:T(8,128)(2,1)}, bf16[2048,128]{1,0:T(8,128)(2,1)S(1)}) custom-call(s32[2]{0:T(128)S(1)} %pad_add_fusion.3.at_ref, bf16[2048,256]{1,0:T(8,128)(2,1)} %get-tuple-element.1064.table_ref, s32[4,512]{1,0:T(4,128)S(1)} %copy-done.9, ...), custom_call_target="tpu_custom_call" | custom-call | flops 5000000000 | bytes 5137408 | tf_op jit(solution)/shard_map/while/body/eval_jaxpr/prep/pallas_call | solution.py:26
  177.1 10.9 %all-to-all-done = bf16[32,32,256]{2,1,0:T(8,128)(2,1)S(1)} async-done(((bf16[32,32,256]{2,1,0:T(8,128)(2,1)}), bf16[32,32,256]{2,1,0:T(8,128)(2,1)S(1)}, u32[]{:S(2)}, u32[]{:S(2)}) %all-to-all-start) | async-done | bytes 524320 | tf_op jit(solution)/shard_map/while/body/eval_jaxpr/all_to_all | solution.py:447
  188.0 8.8 %update.5 = (bf16[2048,256]{1,0:T(8,128)(2,1)}, bf16[256,256]{1,0:T(8,128)(2,1)S(1)}, bf16[256,256]{1,0:T(8,128)(2,1)S(1)}, bf16[256,256]{1,0:T(8,128)(2,1)S(1)}...) custom-call(s32[2]{0:T(128)S(1)} %pad_add_fusion.3.at_ref, ...), custom_call_target="tpu_custom_call", output_to_operand_aliasing={{0}: (1, {})} | custom-call | flops 6000000000 | bytes 7608320 | tf_op jit(solution)/shard_map/while/body/eval_jaxpr/update/pallas_call | solution.py:26
  198.0 22.2 %conditional.2 = (bf16[32,32,256]{2,1,0:T(8,128)(2,1)}) conditional(s32[]{:T(128)} %bitcast.42, (bf16[2048,256]{1,0:T(8,128)(2,1)}, bf16[1024,128]{1,0:T(8,128)(2,1)}, bf16[256,256]{1,0:T(8,128)(2,1)}, bf16[256,256]{1,0:T(8,128)(2,1)S(1)}, bf16[256,256]{1,0:T(8,128)(2,1)S(1)}, ...), branch_computations={%region_1.1_spmd, %region_2.2_spmd, %region_3.3_spmd, %region_4.4_... | conditional | flops 2000458752 | bytes 6947203 | solution.py:359
  203.4 4.0 %collective-permute-done.53 = bf16[256,256]{1,0:T(8,128)(2,1)S(1)} collective-permute-done((bf16[256,256]{1,0:T(8,128)(2,1)S(1)}, bf16[256,256]{1,0:T(8,128)(2,1)S(1)}, u32[]{:S(2)}, u32[]{:S(2)}) %collective-permute-start.53) | collective-permute-done | bytes 131104 | tf_op jit(solution)/shard_map/while/body/eval_jaxpr/cond/branch_7_fun/ppermute | solution.py:332
  209.6 3.3 %serve.16 = bf16[1024,256]{1,0:T(8,128)(2,1)} custom-call(bf16[2048,256]{1,0:T(8,128)(2,1)} %get-tuple-element.712.table_ref, bf16[1024,128]{1,0:T(8,128)(2,1)} %get-tuple-element.713.own_code_ref), custom_call_target="tpu_custom_call" | custom-call | flops 2000000000 | bytes 1835008 | tf_op jit(solution)/shard_map/while/body/eval_jaxpr/cond/branch_7_fun/serve/pallas_call | solution.py:26
  213.1 5.4 %collective-permute-done.55 = bf16[256,256]{1,0:T(8,128)(2,1)S(1)} collective-permute-done((bf16[256,256]{1,0:T(8,128)(2,1)S(1)}, bf16[256,256]{1,0:T(8,128)(2,1)S(1)}, u32[]{:S(2)}, u32[]{:S(2)}) %collective-permute-start.55) | collective-permute-done | bytes 131104 | tf_op jit(solution)/shard_map/while/body/eval_jaxpr/cond/branch_7_fun/ppermute | solution.py:345
  218.5 1.7 bitcast_dynamic-update-slice_fusion.7
  220.2 5.7 %all-to-all-start = ((bf16[32,32,256]{2,1,0:T(8,128)(2,1)}), bf16[32,32,256]{2,1,0:T(8,128)(2,1)S(1)}, u32[]{:S(2)}, u32[]{:S(2)}) async-start(bf16[32,32,256]{2,1,0:T(8,128)(2,1)} %get-tuple-element.1121._), calls=%async_computation | async-start | bytes 1048576 | tf_op jit(solution)/shard_map/while/body/eval_jaxpr/all_to_all | solution.py:447
  226.7 4.7 %prep.5 = (f32[512,512]{1,0:T(8,128)S(1)}, bf16[128,512]{1,0:T(8,128)(2,1)S(1)}, bf16[512,512]{1,0:T(8,128)(2,1)S(1)}, bf16[1024,128]{1,0:T(8,128)(2,1)}, bf16[2048,128]{1,0:T(8,128)(2,1)S(1)}) custom-call(s32[2]{0:T(128)S(1)} %pad_add_fusion.3.at_ref, bf16[2048,256]{1,0:T(8,128)(2,1)} %get-tuple-element.1064.table_ref, s32[4,512]{1,0:T(4,128)S(1)} %copy-done.9, ...), custom_call_target="tpu_custom_call" | custom-call | flops 5000000000 | bytes 5137408 | tf_op jit(solution)/shard_map/while/body/eval_jaxpr/prep/pallas_call | solution.py:26
  231.5 10.9 %all-to-all-done = bf16[32,32,256]{2,1,0:T(8,128)(2,1)S(1)} async-done(((bf16[32,32,256]{2,1,0:T(8,128)(2,1)}), bf16[32,32,256]{2,1,0:T(8,128)(2,1)S(1)}, u32[]{:S(2)}, u32[]{:S(2)}) %all-to-all-start) | async-done | bytes 524320 | tf_op jit(solution)/shard_map/while/body/eval_jaxpr/all_to_all | solution.py:447
  242.3 6.5 %update.5 = (bf16[2048,256]{1,0:T(8,128)(2,1)}, bf16[256,256]{1,0:T(8,128)(2,1)S(1)}, bf16[256,256]{1,0:T(8,128)(2,1)S(1)}, bf16[256,256]{1,0:T(8,128)(2,1)S(1)}...) custom-call(s32[2]{0:T(128)S(1)} %pad_add_fusion.3.at_ref, ...), custom_call_target="tpu_custom_call", output_to_operand_aliasing={{0}: (1, {})} | custom-call | flops 6000000000 | bytes 7608320 | tf_op jit(solution)/shard_map/while/body/eval_jaxpr/update/pallas_call | solution.py:26
  (125 shorter events, 30.4 us)
Async XLA Ops:
  0.0 0.7 copy-start.7
  4.5 27.1 %all-to-all-start.1 = ((s32[256,1,128]{2,1,0:T(1,128)}), s32[256,1,128]{2,1,0:T(1,128)}, u32[]{:S(2)}, u32[]{:S(2)}) async-start(s32[256,1,128]{2,1,0:T(1,128)} %bitcast.25), calls=%async_computation.1 | async-start | bytes 262144 | tf_op jit(solution)/shard_map/all_to_all | solution.py:416
  21.2 1.2 copy-start.1
  31.6 2.7 %copy-start.2 = (bf16[2048,256]{1,0:T(8,128)(2,1)S(1)}, bf16[2048,256]{1,0:T(8,128)(2,1)}, u32[]{:S(2)}) copy-start(bf16[2048,256]{1,0:T(8,128)(2,1)} %table_ref.1) | copy-start | bytes 3145732
  38.5 6.6 %collective-permute-start.38 = (bf16[256,256]{1,0:T(8,128)(2,1)S(1)}, bf16[256,256]{1,0:T(8,128)(2,1)S(1)}, u32[]{:S(2)}, u32[]{:S(2)}) collective-permute-start(bf16[256,256]{1,0:T(8,128)(2,1)S(1)} %get-tuple-element.698), channel_id=1, source_target_pairs={{128,64},{160,96},{129,65},{161,97},{130,66},{162,98},{131,67},{16... | collective-permute-start | bytes 393224 | tf_op jit(solution)/shard_map/while/body/eval_jaxpr/cond/branch_5_fun/ppermute | solution.py:332
  39.8 6.0 %collective-permute-start.39 = (bf16[256,256]{1,0:T(8,128)(2,1)S(1)}, bf16[256,256]{1,0:T(8,128)(2,1)S(1)}, u32[]{:S(2)}, u32[]{:S(2)}) collective-permute-start(bf16[256,256]{1,0:T(8,128)(2,1)S(1)} %get-tuple-element.699), channel_id=1, source_target_pairs={{128,0},{160,32},{129,1},{161,33},{130,2},{162,34},{131,3},{163,35... | collective-permute-start | bytes 393224 | tf_op jit(solution)/shard_map/while/body/eval_jaxpr/cond/branch_5_fun/ppermute | solution.py:332
  40.5 5.3 %collective-permute-start.40 = (bf16[256,256]{1,0:T(8,128)(2,1)}, bf16[256,256]{1,0:T(8,128)(2,1)S(1)}, u32[]{:S(2)}, u32[]{:S(2)}) collective-permute-start(bf16[256,256]{1,0:T(8,128)(2,1)} %get-tuple-element.700), channel_id=1, source_target_pairs={{128,192},{160,224},{129,193},{161,225},{130,194},{162,226},{131,1... | collective-permute-start | bytes 393224 | tf_op jit(solution)/shard_map/while/body/eval_jaxpr/cond/branch_5_fun/ppermute | solution.py:332
  41.2 9.3 %collective-permute-start.35 = (bf16[256,256]{1,0:T(8,128)(2,1)S(1)}, bf16[256,256]{1,0:T(8,128)(2,1)S(1)}, u32[]{:S(2)}, u32[]{:S(2)}) collective-permute-start(bf16[256,256]{1,0:T(8,128)(2,1)S(1)} %get-tuple-element.694), channel_id=1, source_target_pairs={{128,64},{160,96},{129,65},{161,97},{130,66},{162,98},{131,67},{16... | collective-permute-start | bytes 393224 | tf_op jit(solution)/shard_map/while/body/eval_jaxpr/cond/branch_5_fun/ppermute | solution.py:332
  42.5 8.0 %collective-permute-start.36 = (bf16[256,256]{1,0:T(8,128)(2,1)S(1)}, bf16[256,256]{1,0:T(8,128)(2,1)S(1)}, u32[]{:S(2)}, u32[]{:S(2)}) collective-permute-start(bf16[256,256]{1,0:T(8,128)(2,1)S(1)} %get-tuple-element.695), channel_id=1, source_target_pairs={{128,0},{160,32},{129,1},{161,33},{130,2},{162,34},{131,3},{163,35... | collective-permute-start | bytes 393224 | tf_op jit(solution)/shard_map/while/body/eval_jaxpr/cond/branch_5_fun/ppermute | solution.py:332
  45.1 5.4 %collective-permute-start.37 = (bf16[256,256]{1,0:T(8,128)(2,1)}, bf16[256,256]{1,0:T(8,128)(2,1)S(1)}, u32[]{:S(2)}, u32[]{:S(2)}) collective-permute-start(bf16[256,256]{1,0:T(8,128)(2,1)} %get-tuple-element.696), channel_id=1, source_target_pairs={{128,192},{160,224},{129,193},{161,225},{130,194},{162,226},{131,1... | collective-permute-start | bytes 393224 | tf_op jit(solution)/shard_map/while/body/eval_jaxpr/cond/branch_5_fun/ppermute | solution.py:332
  45.9 10.6 %collective-permute-start.41 = (bf16[256,256]{1,0:T(8,128)(2,1)S(1)}, bf16[256,256]{1,0:T(8,128)(2,1)S(1)}, u32[]{:S(2)}, u32[]{:S(2)}) collective-permute-start(bf16[256,256]{1,0:T(8,128)(2,1)S(1)} %select_select_fusion.5), channel_id=1, source_target_pairs={{32,24},{33,25},{34,26},{35,27},{36,28},{37,29},{38,30},{39,31},{4... | collective-permute-start | bytes 393224 | tf_op jit(solution)/shard_map/while/body/eval_jaxpr/cond/branch_5_fun/ppermute | solution.py:345
  57.2 5.0 %copy-start.8 = (bf16[4,512,128]{2,1,0:T(8,128)(2,1)S(1)}, bf16[4,512,128]{2,1,0:T(8,128)(2,1)}, u32[]{:S(2)}) copy-start(bf16[4,512,128]{2,1,0:T(8,128)(2,1)} %get-tuple-element.1108.edge_ref) | copy-start | bytes 1572868 | tf_op jit(solution)/shard_map/while
  57.2 5.0 %copy-start.12 = (s32[1,2048]{1,0:T(1,128)S(1)}, s32[1,2048]{1,0:T(1,128)}, u32[]{:S(2)}) copy-start(s32[1,2048]{1,0:T(1,128)} %get-tuple-element.1107.node_time_ref) | copy-start | bytes 24580 | tf_op jit(solution)/shard_map/while
  57.2 21.5 %all-to-all-start = ((bf16[32,32,256]{2,1,0:T(8,128)(2,1)}), bf16[32,32,256]{2,1,0:T(8,128)(2,1)S(1)}, u32[]{:S(2)}, u32[]{:S(2)}) async-start(bf16[32,32,256]{2,1,0:T(8,128)(2,1)} %get-tuple-element.1121._), calls=%async_computation | async-start | bytes 1048576 | tf_op jit(solution)/shard_map/while/body/eval_jaxpr/all_to_all | solution.py:447
  62.2 0.7 copy-start.14
  88.6 4.0 %collective-permute-start.3 = (bf16[256,256]{1,0:T(8,128)(2,1)}, bf16[256,256]{1,0:T(8,128)(2,1)S(1)}, u32[]{:S(2)}, u32[]{:S(2)}) collective-permute-start(bf16[256,256]{1,0:T(8,128)(2,1)} %get-tuple-element.648), channel_id=1, source_target_pairs={{0,192},{32,224},{1,193},{33,225},{2,194},{34,226},{3,195},{35,227... | collective-permute-start | bytes 393224 | tf_op jit(solution)/shard_map/while/body/eval_jaxpr/cond/branch_0_fun/ppermute | solution.py:332
  89.3 4.7 %collective-permute-start.4 = (bf16[256,256]{1,0:T(8,128)(2,1)S(1)}, bf16[256,256]{1,0:T(8,128)(2,1)S(1)}, u32[]{:S(2)}, u32[]{:S(2)}) collective-permute-start(bf16[256,256]{1,0:T(8,128)(2,1)S(1)} %get-tuple-element.649), channel_id=1, source_target_pairs={{0,128},{32,160},{1,129},{33,161},{2,130},{34,162},{3,131},{35,163... | collective-permute-start | bytes 393224 | tf_op jit(solution)/shard_map/while/body/eval_jaxpr/cond/branch_0_fun/ppermute | solution.py:332
  90.0 14.7 %collective-permute-start.5 = (bf16[256,256]{1,0:T(8,128)(2,1)S(1)}, bf16[256,256]{1,0:T(8,128)(2,1)S(1)}, u32[]{:S(2)}, u32[]{:S(2)}) collective-permute-start(bf16[256,256]{1,0:T(8,128)(2,1)S(1)} %get-tuple-element.650), channel_id=1, source_target_pairs={{0,64},{32,96},{1,65},{33,97},{2,66},{34,98},{3,67},{35,99},{4,68}... | collective-permute-start | bytes 393224 | tf_op jit(solution)/shard_map/while/body/eval_jaxpr/cond/branch_0_fun/ppermute | solution.py:332
  91.3 18.1 %collective-permute-start = (bf16[256,256]{1,0:T(8,128)(2,1)}, bf16[256,256]{1,0:T(8,128)(2,1)S(1)}, u32[]{:S(2)}, u32[]{:S(2)}) collective-permute-start(bf16[256,256]{1,0:T(8,128)(2,1)} %get-tuple-element.644), channel_id=1, source_target_pairs={{0,192},{32,224},{1,193},{33,225},{2,194},{34,226},{3,195},{35,227... | collective-permute-start | bytes 393224 | tf_op jit(solution)/shard_map/while/body/eval_jaxpr/cond/branch_0_fun/ppermute | solution.py:332
  92.0 17.4 %collective-permute-start.1 = (bf16[256,256]{1,0:T(8,128)(2,1)S(1)}, bf16[256,256]{1,0:T(8,128)(2,1)S(1)}, u32[]{:S(2)}, u32[]{:S(2)}) collective-permute-start(bf16[256,256]{1,0:T(8,128)(2,1)S(1)} %get-tuple-element.645), channel_id=1, source_target_pairs={{0,128},{32,160},{1,129},{33,161},{2,130},{34,162},{3,131},{35,163... | collective-permute-start | bytes 393224 | tf_op jit(solution)/shard_map/while/body/eval_jaxpr/cond/branch_0_fun/ppermute | solution.py:332
  92.7 17.6 %collective-permute-start.2 = (bf16[256,256]{1,0:T(8,128)(2,1)S(1)}, bf16[256,256]{1,0:T(8,128)(2,1)S(1)}, u32[]{:S(2)}, u32[]{:S(2)}) collective-permute-start(bf16[256,256]{1,0:T(8,128)(2,1)S(1)} %get-tuple-element.646), channel_id=1, source_target_pairs={{0,64},{32,96},{1,65},{33,97},{2,66},{34,98},{3,67},{35,99},{4,68}... | collective-permute-start | bytes 393224 | tf_op jit(solution)/shard_map/while/body/eval_jaxpr/cond/branch_0_fun/ppermute | solution.py:332
  104.7 7.0 %collective-permute-start.6 = (bf16[256,256]{1,0:T(8,128)(2,1)S(1)}, bf16[256,256]{1,0:T(8,128)(2,1)S(1)}, u32[]{:S(2)}, u32[]{:S(2)}) collective-permute-start(bf16[256,256]{1,0:T(8,128)(2,1)S(1)} %select_select_fusion), channel_id=1, source_target_pairs={{0,56},{1,57},{2,58},{3,59},{4,60},{5,61},{6,62},{7,63},{8,48},{9,... | collective-permute-start | bytes 393224 | tf_op jit(solution)/shard_map/while/body/eval_jaxpr/cond/branch_0_fun/ppermute | solution.py:345
  112.5 4.8 %copy-start.8 = (bf16[4,512,128]{2,1,0:T(8,128)(2,1)S(1)}, bf16[4,512,128]{2,1,0:T(8,128)(2,1)}, u32[]{:S(2)}) copy-start(bf16[4,512,128]{2,1,0:T(8,128)(2,1)} %get-tuple-element.1108.edge_ref) | copy-start | bytes 1572868 | tf_op jit(solution)/shard_map/while
  112.5 4.8 %copy-start.12 = (s32[1,2048]{1,0:T(1,128)S(1)}, s32[1,2048]{1,0:T(1,128)}, u32[]{:S(2)}) copy-start(s32[1,2048]{1,0:T(1,128)} %get-tuple-element.1107.node_time_ref) | copy-start | bytes 24580 | tf_op jit(solution)/shard_map/while
  112.5 21.1 %all-to-all-start = ((bf16[32,32,256]{2,1,0:T(8,128)(2,1)}), bf16[32,32,256]{2,1,0:T(8,128)(2,1)S(1)}, u32[]{:S(2)}, u32[]{:S(2)}) async-start(bf16[32,32,256]{2,1,0:T(8,128)(2,1)} %get-tuple-element.1121._), calls=%async_computation | async-start | bytes 1048576 | tf_op jit(solution)/shard_map/while/body/eval_jaxpr/all_to_all | solution.py:447
  117.2 0.7 copy-start.14
  143.5 4.6 %collective-permute-start.52 = (bf16[256,256]{1,0:T(8,128)(2,1)S(1)}, bf16[256,256]{1,0:T(8,128)(2,1)S(1)}, u32[]{:S(2)}, u32[]{:S(2)}) collective-permute-start(bf16[256,256]{1,0:T(8,128)(2,1)S(1)} %get-tuple-element.718), channel_id=1, source_target_pairs={{192,128},{224,160},{193,129},{225,161},{194,130},{226,162},{195,1... | collective-permute-start | bytes 393224 | tf_op jit(solution)/shard_map/while/body/eval_jaxpr/cond/branch_7_fun/ppermute | solution.py:332
  144.2 8.7 %collective-permute-start.53 = (bf16[256,256]{1,0:T(8,128)(2,1)S(1)}, bf16[256,256]{1,0:T(8,128)(2,1)S(1)}, u32[]{:S(2)}, u32[]{:S(2)}) collective-permute-start(bf16[256,256]{1,0:T(8,128)(2,1)S(1)} %get-tuple-element.719), channel_id=1, source_target_pairs={{192,64},{224,96},{193,65},{225,97},{194,66},{226,98},{195,67},{22... | collective-permute-start | bytes 393224 | tf_op jit(solution)/shard_map/while/body/eval_jaxpr/cond/branch_7_fun/ppermute | solution.py:332
  145.5 7.4 %collective-permute-start.54 = (bf16[256,256]{1,0:T(8,128)(2,1)S(1)}, bf16[256,256]{1,0:T(8,128)(2,1)S(1)}, u32[]{:S(2)}, u32[]{:S(2)}) collective-permute-start(bf16[256,256]{1,0:T(8,128)(2,1)S(1)} %get-tuple-element.720), channel_id=1, source_target_pairs={{192,0},{224,32},{193,1},{225,33},{194,2},{226,34},{195,3},{227,35... | collective-permute-start | bytes 393224 | tf_op jit(solution)/shard_map/while/body/eval_jaxpr/cond/branch_7_fun/ppermute | solution.py:332
  146.2 12.3 %collective-permute-start.49 = (bf16[256,256]{1,0:T(8,128)(2,1)S(1)}, bf16[256,256]{1,0:T(8,128)(2,1)S(1)}, u32[]{:S(2)}, u32[]{:S(2)}) collective-permute-start(bf16[256,256]{1,0:T(8,128)(2,1)S(1)} %get-tuple-element.714), channel_id=1, source_target_pairs={{192,128},{224,160},{193,129},{225,161},{194,130},{226,162},{195,1... | collective-permute-start | bytes 393224 | tf_op jit(solution)/shard_map/while/body/eval_jaxpr/cond/branch_7_fun/ppermute | solution.py:332
  146.9 11.7 %collective-permute-start.50 = (bf16[256,256]{1,0:T(8,128)(2,1)S(1)}, bf16[256,256]{1,0:T(8,128)(2,1)S(1)}, u32[]{:S(2)}, u32[]{:S(2)}) collective-permute-start(bf16[256,256]{1,0:T(8,128)(2,1)S(1)} %get-tuple-element.715), channel_id=1, source_target_pairs={{192,64},{224,96},{193,65},{225,97},{194,66},{226,98},{195,67},{22... | collective-permute-start | bytes 393224 | tf_op jit(solution)/shard_map/while/body/eval_jaxpr/cond/branch_7_fun/ppermute | solution.py:332
  148.2 10.4 %collective-permute-start.51 = (bf16[256,256]{1,0:T(8,128)(2,1)S(1)}, bf16[256,256]{1,0:T(8,128)(2,1)S(1)}, u32[]{:S(2)}, u32[]{:S(2)}) collective-permute-start(bf16[256,256]{1,0:T(8,128)(2,1)S(1)} %get-tuple-element.716), channel_id=1, source_target_pairs={{192,0},{224,32},{193,1},{225,33},{194,2},{226,34},{195,3},{227,35... | collective-permute-start | bytes 393224 | tf_op jit(solution)/shard_map/while/body/eval_jaxpr/cond/branch_7_fun/ppermute | solution.py:332
  153.9 10.2 %collective-permute-start.55 = (bf16[256,256]{1,0:T(8,128)(2,1)S(1)}, bf16[256,256]{1,0:T(8,128)(2,1)S(1)}, u32[]{:S(2)}, u32[]{:S(2)}) collective-permute-start(bf16[256,256]{1,0:T(8,128)(2,1)S(1)} %select_select_fusion.7), channel_id=1, source_target_pairs={{32,24},{33,25},{34,26},{35,27},{36,28},{37,29},{38,30},{39,31},{4... | collective-permute-start | bytes 393224 | tf_op jit(solution)/shard_map/while/body/eval_jaxpr/cond/branch_7_fun/ppermute | solution.py:345
  165.8 5.9 %copy-start.8 = (bf16[4,512,128]{2,1,0:T(8,128)(2,1)S(1)}, bf16[4,512,128]{2,1,0:T(8,128)(2,1)}, u32[]{:S(2)}) copy-start(bf16[4,512,128]{2,1,0:T(8,128)(2,1)} %get-tuple-element.1108.edge_ref) | copy-start | bytes 1572868 | tf_op jit(solution)/shard_map/while
  165.8 5.9 %copy-start.12 = (s32[1,2048]{1,0:T(1,128)S(1)}, s32[1,2048]{1,0:T(1,128)}, u32[]{:S(2)}) copy-start(s32[1,2048]{1,0:T(1,128)} %get-tuple-element.1107.node_time_ref) | copy-start | bytes 24580 | tf_op jit(solution)/shard_map/while
  165.8 22.2 %all-to-all-start = ((bf16[32,32,256]{2,1,0:T(8,128)(2,1)}), bf16[32,32,256]{2,1,0:T(8,128)(2,1)S(1)}, u32[]{:S(2)}, u32[]{:S(2)}) async-start(bf16[32,32,256]{2,1,0:T(8,128)(2,1)} %get-tuple-element.1121._), calls=%async_computation | async-start | bytes 1048576 | tf_op jit(solution)/shard_map/while/body/eval_jaxpr/all_to_all | solution.py:447
  171.7 0.7 copy-start.14
  198.0 4.6 %collective-permute-start.52 = (bf16[256,256]{1,0:T(8,128)(2,1)S(1)}, bf16[256,256]{1,0:T(8,128)(2,1)S(1)}, u32[]{:S(2)}, u32[]{:S(2)}) collective-permute-start(bf16[256,256]{1,0:T(8,128)(2,1)S(1)} %get-tuple-element.718), channel_id=1, source_target_pairs={{192,128},{224,160},{193,129},{225,161},{194,130},{226,162},{195,1... | collective-permute-start | bytes 393224 | tf_op jit(solution)/shard_map/while/body/eval_jaxpr/cond/branch_7_fun/ppermute | solution.py:332
  198.7 8.7 %collective-permute-start.53 = (bf16[256,256]{1,0:T(8,128)(2,1)S(1)}, bf16[256,256]{1,0:T(8,128)(2,1)S(1)}, u32[]{:S(2)}, u32[]{:S(2)}) collective-permute-start(bf16[256,256]{1,0:T(8,128)(2,1)S(1)} %get-tuple-element.719), channel_id=1, source_target_pairs={{192,64},{224,96},{193,65},{225,97},{194,66},{226,98},{195,67},{22... | collective-permute-start | bytes 393224 | tf_op jit(solution)/shard_map/while/body/eval_jaxpr/cond/branch_7_fun/ppermute | solution.py:332
  200.0 7.4 %collective-permute-start.54 = (bf16[256,256]{1,0:T(8,128)(2,1)S(1)}, bf16[256,256]{1,0:T(8,128)(2,1)S(1)}, u32[]{:S(2)}, u32[]{:S(2)}) collective-permute-start(bf16[256,256]{1,0:T(8,128)(2,1)S(1)} %get-tuple-element.720), channel_id=1, source_target_pairs={{192,0},{224,32},{193,1},{225,33},{194,2},{226,34},{195,3},{227,35... | collective-permute-start | bytes 393224 | tf_op jit(solution)/shard_map/while/body/eval_jaxpr/cond/branch_7_fun/ppermute | solution.py:332
  200.7 12.3 %collective-permute-start.49 = (bf16[256,256]{1,0:T(8,128)(2,1)S(1)}, bf16[256,256]{1,0:T(8,128)(2,1)S(1)}, u32[]{:S(2)}, u32[]{:S(2)}) collective-permute-start(bf16[256,256]{1,0:T(8,128)(2,1)S(1)} %get-tuple-element.714), channel_id=1, source_target_pairs={{192,128},{224,160},{193,129},{225,161},{194,130},{226,162},{195,1... | collective-permute-start | bytes 393224 | tf_op jit(solution)/shard_map/while/body/eval_jaxpr/cond/branch_7_fun/ppermute | solution.py:332
  201.4 11.7 %collective-permute-start.50 = (bf16[256,256]{1,0:T(8,128)(2,1)S(1)}, bf16[256,256]{1,0:T(8,128)(2,1)S(1)}, u32[]{:S(2)}, u32[]{:S(2)}) collective-permute-start(bf16[256,256]{1,0:T(8,128)(2,1)S(1)} %get-tuple-element.715), channel_id=1, source_target_pairs={{192,64},{224,96},{193,65},{225,97},{194,66},{226,98},{195,67},{22... | collective-permute-start | bytes 393224 | tf_op jit(solution)/shard_map/while/body/eval_jaxpr/cond/branch_7_fun/ppermute | solution.py:332
  202.7 10.4 %collective-permute-start.51 = (bf16[256,256]{1,0:T(8,128)(2,1)S(1)}, bf16[256,256]{1,0:T(8,128)(2,1)S(1)}, u32[]{:S(2)}, u32[]{:S(2)}) collective-permute-start(bf16[256,256]{1,0:T(8,128)(2,1)S(1)} %get-tuple-element.716), channel_id=1, source_target_pairs={{192,0},{224,32},{193,1},{225,33},{194,2},{226,34},{195,3},{227,35... | collective-permute-start | bytes 393224 | tf_op jit(solution)/shard_map/while/body/eval_jaxpr/cond/branch_7_fun/ppermute | solution.py:332
  208.3 10.2 %collective-permute-start.55 = (bf16[256,256]{1,0:T(8,128)(2,1)S(1)}, bf16[256,256]{1,0:T(8,128)(2,1)S(1)}, u32[]{:S(2)}, u32[]{:S(2)}) collective-permute-start(bf16[256,256]{1,0:T(8,128)(2,1)S(1)} %select_select_fusion.7), channel_id=1, source_target_pairs={{32,24},{33,25},{34,26},{35,27},{36,28},{37,29},{38,30},{39,31},{4... | collective-permute-start | bytes 393224 | tf_op jit(solution)/shard_map/while/body/eval_jaxpr/cond/branch_7_fun/ppermute | solution.py:345
  220.2 5.8 %copy-start.8 = (bf16[4,512,128]{2,1,0:T(8,128)(2,1)S(1)}, bf16[4,512,128]{2,1,0:T(8,128)(2,1)}, u32[]{:S(2)}) copy-start(bf16[4,512,128]{2,1,0:T(8,128)(2,1)} %get-tuple-element.1108.edge_ref) | copy-start | bytes 1572868 | tf_op jit(solution)/shard_map/while
  220.2 5.8 %copy-start.12 = (s32[1,2048]{1,0:T(1,128)S(1)}, s32[1,2048]{1,0:T(1,128)}, u32[]{:S(2)}) copy-start(s32[1,2048]{1,0:T(1,128)} %get-tuple-element.1107.node_time_ref) | copy-start | bytes 24580 | tf_op jit(solution)/shard_map/while
  220.2 22.1 %all-to-all-start = ((bf16[32,32,256]{2,1,0:T(8,128)(2,1)}), bf16[32,32,256]{2,1,0:T(8,128)(2,1)S(1)}, u32[]{:S(2)}, u32[]{:S(2)}) async-start(bf16[32,32,256]{2,1,0:T(8,128)(2,1)} %get-tuple-element.1121._), calls=%async_computation | async-start | bytes 1048576 | tf_op jit(solution)/shard_map/while/body/eval_jaxpr/all_to_all | solution.py:447
  226.0 0.7 copy-start.14
  (18 other events, 12.5 us)

commit v4 on v3

--- a/solution.py
+++ b/solution.py
@@ -72,7 +72,7 @@
         kept[...] = given[...]
 
 
-def plan_kernel(cap, ocap, node_dev, flip_ref, source_ref, ids_ref, pcode_ref):
+def plan_kernel(cap, ocap, node_dev, turn, owner_ref, me_ref, source_ref, ids_ref, pcode_ref):
     batches, events = source_ref.shape
     rows = ids_ref.shape[1]
     per = cap + ocap
@@ -102,7 +102,8 @@
         spot = (slot + b * per == lane_iota).astype(F32)
         high = high + dot_nt(both, (spot * (offset >> 6).astype(F32)).astype(BF16))
         low = low + dot_nt(both, (spot * (offset & 63).astype(F32)).astype(BF16))
-        places.append(jnp.where(far, dest ^ flip_ref[b], dest) * per + slot)
+        flip = jnp.where(((owner_ref[b] ^ me_ref[0]) & 1) == 0, 0, turn)
+        places.append(jnp.where(far, dest ^ flip, dest) * per + slot)
     ids = high.astype(I32) * 64 + low.astype(I32)
     for g in range(ids_ref.shape[0]):
         ids_ref[g] = ids
@@ -385,7 +386,6 @@
     shape = jax.ShapeDtypeStruct
     me = lax.axis_index("dom").astype(I32)
     turn = rows - rows // 4
-    flip = jnp.where((owner_group & 1) == (me & 1), 0, turn).astype(I32)
     row_vectors = (
         node_time.reshape(1, node_dev),
         frequency.reshape(1, -1),
@@ -395,14 +395,14 @@
     hidden_row = bias_hidden.reshape(1, -1)
     anywhere = pl.BlockSpec(memory_space=pl.ANY)
     ids, pcode = call(
-        functools.partial(plan_kernel, cap, ocap, node_dev),
+        functools.partial(plan_kernel, cap, ocap, node_dev, turn),
         (
             shape((groups, rows, batches * per), I32),
             shape((batches, events, LANES), BF16),
         ),
         (source,),
         name="plan",
-        scalars=(flip,),
+        scalars=(owner_group, me.reshape(1)),
     )
     given = (memory,) + row_vectors
     table, times_row, freq_row, phase_row = call(
@@ -434,13 +434,13 @@
     )
 
     def batch(b, carry):
-        table, own_code, *far_rows = carry
+        owners, table, own_code, *far_rows = carry
         at = jnp.stack([b, me])
         sent = collect(
             table,
             own_code,
             far_rows,
-            lax.dynamic_index_in_dim(owner_group, b, 0, keepdims=False),
+            owners[0],
             turn,
             rows,
         )
@@ -485,9 +485,10 @@
             scalars=(at,),
             aliases={1: 0},
         )
-        return (result[0], next_own) + tuple(result[1:])
-
-    return lax.fori_loop(0, batches, batch, (table, own_code, *far_rows))[0]
+        return (owners[1:] + owners[:1], result[0], next_own) + tuple(result[1:])
+
+    owners = tuple(owner_group[b] for b in range(batches))
+    return lax.fori_loop(0, batches, batch, (owners, table, own_code, *far_rows))[1]
 
 
 def solution(mesh):

time: 250 us -> 253 us (1.012)
  waiting for transfers between devices: 92 us -> 72.8 us
  loops' own time: 2.93 us -> 19.4 us
  starting transfers between devices: 63.2 us -> 72 us
    another operation x1, loops' own time: 2.43 us -> 18.9 us  [shards(): lax.fori_loop(0, batches, batch, (owners, table, own_code, *far_rows))[1]]
    ppermute x24, waiting for transfers between devices: 22 us -> 12.9 us  [spread(): block = lax.ppermute(far_rows[2 * there + which], 'dom', pairs)]
    all_to_all x4, waiting for transfers between devices: 43.6 us -> 36.3 us  [batch(): lax.all_to_all(sent, 'row', 0, 0, tiled=True).reshape(rows * per, width)]
    ppermute x24, starting transfers between devices: 21 us -> 28.1 us  [spread(): block = lax.ppermute(far_rows[2 * there + which], 'dom', pairs)]
    ppermute x4, waiting for transfers between devices: 18.3 us -> 15.5 us  [body(): lax.ppermute(spread(1 - z), ('dom', 'row'), [((2 * i + z) * rows + r, (2...]
  transfers between devices with their start and end apart: 33 -> 33, of which waited for: 15 -> 12; matrix products, arithmetic and copies ran while one was open for 1% -> 1% of each run, Pallas kernels for 13% -> 13%
where the time goes in v4:
time: 253 us; the launch traced here: 251 us
  Pallas kernels  75 us (30%)
  waiting for transfers between devices  72.8 us (29%)
  starting transfers between devices  72 us (28%)
  loops' own time  19.4 us (8%)
  local copies, waits for them, and re-layouts  6.7 us (3%)
  other arithmetic  5.42 us (2%)
    pallas_call x16, Pallas kernels, call(): pl.pallas_call(kernel, out_shape=out_shape, grid_spec=pltpu.PrefetchScala...  75 us
    all_to_all x4, waiting for transfers between devices, batch(): lax.all_to_all(sent, 'row', 0, 0, tiled=True).reshape(rows * per, width)  36.3 us
    ppermute x24, starting transfers between devices, spread(): block = lax.ppermute(far_rows[2 * there + which], 'dom', pairs)  28.1 us
    all_to_all x4, starting transfers between devices, batch(): lax.all_to_all(sent, 'row', 0, 0, tiled=True).reshape(rows * per, width)  22.1 us
    another operation x1, loops' own time, shards(): lax.fori_loop(0, batches, batch, (owners, table, own_code, *far_rows))[1]  18.9 us
    all_to_all x1, starting transfers between devices, shards(): lax.all_to_all(ids.reshape(groups * rows, 1, batches * per), ('dom', 'row...  15.9 us
    ppermute x4, waiting for transfers between devices, body(): lax.ppermute(spread(1 - z), ('dom', 'row'), [((2 * i + z) * rows + r, (2...  15.5 us
    ppermute x24, waiting for transfers between devices, spread(): block = lax.ppermute(far_rows[2 * there + which], 'dom', pairs)  12.9 us
  transfers between devices with their start and end apart: 33, of which 12 were waited for; matrix products, arithmetic and copies ran while one was open for 1% of the time, Pallas kernels for 13%

profile of v4, /device:TPU:9, one launch (start us, length us, event | category | flops | bytes accessed | tf_op | source)
XLA Modules:
  0.0 251.4 jit_solution(12881855789895913014)
XLA Ops:
  2.0 3.1 %plan.1 = (s32[8,32,128]{2,1,0:T(8,128)}, bf16[4,512,128]{2,1,0:T(8,128)(2,1)}) custom-call(s32[4]{0:T(128)S(1)} %copy-done, s32[1]{0:T(128)} %bitcast.23.me_ref, s32[4,512]{1,0:T(4,128)S(1)} %copy-done.1), custom_call_target="tpu_custom_call" | custom-call | bytes 663552 | tf_op jit(solution)/shard_map/plan/pallas_call | solution.py:26
  5.1 15.9 %all-to-all-start.1 = ((s32[256,1,128]{2,1,0:T(1,128)}), s32[256,1,128]{2,1,0:T(1,128)}, u32[]{:S(2)}, u32[]{:S(2)}) async-start(s32[256,1,128]{2,1,0:T(1,128)} %bitcast.28), calls=%async_computation.1 | async-start | bytes 262144 | tf_op jit(solution)/shard_map/all_to_all | solution.py:416
  24.1 8.2 %all-to-all-done.1 = s32[256,1,128]{2,1,0:T(1,128)} async-done(((s32[256,1,128]{2,1,0:T(1,128)}), s32[256,1,128]{2,1,0:T(1,128)}, u32[]{:S(2)}, u32[]{:S(2)}) %all-to-all-start.1) | async-done | bytes 131104 | tf_op jit(solution)/shard_map/all_to_all | solution.py:416
  32.2 2.7 %codes.1 = (bf16[1024,128]{1,0:T(8,128)(2,1)}, bf16[2048,128]{1,0:T(8,128)(2,1)S(1)}) custom-call(s32[2]{0:T(128)S(1)} %pad_add_fusion.1.at_ref, s32[8,32,128]{2,1,0:T(8,128)} %bitcast.29.asked_ref), custom_call_target="tpu_custom_call" | custom-call | flops 2000000000 | bytes 917504 | tf_op jit(solution)/shard_map/codes/pallas_call | solution.py:26
  34.9 3.0 %serve.17 = (bf16[256,256]{1,0:T(8,128)(2,1)S(1)}, bf16[256,256]{1,0:T(8,128)(2,1)S(1)}, bf16[256,256]{1,0:T(8,128)(2,1)S(1)}, bf16[256,256]{1,0:T(8,128)(2,1)S(...) custom-call(bf16[2048,256]{1,0:T(8,128)(2,1)S(1)} %copy-done.3, ...), custom_call_target="tpu_custom_call" | custom-call | flops 4000000000 | bytes 2621440 | tf_op jit(solution)/shard_map/serve/pallas_call | solution.py:26
  37.9 213.4 %while.47 = (s32[]{:T(128)}, s32[]{:T(128)}, s32[]{:T(128)}, s32[]{:T(128)}, s32[]{:T(128)}, /*index=5*/bf16[2048,256]{1,0:T(8,128)(2,1)}, bf16[1024,128]{1,0:T(...) while((s32[]{:T(128)}, s32[]{:T(128)}, s32[]{:T(128)}, ...), condition=%wide.region_9.10_spmd, body=%wide.region_0.9_spmd.sunk | while | flops 13000458240 | bytes 23464468 | solution.py:491
  38.6 17.6 %conditional.2 = (bf16[32,32,256]{2,1,0:T(8,128)(2,1)}) conditional(s32[]{:T(128)} %clamp.8, (bf16[2048,256]{1,0:T(8,128)(2,1)}, bf16[1024,128]{1,0:T(8,128)(2,1)}, bf16[256,256]{1,0:T(8,128)(2,1)}, bf16[256,256]{1,0:T(8,128)(2,1)S(1)}, bf16[256,256]{1,0:T(8,128)(2,1)S(1)}, /*index=5*/bf16[256,256]{1,0:T(8,128)(2,1)S(1)}, ...), branch_computations={%region_1.1_spmd, %region_2.0_spmd, %region_3.3_spmd, %region_4.0_... | conditional | flops 2000458752 | bytes 6947203 | solution.py:360
  40.0 1.3 collective-permute-start.5
  42.7 1.3 collective-permute-start.2
  44.0 5.8 %collective-permute-done.5 = bf16[256,256]{1,0:T(8,128)(2,1)S(1)} collective-permute-done((bf16[256,256]{1,0:T(8,128)(2,1)S(1)}, bf16[256,256]{1,0:T(8,128)(2,1)S(1)}, u32[]{:S(2)}, u32[]{:S(2)}) %collective-permute-start.5) | collective-permute-done | bytes 131104 | tf_op jit(solution)/shard_map/while/body/eval_jaxpr/cond/branch_0_fun/ppermute | solution.py:333
  49.8 1.9 collective-permute-start.6
  51.8 3.3 %serve.9 = bf16[1024,256]{1,0:T(8,128)(2,1)} custom-call(bf16[2048,256]{1,0:T(8,128)(2,1)} %get-tuple-element.684.table_ref, bf16[1024,128]{1,0:T(8,128)(2,1)} %get-tuple-element.685.own_code_ref), custom_call_target="tpu_custom_call" | custom-call | flops 2000000000 | bytes 1835008 | tf_op jit(solution)/shard_map/while/body/eval_jaxpr/cond/branch_0_fun/serve/pallas_call | solution.py:26
  56.2 7.0 %all-to-all-start = ((bf16[32,32,256]{2,1,0:T(8,128)(2,1)}), bf16[32,32,256]{2,1,0:T(8,128)(2,1)S(1)}, u32[]{:S(2)}, u32[]{:S(2)}) async-start(bf16[32,32,256]{2,1,0:T(8,128)(2,1)} %get-tuple-element.1203._), calls=%async_computation | async-start | bytes 1048576 | tf_op jit(solution)/shard_map/while/body/eval_jaxpr/all_to_all | solution.py:447
  65.8 4.7 %prep.5 = (f32[512,512]{1,0:T(8,128)S(1)}, bf16[128,512]{1,0:T(8,128)(2,1)S(1)}, bf16[512,512]{1,0:T(8,128)(2,1)S(1)}, bf16[1024,128]{1,0:T(8,128)(2,1)}, bf16[2048,128]{1,0:T(8,128)(2,1)S(1)}) custom-call(s32[2]{0:T(128)S(1)} %pad_add_fusion.3.at_ref, bf16[2048,256]{1,0:T(8,128)(2,1)} %get-tuple-element.1144.table_ref, s32[4,512]{1,0:T(4,128)S(1)} %copy-done.10, ...), custom_call_target="tpu_custom_call" | custom-call | flops 5000000000 | bytes 5137408 | tf_op jit(solution)/shard_map/while/body/eval_jaxpr/prep/pallas_call | solution.py:26
  70.5 9.1 %all-to-all-done = bf16[32,32,256]{2,1,0:T(8,128)(2,1)S(1)} async-done(((bf16[32,32,256]{2,1,0:T(8,128)(2,1)}), bf16[32,32,256]{2,1,0:T(8,128)(2,1)S(1)}, u32[]{:S(2)}, u32[]{:S(2)}) %all-to-all-start) | async-done | bytes 524320 | tf_op jit(solution)/shard_map/while/body/eval_jaxpr/all_to_all | solution.py:447
  79.6 8.8 %update.5 = (bf16[2048,256]{1,0:T(8,128)(2,1)}, bf16[256,256]{1,0:T(8,128)(2,1)S(1)}, bf16[256,256]{1,0:T(8,128)(2,1)S(1)}, bf16[256,256]{1,0:T(8,128)(2,1)S(1)}...) custom-call(s32[2]{0:T(128)S(1)} %pad_add_fusion.3.at_ref, ...), custom_call_target="tpu_custom_call", output_to_operand_aliasing={{0}: (1, {})} | custom-call | flops 6000000000 | bytes 7608320 | tf_op jit(solution)/shard_map/while/body/eval_jaxpr/update/pallas_call | solution.py:26
  91.2 23.9 %conditional.2 = (bf16[32,32,256]{2,1,0:T(8,128)(2,1)}) conditional(s32[]{:T(128)} %clamp.8, (bf16[2048,256]{1,0:T(8,128)(2,1)}, bf16[1024,128]{1,0:T(8,128)(2,1)}, bf16[256,256]{1,0:T(8,128)(2,1)}, bf16[256,256]{1,0:T(8,128)(2,1)S(1)}, bf16[256,256]{1,0:T(8,128)(2,1)S(1)}, /*index=5*/bf16[256,256]{1,0:T(8,128)(2,1)S(1)}, ...), branch_computations={%region_1.1_spmd, %region_2.0_spmd, %region_3.3_spmd, %region_4.0_... | conditional | flops 2000458752 | bytes 6947203 | solution.py:360
  96.6 4.1 %collective-permute-done.53 = bf16[256,256]{1,0:T(8,128)(2,1)S(1)} collective-permute-done((bf16[256,256]{1,0:T(8,128)(2,1)S(1)}, bf16[256,256]{1,0:T(8,128)(2,1)S(1)}, u32[]{:S(2)}, u32[]{:S(2)}) %collective-permute-start.53) | collective-permute-done | bytes 131104 | tf_op jit(solution)/shard_map/while/body/eval_jaxpr/cond/branch_7_fun/ppermute | solution.py:333
  103.0 3.3 %serve.16 = bf16[1024,256]{1,0:T(8,128)(2,1)} custom-call(bf16[2048,256]{1,0:T(8,128)(2,1)} %get-tuple-element.754.table_ref, bf16[1024,128]{1,0:T(8,128)(2,1)} %get-tuple-element.755.own_code_ref), custom_call_target="tpu_custom_call" | custom-call | flops 2000000000 | bytes 1835008 | tf_op jit(solution)/shard_map/while/body/eval_jaxpr/cond/branch_7_fun/serve/pallas_call | solution.py:26
  106.3 7.2 %collective-permute-done.55 = bf16[256,256]{1,0:T(8,128)(2,1)S(1)} collective-permute-done((bf16[256,256]{1,0:T(8,128)(2,1)S(1)}, bf16[256,256]{1,0:T(8,128)(2,1)S(1)}, u32[]{:S(2)}, u32[]{:S(2)}) %collective-permute-start.55) | collective-permute-done | bytes 131104 | tf_op jit(solution)/shard_map/while/body/eval_jaxpr/cond/branch_7_fun/ppermute | solution.py:346
  113.5 1.7 bitcast_dynamic-update-slice_fusion.7
  115.2 5.1 %all-to-all-start = ((bf16[32,32,256]{2,1,0:T(8,128)(2,1)}), bf16[32,32,256]{2,1,0:T(8,128)(2,1)S(1)}, u32[]{:S(2)}, u32[]{:S(2)}) async-start(bf16[32,32,256]{2,1,0:T(8,128)(2,1)} %get-tuple-element.1203._), calls=%async_computation | async-start | bytes 1048576 | tf_op jit(solution)/shard_map/while/body/eval_jaxpr/all_to_all | solution.py:447
  122.9 4.7 %prep.5 = (f32[512,512]{1,0:T(8,128)S(1)}, bf16[128,512]{1,0:T(8,128)(2,1)S(1)}, bf16[512,512]{1,0:T(8,128)(2,1)S(1)}, bf16[1024,128]{1,0:T(8,128)(2,1)}, bf16[2048,128]{1,0:T(8,128)(2,1)S(1)}) custom-call(s32[2]{0:T(128)S(1)} %pad_add_fusion.3.at_ref, bf16[2048,256]{1,0:T(8,128)(2,1)} %get-tuple-element.1144.table_ref, s32[4,512]{1,0:T(4,128)S(1)} %copy-done.10, ...), custom_call_target="tpu_custom_call" | custom-call | flops 5000000000 | bytes 5137408 | tf_op jit(solution)/shard_map/while/body/eval_jaxpr/prep/pallas_call | solution.py:26
  127.7 9.1 %all-to-all-done = bf16[32,32,256]{2,1,0:T(8,128)(2,1)S(1)} async-done(((bf16[32,32,256]{2,1,0:T(8,128)(2,1)}), bf16[32,32,256]{2,1,0:T(8,128)(2,1)S(1)}, u32[]{:S(2)}, u32[]{:S(2)}) %all-to-all-start) | async-done | bytes 524320 | tf_op jit(solution)/shard_map/while/body/eval_jaxpr/all_to_all | solution.py:447
  136.7 8.8 %update.5 = (bf16[2048,256]{1,0:T(8,128)(2,1)}, bf16[256,256]{1,0:T(8,128)(2,1)S(1)}, bf16[256,256]{1,0:T(8,128)(2,1)S(1)}, bf16[256,256]{1,0:T(8,128)(2,1)S(1)}...) custom-call(s32[2]{0:T(128)S(1)} %pad_add_fusion.3.at_ref, ...), custom_call_target="tpu_custom_call", output_to_operand_aliasing={{0}: (1, {})} | custom-call | flops 6000000000 | bytes 7608320 | tf_op jit(solution)/shard_map/while/body/eval_jaxpr/update/pallas_call | solution.py:26
  148.4 19.2 %conditional.2 = (bf16[32,32,256]{2,1,0:T(8,128)(2,1)}) conditional(s32[]{:T(128)} %clamp.8, (bf16[2048,256]{1,0:T(8,128)(2,1)}, bf16[1024,128]{1,0:T(8,128)(2,1)}, bf16[256,256]{1,0:T(8,128)(2,1)}, bf16[256,256]{1,0:T(8,128)(2,1)S(1)}, bf16[256,256]{1,0:T(8,128)(2,1)S(1)}, /*index=5*/bf16[256,256]{1,0:T(8,128)(2,1)S(1)}, ...), branch_computations={%region_1.1_spmd, %region_2.0_spmd, %region_3.3_spmd, %region_4.0_... | conditional | flops 2000458752 | bytes 6947203 | solution.py:360
  151.1 1.3 collective-permute-start.35
  153.1 2.6 %collective-permute-done.38 = bf16[256,256]{1,0:T(8,128)(2,1)S(1)} collective-permute-done((bf16[256,256]{1,0:T(8,128)(2,1)S(1)}, bf16[256,256]{1,0:T(8,128)(2,1)S(1)}, u32[]{:S(2)}, u32[]{:S(2)}) %collective-permute-start.38) | collective-permute-done | bytes 131104 | tf_op jit(solution)/shard_map/while/body/eval_jaxpr/cond/branch_5_fun/ppermute | solution.py:333
  157.7 3.3 %serve.14 = bf16[1024,256]{1,0:T(8,128)(2,1)} custom-call(bf16[2048,256]{1,0:T(8,128)(2,1)} %get-tuple-element.734.table_ref, bf16[1024,128]{1,0:T(8,128)(2,1)} %get-tuple-element.735.own_code_ref), custom_call_target="tpu_custom_call" | custom-call | flops 2000000000 | bytes 1835008 | tf_op jit(solution)/shard_map/while/body/eval_jaxpr/cond/branch_5_fun/serve/pallas_call | solution.py:26
  161.0 5.8 %collective-permute-done.41 = bf16[256,256]{1,0:T(8,128)(2,1)S(1)} collective-permute-done((bf16[256,256]{1,0:T(8,128)(2,1)S(1)}, bf16[256,256]{1,0:T(8,128)(2,1)S(1)}, u32[]{:S(2)}, u32[]{:S(2)}) %collective-permute-start.41) | collective-permute-done | bytes 131104 | tf_op jit(solution)/shard_map/while/body/eval_jaxpr/cond/branch_5_fun/ppermute | solution.py:346
  167.6 5.3 %all-to-all-start = ((bf16[32,32,256]{2,1,0:T(8,128)(2,1)}), bf16[32,32,256]{2,1,0:T(8,128)(2,1)S(1)}, u32[]{:S(2)}, u32[]{:S(2)}) async-start(bf16[32,32,256]{2,1,0:T(8,128)(2,1)} %get-tuple-element.1203._), calls=%async_computation | async-start | bytes 1048576 | tf_op jit(solution)/shard_map/while/body/eval_jaxpr/all_to_all | solution.py:447
  175.5 4.7 %prep.5 = (f32[512,512]{1,0:T(8,128)S(1)}, bf16[128,512]{1,0:T(8,128)(2,1)S(1)}, bf16[512,512]{1,0:T(8,128)(2,1)S(1)}, bf16[1024,128]{1,0:T(8,128)(2,1)}, bf16[2048,128]{1,0:T(8,128)(2,1)S(1)}) custom-call(s32[2]{0:T(128)S(1)} %pad_add_fusion.3.at_ref, bf16[2048,256]{1,0:T(8,128)(2,1)} %get-tuple-element.1144.table_ref, s32[4,512]{1,0:T(4,128)S(1)} %copy-done.10, ...), custom_call_target="tpu_custom_call" | custom-call | flops 5000000000 | bytes 5137408 | tf_op jit(solution)/shard_map/while/body/eval_jaxpr/prep/pallas_call | solution.py:26
  180.2 9.1 %all-to-all-done = bf16[32,32,256]{2,1,0:T(8,128)(2,1)S(1)} async-done(((bf16[32,32,256]{2,1,0:T(8,128)(2,1)}), bf16[32,32,256]{2,1,0:T(8,128)(2,1)S(1)}, u32[]{:S(2)}, u32[]{:S(2)}) %all-to-all-start) | async-done | bytes 524320 | tf_op jit(solution)/shard_map/while/body/eval_jaxpr/all_to_all | solution.py:447
  189.3 8.8 %update.5 = (bf16[2048,256]{1,0:T(8,128)(2,1)}, bf16[256,256]{1,0:T(8,128)(2,1)S(1)}, bf16[256,256]{1,0:T(8,128)(2,1)S(1)}, bf16[256,256]{1,0:T(8,128)(2,1)S(1)}...) custom-call(s32[2]{0:T(128)S(1)} %pad_add_fusion.3.at_ref, ...), custom_call_target="tpu_custom_call", output_to_operand_aliasing={{0}: (1, {})} | custom-call | flops 6000000000 | bytes 7608320 | tf_op jit(solution)/shard_map/while/body/eval_jaxpr/update/pallas_call | solution.py:26
  200.9 20.5 %conditional.2 = (bf16[32,32,256]{2,1,0:T(8,128)(2,1)}) conditional(s32[]{:T(128)} %clamp.8, (bf16[2048,256]{1,0:T(8,128)(2,1)}, bf16[1024,128]{1,0:T(8,128)(2,1)}, bf16[256,256]{1,0:T(8,128)(2,1)}, bf16[256,256]{1,0:T(8,128)(2,1)S(1)}, bf16[256,256]{1,0:T(8,128)(2,1)S(1)}, /*index=5*/bf16[256,256]{1,0:T(8,128)(2,1)S(1)}, ...), branch_computations={%region_1.1_spmd, %region_2.0_spmd, %region_3.3_spmd, %region_4.0_... | conditional | flops 2000458752 | bytes 6947203 | solution.py:360
  201.0 4.3 %collective-permute-start.17 = (bf16[256,256]{1,0:T(8,128)(2,1)S(1)}, bf16[256,256]{1,0:T(8,128)(2,1)S(1)}, u32[]{:S(2)}, u32[]{:S(2)}) collective-permute-start(bf16[256,256]{1,0:T(8,128)(2,1)S(1)} %get-tuple-element.710), channel_id=1, source_target_pairs={{64,0},{96,32},{65,1},{97,33},{66,2},{98,34},{67,3},{99,35},{68,4}... | collective-permute-start | bytes 393224 | tf_op jit(solution)/shard_map/while/body/eval_jaxpr/cond/branch_2_fun/ppermute | solution.py:333
  205.3 2.9 %collective-permute-start.18 = (bf16[256,256]{1,0:T(8,128)(2,1)}, bf16[256,256]{1,0:T(8,128)(2,1)S(1)}, u32[]{:S(2)}, u32[]{:S(2)}) collective-permute-start(bf16[256,256]{1,0:T(8,128)(2,1)} %get-tuple-element.711), channel_id=1, source_target_pairs={{64,192},{96,224},{65,193},{97,225},{66,194},{98,226},{67,195},{99... | collective-permute-start | bytes 393224 | tf_op jit(solution)/shard_map/while/body/eval_jaxpr/cond/branch_2_fun/ppermute | solution.py:333
  208.2 1.3 collective-permute-start.19
  209.5 1.3 collective-permute-start.14
  210.8 1.3 collective-permute-start.15
  212.1 1.3 collective-permute-start.16
  213.5 1.3 collective-permute-start.20
  214.8 3.3 %serve.11 = bf16[1024,256]{1,0:T(8,128)(2,1)} custom-call(bf16[2048,256]{1,0:T(8,128)(2,1)} %get-tuple-element.704.table_ref, bf16[1024,128]{1,0:T(8,128)(2,1)} %get-tuple-element.705.own_code_ref), custom_call_target="tpu_custom_call" | custom-call | flops 2000000000 | bytes 1835008 | tf_op jit(solution)/shard_map/while/body/eval_jaxpr/cond/branch_2_fun/serve/pallas_call | solution.py:26
  218.1 2.6 %collective-permute-done.20 = bf16[256,256]{1,0:T(8,128)(2,1)S(1)} collective-permute-done((bf16[256,256]{1,0:T(8,128)(2,1)S(1)}, bf16[256,256]{1,0:T(8,128)(2,1)S(1)}, u32[]{:S(2)}, u32[]{:S(2)}) %collective-permute-start.20) | collective-permute-done | bytes 131104 | tf_op jit(solution)/shard_map/while/body/eval_jaxpr/cond/branch_2_fun/ppermute | solution.py:346
  221.5 4.8 %all-to-all-start = ((bf16[32,32,256]{2,1,0:T(8,128)(2,1)}), bf16[32,32,256]{2,1,0:T(8,128)(2,1)S(1)}, u32[]{:S(2)}, u32[]{:S(2)}) async-start(bf16[32,32,256]{2,1,0:T(8,128)(2,1)} %get-tuple-element.1203._), calls=%async_computation | async-start | bytes 1048576 | tf_op jit(solution)/shard_map/while/body/eval_jaxpr/all_to_all | solution.py:447
  228.9 4.7 %prep.5 = (f32[512,512]{1,0:T(8,128)S(1)}, bf16[128,512]{1,0:T(8,128)(2,1)S(1)}, bf16[512,512]{1,0:T(8,128)(2,1)S(1)}, bf16[1024,128]{1,0:T(8,128)(2,1)}, bf16[2048,128]{1,0:T(8,128)(2,1)S(1)}) custom-call(s32[2]{0:T(128)S(1)} %pad_add_fusion.3.at_ref, bf16[2048,256]{1,0:T(8,128)(2,1)} %get-tuple-element.1144.table_ref, s32[4,512]{1,0:T(4,128)S(1)} %copy-done.10, ...), custom_call_target="tpu_custom_call" | custom-call | flops 5000000000 | bytes 5137408 | tf_op jit(solution)/shard_map/while/body/eval_jaxpr/prep/pallas_call | solution.py:26
  233.6 9.1 %all-to-all-done = bf16[32,32,256]{2,1,0:T(8,128)(2,1)S(1)} async-done(((bf16[32,32,256]{2,1,0:T(8,128)(2,1)}), bf16[32,32,256]{2,1,0:T(8,128)(2,1)S(1)}, u32[]{:S(2)}, u32[]{:S(2)}) %all-to-all-start) | async-done | bytes 524320 | tf_op jit(solution)/shard_map/while/body/eval_jaxpr/all_to_all | solution.py:447
  242.7 6.5 %update.5 = (bf16[2048,256]{1,0:T(8,128)(2,1)}, bf16[256,256]{1,0:T(8,128)(2,1)S(1)}, bf16[256,256]{1,0:T(8,128)(2,1)S(1)}, bf16[256,256]{1,0:T(8,128)(2,1)S(1)}...) custom-call(s32[2]{0:T(128)S(1)} %pad_add_fusion.3.at_ref, ...), custom_call_target="tpu_custom_call", output_to_operand_aliasing={{0}: (1, {})} | custom-call | flops 6000000000 | bytes 7608320 | tf_op jit(solution)/shard_map/while/body/eval_jaxpr/update/pallas_call | solution.py:26
  (113 shorter events, 26.3 us)
Async XLA Ops:
  0.0 1.3 copy-start.7
  5.1 16.0 %copy-start.4 = (s32[2048]{0:T(1024)S(1)}, s32[2048]{0:T(1024)}, u32[]{:S(2)}) copy-start(s32[2048]{0:T(1024)} %param.41) | copy-start | bytes 24580
  5.1 27.1 %all-to-all-start.1 = ((s32[256,1,128]{2,1,0:T(1,128)}), s32[256,1,128]{2,1,0:T(1,128)}, u32[]{:S(2)}, u32[]{:S(2)}) async-start(s32[256,1,128]{2,1,0:T(1,128)} %bitcast.28), calls=%async_computation.1 | async-start | bytes 262144 | tf_op jit(solution)/shard_map/all_to_all | solution.py:416
  21.8 1.2 copy-start.2
  32.2 2.7 %copy-start.3 = (bf16[2048,256]{1,0:T(8,128)(2,1)S(1)}, bf16[2048,256]{1,0:T(8,128)(2,1)}, u32[]{:S(2)}) copy-start(bf16[2048,256]{1,0:T(8,128)(2,1)} %table_ref.1) | copy-start | bytes 3145732
  38.6 4.0 %collective-permute-start.3 = (bf16[256,256]{1,0:T(8,128)(2,1)}, bf16[256,256]{1,0:T(8,128)(2,1)S(1)}, u32[]{:S(2)}, u32[]{:S(2)}) collective-permute-start(bf16[256,256]{1,0:T(8,128)(2,1)} %get-tuple-element.690), channel_id=1, source_target_pairs={{0,192},{32,224},{1,193},{33,225},{2,194},{34,226},{3,195},{35,227... | collective-permute-start | bytes 393224 | tf_op jit(solution)/shard_map/while/body/eval_jaxpr/cond/branch_0_fun/ppermute | solution.py:333
  39.3 4.7 %collective-permute-start.4 = (bf16[256,256]{1,0:T(8,128)(2,1)S(1)}, bf16[256,256]{1,0:T(8,128)(2,1)S(1)}, u32[]{:S(2)}, u32[]{:S(2)}) collective-permute-start(bf16[256,256]{1,0:T(8,128)(2,1)S(1)} %get-tuple-element.691), channel_id=1, source_target_pairs={{0,128},{32,160},{1,129},{33,161},{2,130},{34,162},{3,131},{35,163... | collective-permute-start | bytes 393224 | tf_op jit(solution)/shard_map/while/body/eval_jaxpr/cond/branch_0_fun/ppermute | solution.py:333
  40.0 9.8 %collective-permute-start.5 = (bf16[256,256]{1,0:T(8,128)(2,1)S(1)}, bf16[256,256]{1,0:T(8,128)(2,1)S(1)}, u32[]{:S(2)}, u32[]{:S(2)}) collective-permute-start(bf16[256,256]{1,0:T(8,128)(2,1)S(1)} %get-tuple-element.692), channel_id=1, source_target_pairs={{0,64},{32,96},{1,65},{33,97},{2,66},{34,98},{3,67},{35,99},{4,68}... | collective-permute-start | bytes 393224 | tf_op jit(solution)/shard_map/while/body/eval_jaxpr/cond/branch_0_fun/ppermute | solution.py:333
  41.3 13.8 %collective-permute-start = (bf16[256,256]{1,0:T(8,128)(2,1)}, bf16[256,256]{1,0:T(8,128)(2,1)S(1)}, u32[]{:S(2)}, u32[]{:S(2)}) collective-permute-start(bf16[256,256]{1,0:T(8,128)(2,1)} %get-tuple-element.686), channel_id=1, source_target_pairs={{0,192},{32,224},{1,193},{33,225},{2,194},{34,226},{3,195},{35,227... | collective-permute-start | bytes 393224 | tf_op jit(solution)/shard_map/while/body/eval_jaxpr/cond/branch_0_fun/ppermute | solution.py:333
  42.0 13.1 %collective-permute-start.1 = (bf16[256,256]{1,0:T(8,128)(2,1)S(1)}, bf16[256,256]{1,0:T(8,128)(2,1)S(1)}, u32[]{:S(2)}, u32[]{:S(2)}) collective-permute-start(bf16[256,256]{1,0:T(8,128)(2,1)S(1)} %get-tuple-element.687), channel_id=1, source_target_pairs={{0,128},{32,160},{1,129},{33,161},{2,130},{34,162},{3,131},{35,163... | collective-permute-start | bytes 393224 | tf_op jit(solution)/shard_map/while/body/eval_jaxpr/cond/branch_0_fun/ppermute | solution.py:333
  42.7 12.7 %collective-permute-start.2 = (bf16[256,256]{1,0:T(8,128)(2,1)S(1)}, bf16[256,256]{1,0:T(8,128)(2,1)S(1)}, u32[]{:S(2)}, u32[]{:S(2)}) collective-permute-start(bf16[256,256]{1,0:T(8,128)(2,1)S(1)} %get-tuple-element.688), channel_id=1, source_target_pairs={{0,64},{32,96},{1,65},{33,97},{2,66},{34,98},{3,67},{35,99},{4,68}... | collective-permute-start | bytes 393224 | tf_op jit(solution)/shard_map/while/body/eval_jaxpr/cond/branch_0_fun/ppermute | solution.py:333
  49.8 5.6 %collective-permute-start.6 = (bf16[256,256]{1,0:T(8,128)(2,1)S(1)}, bf16[256,256]{1,0:T(8,128)(2,1)S(1)}, u32[]{:S(2)}, u32[]{:S(2)}) collective-permute-start(bf16[256,256]{1,0:T(8,128)(2,1)S(1)} %select_select_fusion), channel_id=1, source_target_pairs={{0,56},{1,57},{2,58},{3,59},{4,60},{5,61},{6,62},{7,63},{8,48},{9,... | collective-permute-start | bytes 393224 | tf_op jit(solution)/shard_map/while/body/eval_jaxpr/cond/branch_0_fun/ppermute | solution.py:346
  56.2 8.9 %copy-start.9 = (bf16[4,512,128]{2,1,0:T(8,128)(2,1)S(1)}, bf16[4,512,128]{2,1,0:T(8,128)(2,1)}, u32[]{:S(2)}) copy-start(bf16[4,512,128]{2,1,0:T(8,128)(2,1)} %get-tuple-element.1190.edge_ref) | copy-start | bytes 1572868 | tf_op jit(solution)/shard_map/while
  56.2 8.9 %copy-start.12 = (s32[1,2048]{1,0:T(1,128)S(1)}, s32[1,2048]{1,0:T(1,128)}, u32[]{:S(2)}) copy-start(s32[1,2048]{1,0:T(1,128)} %get-tuple-element.1189.node_time_ref) | copy-start | bytes 24580 | tf_op jit(solution)/shard_map/while
  56.2 23.4 %all-to-all-start = ((bf16[32,32,256]{2,1,0:T(8,128)(2,1)}), bf16[32,32,256]{2,1,0:T(8,128)(2,1)S(1)}, u32[]{:S(2)}, u32[]{:S(2)}) async-start(bf16[32,32,256]{2,1,0:T(8,128)(2,1)} %get-tuple-element.1203._), calls=%async_computation | async-start | bytes 1048576 | tf_op jit(solution)/shard_map/while/body/eval_jaxpr/all_to_all | solution.py:447
  65.0 0.7 copy-start.11
  91.3 4.6 %collective-permute-start.52 = (bf16[256,256]{1,0:T(8,128)(2,1)S(1)}, bf16[256,256]{1,0:T(8,128)(2,1)S(1)}, u32[]{:S(2)}, u32[]{:S(2)}) collective-permute-start(bf16[256,256]{1,0:T(8,128)(2,1)S(1)} %get-tuple-element.760), channel_id=1, source_target_pairs={{192,128},{224,160},{193,129},{225,161},{194,130},{226,162},{195,1... | collective-permute-start | bytes 393224 | tf_op jit(solution)/shard_map/while/body/eval_jaxpr/cond/branch_7_fun/ppermute | solution.py:333
  92.0 8.7 %collective-permute-start.53 = (bf16[256,256]{1,0:T(8,128)(2,1)S(1)}, bf16[256,256]{1,0:T(8,128)(2,1)S(1)}, u32[]{:S(2)}, u32[]{:S(2)}) collective-permute-start(bf16[256,256]{1,0:T(8,128)(2,1)S(1)} %get-tuple-element.761), channel_id=1, source_target_pairs={{192,64},{224,96},{193,65},{225,97},{194,66},{226,98},{195,67},{22... | collective-permute-start | bytes 393224 | tf_op jit(solution)/shard_map/while/body/eval_jaxpr/cond/branch_7_fun/ppermute | solution.py:333
  93.3 7.4 %collective-permute-start.54 = (bf16[256,256]{1,0:T(8,128)(2,1)S(1)}, bf16[256,256]{1,0:T(8,128)(2,1)S(1)}, u32[]{:S(2)}, u32[]{:S(2)}) collective-permute-start(bf16[256,256]{1,0:T(8,128)(2,1)S(1)} %get-tuple-element.762), channel_id=1, source_target_pairs={{192,0},{224,32},{193,1},{225,33},{194,2},{226,34},{195,3},{227,35... | collective-permute-start | bytes 393224 | tf_op jit(solution)/shard_map/while/body/eval_jaxpr/cond/branch_7_fun/ppermute | solution.py:333
  93.9 12.3 %collective-permute-start.49 = (bf16[256,256]{1,0:T(8,128)(2,1)S(1)}, bf16[256,256]{1,0:T(8,128)(2,1)S(1)}, u32[]{:S(2)}, u32[]{:S(2)}) collective-permute-start(bf16[256,256]{1,0:T(8,128)(2,1)S(1)} %get-tuple-element.756), channel_id=1, source_target_pairs={{192,128},{224,160},{193,129},{225,161},{194,130},{226,162},{195,1... | collective-permute-start | bytes 393224 | tf_op jit(solution)/shard_map/while/body/eval_jaxpr/cond/branch_7_fun/ppermute | solution.py:333
  94.6 11.7 %collective-permute-start.50 = (bf16[256,256]{1,0:T(8,128)(2,1)S(1)}, bf16[256,256]{1,0:T(8,128)(2,1)S(1)}, u32[]{:S(2)}, u32[]{:S(2)}) collective-permute-start(bf16[256,256]{1,0:T(8,128)(2,1)S(1)} %get-tuple-element.757), channel_id=1, source_target_pairs={{192,64},{224,96},{193,65},{225,97},{194,66},{226,98},{195,67},{22... | collective-permute-start | bytes 393224 | tf_op jit(solution)/shard_map/while/body/eval_jaxpr/cond/branch_7_fun/ppermute | solution.py:333
  95.9 10.4 %collective-permute-start.51 = (bf16[256,256]{1,0:T(8,128)(2,1)S(1)}, bf16[256,256]{1,0:T(8,128)(2,1)S(1)}, u32[]{:S(2)}, u32[]{:S(2)}) collective-permute-start(bf16[256,256]{1,0:T(8,128)(2,1)S(1)} %get-tuple-element.758), channel_id=1, source_target_pairs={{192,0},{224,32},{193,1},{225,33},{194,2},{226,34},{195,3},{227,35... | collective-permute-start | bytes 393224 | tf_op jit(solution)/shard_map/while/body/eval_jaxpr/cond/branch_7_fun/ppermute | solution.py:333
  101.7 11.8 %collective-permute-start.55 = (bf16[256,256]{1,0:T(8,128)(2,1)S(1)}, bf16[256,256]{1,0:T(8,128)(2,1)S(1)}, u32[]{:S(2)}, u32[]{:S(2)}) collective-permute-start(bf16[256,256]{1,0:T(8,128)(2,1)S(1)} %select_select_fusion.7), channel_id=1, source_target_pairs={{32,24},{33,25},{34,26},{35,27},{36,28},{37,29},{38,30},{39,31},{4... | collective-permute-start | bytes 393224 | tf_op jit(solution)/shard_map/while/body/eval_jaxpr/cond/branch_7_fun/ppermute | solution.py:346
  115.2 7.0 %copy-start.9 = (bf16[4,512,128]{2,1,0:T(8,128)(2,1)S(1)}, bf16[4,512,128]{2,1,0:T(8,128)(2,1)}, u32[]{:S(2)}) copy-start(bf16[4,512,128]{2,1,0:T(8,128)(2,1)} %get-tuple-element.1190.edge_ref) | copy-start | bytes 1572868 | tf_op jit(solution)/shard_map/while
  115.2 7.0 %copy-start.12 = (s32[1,2048]{1,0:T(1,128)S(1)}, s32[1,2048]{1,0:T(1,128)}, u32[]{:S(2)}) copy-start(s32[1,2048]{1,0:T(1,128)} %get-tuple-element.1189.node_time_ref) | copy-start | bytes 24580 | tf_op jit(solution)/shard_map/while
  115.2 21.5 %all-to-all-start = ((bf16[32,32,256]{2,1,0:T(8,128)(2,1)}), bf16[32,32,256]{2,1,0:T(8,128)(2,1)S(1)}, u32[]{:S(2)}, u32[]{:S(2)}) async-start(bf16[32,32,256]{2,1,0:T(8,128)(2,1)} %get-tuple-element.1203._), calls=%async_computation | async-start | bytes 1048576 | tf_op jit(solution)/shard_map/while/body/eval_jaxpr/all_to_all | solution.py:447
  122.1 0.7 copy-start.11
  148.4 7.2 %collective-permute-start.38 = (bf16[256,256]{1,0:T(8,128)(2,1)S(1)}, bf16[256,256]{1,0:T(8,128)(2,1)S(1)}, u32[]{:S(2)}, u32[]{:S(2)}) collective-permute-start(bf16[256,256]{1,0:T(8,128)(2,1)S(1)} %get-tuple-element.740), channel_id=1, source_target_pairs={{128,64},{160,96},{129,65},{161,97},{130,66},{162,98},{131,67},{16... | collective-permute-start | bytes 393224 | tf_op jit(solution)/shard_map/while/body/eval_jaxpr/cond/branch_5_fun/ppermute | solution.py:333
  149.7 6.6 %collective-permute-start.39 = (bf16[256,256]{1,0:T(8,128)(2,1)S(1)}, bf16[256,256]{1,0:T(8,128)(2,1)S(1)}, u32[]{:S(2)}, u32[]{:S(2)}) collective-permute-start(bf16[256,256]{1,0:T(8,128)(2,1)S(1)} %get-tuple-element.741), channel_id=1, source_target_pairs={{128,0},{160,32},{129,1},{161,33},{130,2},{162,34},{131,3},{163,35... | collective-permute-start | bytes 393224 | tf_op jit(solution)/shard_map/while/body/eval_jaxpr/cond/branch_5_fun/ppermute | solution.py:333
  150.4 5.9 %collective-permute-start.40 = (bf16[256,256]{1,0:T(8,128)(2,1)}, bf16[256,256]{1,0:T(8,128)(2,1)S(1)}, u32[]{:S(2)}, u32[]{:S(2)}) collective-permute-start(bf16[256,256]{1,0:T(8,128)(2,1)} %get-tuple-element.742), channel_id=1, source_target_pairs={{128,192},{160,224},{129,193},{161,225},{130,194},{162,226},{131,1... | collective-permute-start | bytes 393224 | tf_op jit(solution)/shard_map/while/body/eval_jaxpr/cond/branch_5_fun/ppermute | solution.py:333
  151.1 9.9 %collective-permute-start.35 = (bf16[256,256]{1,0:T(8,128)(2,1)S(1)}, bf16[256,256]{1,0:T(8,128)(2,1)S(1)}, u32[]{:S(2)}, u32[]{:S(2)}) collective-permute-start(bf16[256,256]{1,0:T(8,128)(2,1)S(1)} %get-tuple-element.736), channel_id=1, source_target_pairs={{128,64},{160,96},{129,65},{161,97},{130,66},{162,98},{131,67},{16... | collective-permute-start | bytes 393224 | tf_op jit(solution)/shard_map/while/body/eval_jaxpr/cond/branch_5_fun/ppermute | solution.py:333
  152.4 8.6 %collective-permute-start.36 = (bf16[256,256]{1,0:T(8,128)(2,1)S(1)}, bf16[256,256]{1,0:T(8,128)(2,1)S(1)}, u32[]{:S(2)}, u32[]{:S(2)}) collective-permute-start(bf16[256,256]{1,0:T(8,128)(2,1)S(1)} %get-tuple-element.737), channel_id=1, source_target_pairs={{128,0},{160,32},{129,1},{161,33},{130,2},{162,34},{131,3},{163,35... | collective-permute-start | bytes 393224 | tf_op jit(solution)/shard_map/while/body/eval_jaxpr/cond/branch_5_fun/ppermute | solution.py:333
  155.7 5.4 %collective-permute-start.37 = (bf16[256,256]{1,0:T(8,128)(2,1)}, bf16[256,256]{1,0:T(8,128)(2,1)S(1)}, u32[]{:S(2)}, u32[]{:S(2)}) collective-permute-start(bf16[256,256]{1,0:T(8,128)(2,1)} %get-tuple-element.738), channel_id=1, source_target_pairs={{128,192},{160,224},{129,193},{161,225},{130,194},{162,226},{131,1... | collective-permute-start | bytes 393224 | tf_op jit(solution)/shard_map/while/body/eval_jaxpr/cond/branch_5_fun/ppermute | solution.py:333
  156.4 10.4 %collective-permute-start.41 = (bf16[256,256]{1,0:T(8,128)(2,1)S(1)}, bf16[256,256]{1,0:T(8,128)(2,1)S(1)}, u32[]{:S(2)}, u32[]{:S(2)}) collective-permute-start(bf16[256,256]{1,0:T(8,128)(2,1)S(1)} %select_select_fusion.5), channel_id=1, source_target_pairs={{32,24},{33,25},{34,26},{35,27},{36,28},{37,29},{38,30},{39,31},{4... | collective-permute-start | bytes 393224 | tf_op jit(solution)/shard_map/while/body/eval_jaxpr/cond/branch_5_fun/ppermute | solution.py:346
  167.6 7.2 %copy-start.9 = (bf16[4,512,128]{2,1,0:T(8,128)(2,1)S(1)}, bf16[4,512,128]{2,1,0:T(8,128)(2,1)}, u32[]{:S(2)}) copy-start(bf16[4,512,128]{2,1,0:T(8,128)(2,1)} %get-tuple-element.1190.edge_ref) | copy-start | bytes 1572868 | tf_op jit(solution)/shard_map/while
  167.6 7.2 %copy-start.12 = (s32[1,2048]{1,0:T(1,128)S(1)}, s32[1,2048]{1,0:T(1,128)}, u32[]{:S(2)}) copy-start(s32[1,2048]{1,0:T(1,128)} %get-tuple-element.1189.node_time_ref) | copy-start | bytes 24580 | tf_op jit(solution)/shard_map/while
  167.6 21.7 %all-to-all-start = ((bf16[32,32,256]{2,1,0:T(8,128)(2,1)}), bf16[32,32,256]{2,1,0:T(8,128)(2,1)S(1)}, u32[]{:S(2)}, u32[]{:S(2)}) async-start(bf16[32,32,256]{2,1,0:T(8,128)(2,1)} %get-tuple-element.1203._), calls=%async_computation | async-start | bytes 1048576 | tf_op jit(solution)/shard_map/while/body/eval_jaxpr/all_to_all | solution.py:447
  174.7 0.7 copy-start.11
  201.0 11.1 %collective-permute-start.17 = (bf16[256,256]{1,0:T(8,128)(2,1)S(1)}, bf16[256,256]{1,0:T(8,128)(2,1)S(1)}, u32[]{:S(2)}, u32[]{:S(2)}) collective-permute-start(bf16[256,256]{1,0:T(8,128)(2,1)S(1)} %get-tuple-element.710), channel_id=1, source_target_pairs={{64,0},{96,32},{65,1},{97,33},{66,2},{98,34},{67,3},{99,35},{68,4}... | collective-permute-start | bytes 393224 | tf_op jit(solution)/shard_map/while/body/eval_jaxpr/cond/branch_2_fun/ppermute | solution.py:333
  205.3 8.1 %collective-permute-start.18 = (bf16[256,256]{1,0:T(8,128)(2,1)}, bf16[256,256]{1,0:T(8,128)(2,1)S(1)}, u32[]{:S(2)}, u32[]{:S(2)}) collective-permute-start(bf16[256,256]{1,0:T(8,128)(2,1)} %get-tuple-element.711), channel_id=1, source_target_pairs={{64,192},{96,224},{65,193},{97,225},{66,194},{98,226},{67,195},{99... | collective-permute-start | bytes 393224 | tf_op jit(solution)/shard_map/while/body/eval_jaxpr/cond/branch_2_fun/ppermute | solution.py:333
  208.2 5.3 %collective-permute-start.19 = (bf16[256,256]{1,0:T(8,128)(2,1)S(1)}, bf16[256,256]{1,0:T(8,128)(2,1)S(1)}, u32[]{:S(2)}, u32[]{:S(2)}) collective-permute-start(bf16[256,256]{1,0:T(8,128)(2,1)S(1)} %get-tuple-element.712), channel_id=1, source_target_pairs={{64,128},{96,160},{65,129},{97,161},{66,130},{98,162},{67,131},{99... | collective-permute-start | bytes 393224 | tf_op jit(solution)/shard_map/while/body/eval_jaxpr/cond/branch_2_fun/ppermute | solution.py:333
  209.5 8.6 %collective-permute-start.14 = (bf16[256,256]{1,0:T(8,128)(2,1)S(1)}, bf16[256,256]{1,0:T(8,128)(2,1)S(1)}, u32[]{:S(2)}, u32[]{:S(2)}) collective-permute-start(bf16[256,256]{1,0:T(8,128)(2,1)S(1)} %get-tuple-element.706), channel_id=1, source_target_pairs={{64,0},{96,32},{65,1},{97,33},{66,2},{98,34},{67,3},{99,35},{68,4}... | collective-permute-start | bytes 393224 | tf_op jit(solution)/shard_map/while/body/eval_jaxpr/cond/branch_2_fun/ppermute | solution.py:333
  210.8 7.3 %collective-permute-start.15 = (bf16[256,256]{1,0:T(8,128)(2,1)}, bf16[256,256]{1,0:T(8,128)(2,1)S(1)}, u32[]{:S(2)}, u32[]{:S(2)}) collective-permute-start(bf16[256,256]{1,0:T(8,128)(2,1)} %get-tuple-element.707), channel_id=1, source_target_pairs={{64,192},{96,224},{65,193},{97,225},{66,194},{98,226},{67,195},{99... | collective-permute-start | bytes 393224 | tf_op jit(solution)/shard_map/while/body/eval_jaxpr/cond/branch_2_fun/ppermute | solution.py:333
  212.1 6.0 %collective-permute-start.16 = (bf16[256,256]{1,0:T(8,128)(2,1)S(1)}, bf16[256,256]{1,0:T(8,128)(2,1)S(1)}, u32[]{:S(2)}, u32[]{:S(2)}) collective-permute-start(bf16[256,256]{1,0:T(8,128)(2,1)S(1)} %get-tuple-element.708), channel_id=1, source_target_pairs={{64,128},{96,160},{65,129},{97,161},{66,130},{98,162},{67,131},{99... | collective-permute-start | bytes 393224 | tf_op jit(solution)/shard_map/while/body/eval_jaxpr/cond/branch_2_fun/ppermute | solution.py:333
  213.5 7.2 %collective-permute-start.20 = (bf16[256,256]{1,0:T(8,128)(2,1)S(1)}, bf16[256,256]{1,0:T(8,128)(2,1)S(1)}, u32[]{:S(2)}, u32[]{:S(2)}) collective-permute-start(bf16[256,256]{1,0:T(8,128)(2,1)S(1)} %select_select_fusion.2), channel_id=1, source_target_pairs={{0,56},{1,57},{2,58},{3,59},{4,60},{5,61},{6,62},{7,63},{8,48},{9,... | collective-permute-start | bytes 393224 | tf_op jit(solution)/shard_map/while/body/eval_jaxpr/cond/branch_2_fun/ppermute | solution.py:346
  221.5 6.7 %copy-start.9 = (bf16[4,512,128]{2,1,0:T(8,128)(2,1)S(1)}, bf16[4,512,128]{2,1,0:T(8,128)(2,1)}, u32[]{:S(2)}) copy-start(bf16[4,512,128]{2,1,0:T(8,128)(2,1)} %get-tuple-element.1190.edge_ref) | copy-start | bytes 1572868 | tf_op jit(solution)/shard_map/while
  221.5 6.7 %copy-start.12 = (s32[1,2048]{1,0:T(1,128)S(1)}, s32[1,2048]{1,0:T(1,128)}, u32[]{:S(2)}) copy-start(s32[1,2048]{1,0:T(1,128)} %get-tuple-element.1189.node_time_ref) | copy-start | bytes 24580 | tf_op jit(solution)/shard_map/while
  221.5 21.2 %all-to-all-start = ((bf16[32,32,256]{2,1,0:T(8,128)(2,1)}), bf16[32,32,256]{2,1,0:T(8,128)(2,1)S(1)}, u32[]{:S(2)}, u32[]{:S(2)}) async-start(bf16[32,32,256]{2,1,0:T(8,128)(2,1)} %get-tuple-element.1203._), calls=%async_computation | async-start | bytes 1048576 | tf_op jit(solution)/shard_map/while/body/eval_jaxpr/all_to_all | solution.py:447
  (14 other events, 9.7 us)

commit v5 on v3

--- a/solution.py
+++ b/solution.py
@@ -326,7 +326,7 @@
             def spread(which):
                 part = far_rows[2 * y + which]
                 moved = []
-                for shift in range(1, ys):
+                for shift in sorted(range(1, ys), key=lambda k: -min(k, ys - k)):
                     there = (y + shift) % ys
                     pairs = [(2 * y + side, 2 * there + side) for side in range(2)]
                     block = lax.ppermute(far_rows[2 * there + which], "dom", pairs)

time: 250 us -> 250 us (level)
  other arithmetic: 7.26 us -> 3.65 us
    ppermute x4, waiting for transfers between devices: 18.3 us -> 13.7 us  [body(): lax.ppermute(spread(1 - z), ('dom', 'row'), [((2 * i + z) * rows + r, (2...]
    ppermute x24, waiting for transfers between devices: 22 us -> 25.9 us  [spread(): block = lax.ppermute(far_rows[2 * there + which], 'dom', pairs)]
  transfers between devices with their start and end apart: 33 -> 33, of which waited for: 15 -> 17; matrix products, arithmetic and copies ran while one was open for 1% -> 0% of each run, Pallas kernels for 13% -> 13%
where the time goes in v5:
time: 250 us; the launch traced here: 247 us
  waiting for transfers between devices  91.3 us (37%)
  Pallas kernels  74.9 us (30%)
  starting transfers between devices  65.6 us (26%)
  local copies, waits for them, and re-layouts  8.42 us (3%)
  other arithmetic  3.65 us (1%)
  loops' own time  2.92 us (1%)
    pallas_call x16, Pallas kernels, call(): pl.pallas_call(kernel, out_shape=out_shape, grid_spec=pltpu.PrefetchScala...  74.9 us
    all_to_all x4, waiting for transfers between devices, batch(): lax.all_to_all(sent, 'row', 0, 0, tiled=True).reshape(rows * per, width)  43.5 us
    ppermute x24, waiting for transfers between devices, spread(): block = lax.ppermute(far_rows[2 * there + which], 'dom', pairs)  25.9 us
    all_to_all x4, starting transfers between devices, batch(): lax.all_to_all(sent, 'row', 0, 0, tiled=True).reshape(rows * per, width)  23.4 us
    ppermute x24, starting transfers between devices, spread(): block = lax.ppermute(far_rows[2 * there + which], 'dom', pairs)  21 us
    all_to_all x1, starting transfers between devices, shards(): lax.all_to_all(ids.reshape(groups * rows, 1, batches * per), ('dom', 'row...  15.9 us
    ppermute x4, waiting for transfers between devices, body(): lax.ppermute(spread(1 - z), ('dom', 'row'), [((2 * i + z) * rows + r, (2...  13.7 us
    all_to_all x1, waiting for transfers between devices, shards(): lax.all_to_all(ids.reshape(groups * rows, 1, batches * per), ('dom', 'row...  8.14 us
  transfers between devices with their start and end apart: 33, of which 17 were waited for; matrix products, arithmetic and copies ran while one was open for 0% of the time, Pallas kernels for 13%

profile of v5, /device:TPU:9, one launch (start us, length us, event | category | flops | bytes accessed | tf_op | source)
XLA Modules:
  0.0 246.8 jit_solution(10676866699662329120)
XLA Ops:
  1.4 3.1 %plan.1 = (s32[8,32,128]{2,1,0:T(8,128)}, bf16[4,512,128]{2,1,0:T(8,128)(2,1)}) custom-call(s32[4]{0:T(128)S(1)} %compare_select_fusion.flip_ref, s32[4,512]{1,0:T(4,128)S(1)} %copy-done), custom_call_target="tpu_custom_call" | custom-call | bytes 663552 | tf_op jit(solution)/shard_map/plan/pallas_call | solution.py:26
  4.5 15.9 %all-to-all-start.1 = ((s32[256,1,128]{2,1,0:T(1,128)}), s32[256,1,128]{2,1,0:T(1,128)}, u32[]{:S(2)}, u32[]{:S(2)}) async-start(s32[256,1,128]{2,1,0:T(1,128)} %bitcast.25), calls=%async_computation.1 | async-start | bytes 262144 | tf_op jit(solution)/shard_map/all_to_all | solution.py:416
  23.5 8.1 %all-to-all-done.1 = s32[256,1,128]{2,1,0:T(1,128)} async-done(((s32[256,1,128]{2,1,0:T(1,128)}), s32[256,1,128]{2,1,0:T(1,128)}, u32[]{:S(2)}, u32[]{:S(2)}) %all-to-all-start.1) | async-done | bytes 131104 | tf_op jit(solution)/shard_map/all_to_all | solution.py:416
  31.6 2.7 %codes.1 = (bf16[1024,128]{1,0:T(8,128)(2,1)}, bf16[2048,128]{1,0:T(8,128)(2,1)S(1)}) custom-call(s32[2]{0:T(128)S(1)} %pad_add_fusion.1.at_ref, s32[8,32,128]{2,1,0:T(8,128)} %bitcast.26.asked_ref), custom_call_target="tpu_custom_call" | custom-call | flops 2000000000 | bytes 917504 | tf_op jit(solution)/shard_map/codes/pallas_call | solution.py:26
  34.3 3.0 %serve.17 = (bf16[256,256]{1,0:T(8,128)(2,1)S(1)}, bf16[256,256]{1,0:T(8,128)(2,1)S(1)}, bf16[256,256]{1,0:T(8,128)(2,1)S(1)}, bf16[256,256]{1,0:T(8,128)(2,1)S(...) custom-call(bf16[2048,256]{1,0:T(8,128)(2,1)S(1)} %copy-done.2, ...), custom_call_target="tpu_custom_call" | custom-call | flops 4000000000 | bytes 2621440 | tf_op jit(solution)/shard_map/serve/pallas_call | solution.py:26
  37.3 209.5 %while.39 = (s32[]{:T(128)}, bf16[2048,256]{1,0:T(8,128)(2,1)}, bf16[1024,128]{1,0:T(8,128)(2,1)}, bf16[256,256]{1,0:T(8,128)(2,1)S(1)}, bf16[256,256]{1,0:T(8,1...) while((s32[]{:T(128)}, bf16[2048,256]{1,0:T(8,128)(2,1)}, ...), condition=%wide.region_9.10_spmd, body=%wide.region_0.9_spmd.sunk | while | flops 13000458240 | bytes 23466492 | solution.py:490
  38.5 19.5 %conditional.2 = (bf16[32,32,256]{2,1,0:T(8,128)(2,1)}) conditional(s32[]{:T(128)} %bitcast.42, (bf16[2048,256]{1,0:T(8,128)(2,1)}, bf16[1024,128]{1,0:T(8,128)(2,1)}, bf16[256,256]{1,0:T(8,128)(2,1)}, bf16[256,256]{1,0:T(8,128)(2,1)S(1)}, bf16[256,256]{1,0:T(8,128)(2,1)S(1)}, ...), branch_computations={%region_1.1_spmd, %region_2.2_spmd, %region_3.3_spmd, %region_4.4_... | conditional | flops 2000458752 | bytes 6947203 | solution.py:359
  39.9 1.3 collective-permute-start.54
  42.5 1.3 collective-permute-start.51
  43.9 4.6 %collective-permute-done.54 = bf16[256,256]{1,0:T(8,128)(2,1)S(1)} collective-permute-done((bf16[256,256]{1,0:T(8,128)(2,1)S(1)}, bf16[256,256]{1,0:T(8,128)(2,1)S(1)}, u32[]{:S(2)}, u32[]{:S(2)}) %collective-permute-start.54) | collective-permute-done | bytes 131104 | tf_op jit(solution)/shard_map/while/body/eval_jaxpr/cond/branch_7_fun/ppermute | solution.py:332
  49.8 3.3 %serve.16 = bf16[1024,256]{1,0:T(8,128)(2,1)} custom-call(bf16[2048,256]{1,0:T(8,128)(2,1)} %get-tuple-element.712.table_ref, bf16[1024,128]{1,0:T(8,128)(2,1)} %get-tuple-element.713.own_code_ref), custom_call_target="tpu_custom_call" | custom-call | flops 2000000000 | bytes 1835008 | tf_op jit(solution)/shard_map/while/body/eval_jaxpr/cond/branch_7_fun/serve/pallas_call | solution.py:26
  54.0 3.2 %collective-permute-done.55 = bf16[256,256]{1,0:T(8,128)(2,1)S(1)} collective-permute-done((bf16[256,256]{1,0:T(8,128)(2,1)S(1)}, bf16[256,256]{1,0:T(8,128)(2,1)S(1)}, u32[]{:S(2)}, u32[]{:S(2)}) %collective-permute-start.55) | collective-permute-done | bytes 131104 | tf_op jit(solution)/shard_map/while/body/eval_jaxpr/cond/branch_7_fun/ppermute | solution.py:345
  58.0 7.4 %all-to-all-start = ((bf16[32,32,256]{2,1,0:T(8,128)(2,1)}), bf16[32,32,256]{2,1,0:T(8,128)(2,1)S(1)}, u32[]{:S(2)}, u32[]{:S(2)}) async-start(bf16[32,32,256]{2,1,0:T(8,128)(2,1)} %get-tuple-element.1121._), calls=%async_computation | async-start | bytes 1048576 | tf_op jit(solution)/shard_map/while/body/eval_jaxpr/all_to_all | solution.py:447
  66.2 4.7 %prep.5 = (f32[512,512]{1,0:T(8,128)S(1)}, bf16[128,512]{1,0:T(8,128)(2,1)S(1)}, bf16[512,512]{1,0:T(8,128)(2,1)S(1)}, bf16[1024,128]{1,0:T(8,128)(2,1)}, bf16[2048,128]{1,0:T(8,128)(2,1)S(1)}) custom-call(s32[2]{0:T(128)S(1)} %pad_add_fusion.3.at_ref, bf16[2048,256]{1,0:T(8,128)(2,1)} %get-tuple-element.1064.table_ref, s32[4,512]{1,0:T(4,128)S(1)} %copy-done.9, ...), custom_call_target="tpu_custom_call" | custom-call | flops 5000000000 | bytes 5137408 | tf_op jit(solution)/shard_map/while/body/eval_jaxpr/prep/pallas_call | solution.py:26
  71.0 10.9 %all-to-all-done = bf16[32,32,256]{2,1,0:T(8,128)(2,1)S(1)} async-done(((bf16[32,32,256]{2,1,0:T(8,128)(2,1)}), bf16[32,32,256]{2,1,0:T(8,128)(2,1)S(1)}, u32[]{:S(2)}, u32[]{:S(2)}) %all-to-all-start) | async-done | bytes 524320 | tf_op jit(solution)/shard_map/while/body/eval_jaxpr/all_to_all | solution.py:447
  81.9 8.8 %update.5 = (bf16[2048,256]{1,0:T(8,128)(2,1)}, bf16[256,256]{1,0:T(8,128)(2,1)S(1)}, bf16[256,256]{1,0:T(8,128)(2,1)S(1)}, bf16[256,256]{1,0:T(8,128)(2,1)S(1)}...) custom-call(s32[2]{0:T(128)S(1)} %pad_add_fusion.3.at_ref, ...), custom_call_target="tpu_custom_call", output_to_operand_aliasing={{0}: (1, {})} | custom-call | flops 6000000000 | bytes 7608320 | tf_op jit(solution)/shard_map/while/body/eval_jaxpr/update/pallas_call | solution.py:26
  91.8 21.1 %conditional.2 = (bf16[32,32,256]{2,1,0:T(8,128)(2,1)}) conditional(s32[]{:T(128)} %bitcast.42, (bf16[2048,256]{1,0:T(8,128)(2,1)}, bf16[1024,128]{1,0:T(8,128)(2,1)}, bf16[256,256]{1,0:T(8,128)(2,1)}, bf16[256,256]{1,0:T(8,128)(2,1)S(1)}, bf16[256,256]{1,0:T(8,128)(2,1)S(1)}, ...), branch_computations={%region_1.1_spmd, %region_2.2_spmd, %region_3.3_spmd, %region_4.4_... | conditional | flops 2000458752 | bytes 6947203 | solution.py:359
  92.5 1.3 collective-permute-start.11
  95.2 1.3 collective-permute-start.8
  97.2 4.7 %collective-permute-done.11 = bf16[256,256]{1,0:T(8,128)(2,1)S(1)} collective-permute-done((bf16[256,256]{1,0:T(8,128)(2,1)S(1)}, bf16[256,256]{1,0:T(8,128)(2,1)S(1)}, u32[]{:S(2)}, u32[]{:S(2)}) %collective-permute-start.11) | collective-permute-done | bytes 131104 | tf_op jit(solution)/shard_map/while/body/eval_jaxpr/cond/branch_1_fun/ppermute | solution.py:332
  101.9 1.3 collective-permute-start.13
  103.2 3.3 %serve.10 = bf16[1024,256]{1,0:T(8,128)(2,1)} custom-call(bf16[2048,256]{1,0:T(8,128)(2,1)} %get-tuple-element.652.table_ref, bf16[1024,128]{1,0:T(8,128)(2,1)} %get-tuple-element.653.own_code_ref), custom_call_target="tpu_custom_call" | custom-call | flops 2000000000 | bytes 1835008 | tf_op jit(solution)/shard_map/while/body/eval_jaxpr/cond/branch_1_fun/serve/pallas_call | solution.py:26
  107.5 4.6 %collective-permute-done.13 = bf16[256,256]{1,0:T(8,128)(2,1)S(1)} collective-permute-done((bf16[256,256]{1,0:T(8,128)(2,1)S(1)}, bf16[256,256]{1,0:T(8,128)(2,1)S(1)}, u32[]{:S(2)}, u32[]{:S(2)}) %collective-permute-start.13) | collective-permute-done | bytes 131104 | tf_op jit(solution)/shard_map/while/body/eval_jaxpr/cond/branch_1_fun/ppermute | solution.py:345
  112.9 5.4 %all-to-all-start = ((bf16[32,32,256]{2,1,0:T(8,128)(2,1)}), bf16[32,32,256]{2,1,0:T(8,128)(2,1)S(1)}, u32[]{:S(2)}, u32[]{:S(2)}) async-start(bf16[32,32,256]{2,1,0:T(8,128)(2,1)} %get-tuple-element.1121._), calls=%async_computation | async-start | bytes 1048576 | tf_op jit(solution)/shard_map/while/body/eval_jaxpr/all_to_all | solution.py:447
  119.1 4.7 %prep.5 = (f32[512,512]{1,0:T(8,128)S(1)}, bf16[128,512]{1,0:T(8,128)(2,1)S(1)}, bf16[512,512]{1,0:T(8,128)(2,1)S(1)}, bf16[1024,128]{1,0:T(8,128)(2,1)}, bf16[2048,128]{1,0:T(8,128)(2,1)S(1)}) custom-call(s32[2]{0:T(128)S(1)} %pad_add_fusion.3.at_ref, bf16[2048,256]{1,0:T(8,128)(2,1)} %get-tuple-element.1064.table_ref, s32[4,512]{1,0:T(4,128)S(1)} %copy-done.9, ...), custom_call_target="tpu_custom_call" | custom-call | flops 5000000000 | bytes 5137408 | tf_op jit(solution)/shard_map/while/body/eval_jaxpr/prep/pallas_call | solution.py:26
  123.9 10.9 %all-to-all-done = bf16[32,32,256]{2,1,0:T(8,128)(2,1)S(1)} async-done(((bf16[32,32,256]{2,1,0:T(8,128)(2,1)}), bf16[32,32,256]{2,1,0:T(8,128)(2,1)S(1)}, u32[]{:S(2)}, u32[]{:S(2)}) %all-to-all-start) | async-done | bytes 524320 | tf_op jit(solution)/shard_map/while/body/eval_jaxpr/all_to_all | solution.py:447
  134.7 8.8 %update.5 = (bf16[2048,256]{1,0:T(8,128)(2,1)}, bf16[256,256]{1,0:T(8,128)(2,1)S(1)}, bf16[256,256]{1,0:T(8,128)(2,1)S(1)}, bf16[256,256]{1,0:T(8,128)(2,1)S(1)}...) custom-call(s32[2]{0:T(128)S(1)} %pad_add_fusion.3.at_ref, ...), custom_call_target="tpu_custom_call", output_to_operand_aliasing={{0}: (1, {})} | custom-call | flops 6000000000 | bytes 7608320 | tf_op jit(solution)/shard_map/while/body/eval_jaxpr/update/pallas_call | solution.py:26
  144.7 24.9 %conditional.2 = (bf16[32,32,256]{2,1,0:T(8,128)(2,1)}) conditional(s32[]{:T(128)} %bitcast.42, (bf16[2048,256]{1,0:T(8,128)(2,1)}, bf16[1024,128]{1,0:T(8,128)(2,1)}, bf16[256,256]{1,0:T(8,128)(2,1)}, bf16[256,256]{1,0:T(8,128)(2,1)S(1)}, bf16[256,256]{1,0:T(8,128)(2,1)S(1)}, ...), branch_computations={%region_1.1_spmd, %region_2.2_spmd, %region_3.3_spmd, %region_4.4_... | conditional | flops 2000458752 | bytes 6947203 | solution.py:359
  146.1 1.3 collective-permute-start.54
  148.8 1.3 collective-permute-start.51
  150.1 8.4 %collective-permute-done.54 = bf16[256,256]{1,0:T(8,128)(2,1)S(1)} collective-permute-done((bf16[256,256]{1,0:T(8,128)(2,1)S(1)}, bf16[256,256]{1,0:T(8,128)(2,1)S(1)}, u32[]{:S(2)}, u32[]{:S(2)}) %collective-permute-start.54) | collective-permute-done | bytes 131104 | tf_op jit(solution)/shard_map/while/body/eval_jaxpr/cond/branch_7_fun/ppermute | solution.py:332
  158.6 1.3 collective-permute-start.55
  159.9 3.3 %serve.16 = bf16[1024,256]{1,0:T(8,128)(2,1)} custom-call(bf16[2048,256]{1,0:T(8,128)(2,1)} %get-tuple-element.712.table_ref, bf16[1024,128]{1,0:T(8,128)(2,1)} %get-tuple-element.713.own_code_ref), custom_call_target="tpu_custom_call" | custom-call | flops 2000000000 | bytes 1835008 | tf_op jit(solution)/shard_map/while/body/eval_jaxpr/cond/branch_7_fun/serve/pallas_call | solution.py:26
  164.1 4.6 %collective-permute-done.55 = bf16[256,256]{1,0:T(8,128)(2,1)S(1)} collective-permute-done((bf16[256,256]{1,0:T(8,128)(2,1)S(1)}, bf16[256,256]{1,0:T(8,128)(2,1)S(1)}, u32[]{:S(2)}, u32[]{:S(2)}) %collective-permute-start.55) | collective-permute-done | bytes 131104 | tf_op jit(solution)/shard_map/while/body/eval_jaxpr/cond/branch_7_fun/ppermute | solution.py:345
  169.6 5.6 %all-to-all-start = ((bf16[32,32,256]{2,1,0:T(8,128)(2,1)}), bf16[32,32,256]{2,1,0:T(8,128)(2,1)S(1)}, u32[]{:S(2)}, u32[]{:S(2)}) async-start(bf16[32,32,256]{2,1,0:T(8,128)(2,1)} %get-tuple-element.1121._), calls=%async_computation | async-start | bytes 1048576 | tf_op jit(solution)/shard_map/while/body/eval_jaxpr/all_to_all | solution.py:447
  175.9 4.7 %prep.5 = (f32[512,512]{1,0:T(8,128)S(1)}, bf16[128,512]{1,0:T(8,128)(2,1)S(1)}, bf16[512,512]{1,0:T(8,128)(2,1)S(1)}, bf16[1024,128]{1,0:T(8,128)(2,1)}, bf16[2048,128]{1,0:T(8,128)(2,1)S(1)}) custom-call(s32[2]{0:T(128)S(1)} %pad_add_fusion.3.at_ref, bf16[2048,256]{1,0:T(8,128)(2,1)} %get-tuple-element.1064.table_ref, s32[4,512]{1,0:T(4,128)S(1)} %copy-done.9, ...), custom_call_target="tpu_custom_call" | custom-call | flops 5000000000 | bytes 5137408 | tf_op jit(solution)/shard_map/while/body/eval_jaxpr/prep/pallas_call | solution.py:26
  180.7 10.9 %all-to-all-done = bf16[32,32,256]{2,1,0:T(8,128)(2,1)S(1)} async-done(((bf16[32,32,256]{2,1,0:T(8,128)(2,1)}), bf16[32,32,256]{2,1,0:T(8,128)(2,1)S(1)}, u32[]{:S(2)}, u32[]{:S(2)}) %all-to-all-start) | async-done | bytes 524320 | tf_op jit(solution)/shard_map/while/body/eval_jaxpr/all_to_all | solution.py:447
  191.5 8.8 %update.5 = (bf16[2048,256]{1,0:T(8,128)(2,1)}, bf16[256,256]{1,0:T(8,128)(2,1)S(1)}, bf16[256,256]{1,0:T(8,128)(2,1)S(1)}, bf16[256,256]{1,0:T(8,128)(2,1)S(1)}...) custom-call(s32[2]{0:T(128)S(1)} %pad_add_fusion.3.at_ref, ...), custom_call_target="tpu_custom_call", output_to_operand_aliasing={{0}: (1, {})} | custom-call | flops 6000000000 | bytes 7608320 | tf_op jit(solution)/shard_map/while/body/eval_jaxpr/update/pallas_call | solution.py:26
  201.5 17.4 %conditional.2 = (bf16[32,32,256]{2,1,0:T(8,128)(2,1)}) conditional(s32[]{:T(128)} %bitcast.42, (bf16[2048,256]{1,0:T(8,128)(2,1)}, bf16[1024,128]{1,0:T(8,128)(2,1)}, bf16[256,256]{1,0:T(8,128)(2,1)}, bf16[256,256]{1,0:T(8,128)(2,1)S(1)}, bf16[256,256]{1,0:T(8,128)(2,1)S(1)}, ...), branch_computations={%region_1.1_spmd, %region_2.2_spmd, %region_3.3_spmd, %region_4.4_... | conditional | flops 2000458752 | bytes 6947203 | solution.py:359
  202.2 1.3 collective-permute-start.4
  204.9 1.3 collective-permute-start.1
  206.9 4.4 %collective-permute-done.4 = bf16[256,256]{1,0:T(8,128)(2,1)S(1)} collective-permute-done((bf16[256,256]{1,0:T(8,128)(2,1)S(1)}, bf16[256,256]{1,0:T(8,128)(2,1)S(1)}, u32[]{:S(2)}, u32[]{:S(2)}) %collective-permute-start.4) | collective-permute-done | bytes 131104 | tf_op jit(solution)/shard_map/while/body/eval_jaxpr/cond/branch_0_fun/ppermute | solution.py:332
  211.3 1.3 collective-permute-start.6
  212.6 3.3 %serve.9 = bf16[1024,256]{1,0:T(8,128)(2,1)} custom-call(bf16[2048,256]{1,0:T(8,128)(2,1)} %get-tuple-element.642.table_ref, bf16[1024,128]{1,0:T(8,128)(2,1)} %get-tuple-element.643.own_code_ref), custom_call_target="tpu_custom_call" | custom-call | flops 2000000000 | bytes 1835008 | tf_op jit(solution)/shard_map/while/body/eval_jaxpr/cond/branch_0_fun/serve/pallas_call | solution.py:26
  218.9 5.0 %all-to-all-start = ((bf16[32,32,256]{2,1,0:T(8,128)(2,1)}), bf16[32,32,256]{2,1,0:T(8,128)(2,1)S(1)}, u32[]{:S(2)}, u32[]{:S(2)}) async-start(bf16[32,32,256]{2,1,0:T(8,128)(2,1)} %get-tuple-element.1121._), calls=%async_computation | async-start | bytes 1048576 | tf_op jit(solution)/shard_map/while/body/eval_jaxpr/all_to_all | solution.py:447
  224.8 4.7 %prep.5 = (f32[512,512]{1,0:T(8,128)S(1)}, bf16[128,512]{1,0:T(8,128)(2,1)S(1)}, bf16[512,512]{1,0:T(8,128)(2,1)S(1)}, bf16[1024,128]{1,0:T(8,128)(2,1)}, bf16[2048,128]{1,0:T(8,128)(2,1)S(1)}) custom-call(s32[2]{0:T(128)S(1)} %pad_add_fusion.3.at_ref, bf16[2048,256]{1,0:T(8,128)(2,1)} %get-tuple-element.1064.table_ref, s32[4,512]{1,0:T(4,128)S(1)} %copy-done.9, ...), custom_call_target="tpu_custom_call" | custom-call | flops 5000000000 | bytes 5137408 | tf_op jit(solution)/shard_map/while/body/eval_jaxpr/prep/pallas_call | solution.py:26
  229.5 10.9 %all-to-all-done = bf16[32,32,256]{2,1,0:T(8,128)(2,1)S(1)} async-done(((bf16[32,32,256]{2,1,0:T(8,128)(2,1)}), bf16[32,32,256]{2,1,0:T(8,128)(2,1)S(1)}, u32[]{:S(2)}, u32[]{:S(2)}) %all-to-all-start) | async-done | bytes 524320 | tf_op jit(solution)/shard_map/while/body/eval_jaxpr/all_to_all | solution.py:447
  240.4 6.5 %update.5 = (bf16[2048,256]{1,0:T(8,128)(2,1)}, bf16[256,256]{1,0:T(8,128)(2,1)S(1)}, bf16[256,256]{1,0:T(8,128)(2,1)S(1)}, bf16[256,256]{1,0:T(8,128)(2,1)S(1)}...) custom-call(s32[2]{0:T(128)S(1)} %pad_add_fusion.3.at_ref, ...), custom_call_target="tpu_custom_call", output_to_operand_aliasing={{0}: (1, {})} | custom-call | flops 6000000000 | bytes 7608320 | tf_op jit(solution)/shard_map/while/body/eval_jaxpr/update/pallas_call | solution.py:26
  (125 shorter events, 30.2 us)
Async XLA Ops:
  0.0 0.7 copy-start.7
  4.5 27.1 %all-to-all-start.1 = ((s32[256,1,128]{2,1,0:T(1,128)}), s32[256,1,128]{2,1,0:T(1,128)}, u32[]{:S(2)}, u32[]{:S(2)}) async-start(s32[256,1,128]{2,1,0:T(1,128)} %bitcast.25), calls=%async_computation.1 | async-start | bytes 262144 | tf_op jit(solution)/shard_map/all_to_all | solution.py:416
  21.2 1.2 copy-start.1
  31.6 2.7 %copy-start.2 = (bf16[2048,256]{1,0:T(8,128)(2,1)S(1)}, bf16[2048,256]{1,0:T(8,128)(2,1)}, u32[]{:S(2)}) copy-start(bf16[2048,256]{1,0:T(8,128)(2,1)} %table_ref.1) | copy-start | bytes 3145732
  38.5 4.0 %collective-permute-start.52 = (bf16[256,256]{1,0:T(8,128)(2,1)S(1)}, bf16[256,256]{1,0:T(8,128)(2,1)S(1)}, u32[]{:S(2)}, u32[]{:S(2)}) collective-permute-start(bf16[256,256]{1,0:T(8,128)(2,1)S(1)} %get-tuple-element.718), channel_id=1, source_target_pairs={{192,128},{224,160},{193,129},{225,161},{194,130},{226,162},{195,1... | collective-permute-start | bytes 393224 | tf_op jit(solution)/shard_map/while/body/eval_jaxpr/cond/branch_7_fun/ppermute | solution.py:332
  39.2 4.7 %collective-permute-start.53 = (bf16[256,256]{1,0:T(8,128)(2,1)S(1)}, bf16[256,256]{1,0:T(8,128)(2,1)S(1)}, u32[]{:S(2)}, u32[]{:S(2)}) collective-permute-start(bf16[256,256]{1,0:T(8,128)(2,1)S(1)} %get-tuple-element.719), channel_id=1, source_target_pairs={{192,0},{224,32},{193,1},{225,33},{194,2},{226,34},{195,3},{227,35... | collective-permute-start | bytes 393224 | tf_op jit(solution)/shard_map/while/body/eval_jaxpr/cond/branch_7_fun/ppermute | solution.py:332
  39.9 8.6 %collective-permute-start.54 = (bf16[256,256]{1,0:T(8,128)(2,1)S(1)}, bf16[256,256]{1,0:T(8,128)(2,1)S(1)}, u32[]{:S(2)}, u32[]{:S(2)}) collective-permute-start(bf16[256,256]{1,0:T(8,128)(2,1)S(1)} %get-tuple-element.720), channel_id=1, source_target_pairs={{192,64},{224,96},{193,65},{225,97},{194,66},{226,98},{195,67},{22... | collective-permute-start | bytes 393224 | tf_op jit(solution)/shard_map/while/body/eval_jaxpr/cond/branch_7_fun/ppermute | solution.py:332
  41.2 11.9 %collective-permute-start.49 = (bf16[256,256]{1,0:T(8,128)(2,1)S(1)}, bf16[256,256]{1,0:T(8,128)(2,1)S(1)}, u32[]{:S(2)}, u32[]{:S(2)}) collective-permute-start(bf16[256,256]{1,0:T(8,128)(2,1)S(1)} %get-tuple-element.714), channel_id=1, source_target_pairs={{192,128},{224,160},{193,129},{225,161},{194,130},{226,162},{195,1... | collective-permute-start | bytes 393224 | tf_op jit(solution)/shard_map/while/body/eval_jaxpr/cond/branch_7_fun/ppermute | solution.py:332
  41.8 11.3 %collective-permute-start.50 = (bf16[256,256]{1,0:T(8,128)(2,1)S(1)}, bf16[256,256]{1,0:T(8,128)(2,1)S(1)}, u32[]{:S(2)}, u32[]{:S(2)}) collective-permute-start(bf16[256,256]{1,0:T(8,128)(2,1)S(1)} %get-tuple-element.715), channel_id=1, source_target_pairs={{192,0},{224,32},{193,1},{225,33},{194,2},{226,34},{195,3},{227,35... | collective-permute-start | bytes 393224 | tf_op jit(solution)/shard_map/while/body/eval_jaxpr/cond/branch_7_fun/ppermute | solution.py:332
  42.5 11.5 %collective-permute-start.51 = (bf16[256,256]{1,0:T(8,128)(2,1)S(1)}, bf16[256,256]{1,0:T(8,128)(2,1)S(1)}, u32[]{:S(2)}, u32[]{:S(2)}) collective-permute-start(bf16[256,256]{1,0:T(8,128)(2,1)S(1)} %get-tuple-element.716), channel_id=1, source_target_pairs={{192,64},{224,96},{193,65},{225,97},{194,66},{226,98},{195,67},{22... | collective-permute-start | bytes 393224 | tf_op jit(solution)/shard_map/while/body/eval_jaxpr/cond/branch_7_fun/ppermute | solution.py:332
  48.5 8.8 %collective-permute-start.55 = (bf16[256,256]{1,0:T(8,128)(2,1)S(1)}, bf16[256,256]{1,0:T(8,128)(2,1)S(1)}, u32[]{:S(2)}, u32[]{:S(2)}) collective-permute-start(bf16[256,256]{1,0:T(8,128)(2,1)S(1)} %select_select_fusion.7), channel_id=1, source_target_pairs={{32,24},{33,25},{34,26},{35,27},{36,28},{37,29},{38,30},{39,31},{4... | collective-permute-start | bytes 393224 | tf_op jit(solution)/shard_map/while/body/eval_jaxpr/cond/branch_7_fun/ppermute | solution.py:345
  58.0 7.5 %copy-start.8 = (bf16[4,512,128]{2,1,0:T(8,128)(2,1)S(1)}, bf16[4,512,128]{2,1,0:T(8,128)(2,1)}, u32[]{:S(2)}) copy-start(bf16[4,512,128]{2,1,0:T(8,128)(2,1)} %get-tuple-element.1108.edge_ref) | copy-start | bytes 1572868 | tf_op jit(solution)/shard_map/while
  58.0 7.5 %copy-start.12 = (s32[1,2048]{1,0:T(1,128)S(1)}, s32[1,2048]{1,0:T(1,128)}, u32[]{:S(2)}) copy-start(s32[1,2048]{1,0:T(1,128)} %get-tuple-element.1107.node_time_ref) | copy-start | bytes 24580 | tf_op jit(solution)/shard_map/while
  58.0 23.8 %all-to-all-start = ((bf16[32,32,256]{2,1,0:T(8,128)(2,1)}), bf16[32,32,256]{2,1,0:T(8,128)(2,1)S(1)}, u32[]{:S(2)}, u32[]{:S(2)}) async-start(bf16[32,32,256]{2,1,0:T(8,128)(2,1)} %get-tuple-element.1121._), calls=%async_computation | async-start | bytes 1048576 | tf_op jit(solution)/shard_map/while/body/eval_jaxpr/all_to_all | solution.py:447
  65.5 0.7 copy-start.14
  91.8 4.6 %collective-permute-start.10 = (bf16[256,256]{1,0:T(8,128)(2,1)}, bf16[256,256]{1,0:T(8,128)(2,1)S(1)}, u32[]{:S(2)}, u32[]{:S(2)}) collective-permute-start(bf16[256,256]{1,0:T(8,128)(2,1)} %get-tuple-element.658), channel_id=1, source_target_pairs={{0,192},{32,224},{1,193},{33,225},{2,194},{34,226},{3,195},{35,227... | collective-permute-start | bytes 393224 | tf_op jit(solution)/shard_map/while/body/eval_jaxpr/cond/branch_1_fun/ppermute | solution.py:332
  92.5 9.3 %collective-permute-start.11 = (bf16[256,256]{1,0:T(8,128)(2,1)S(1)}, bf16[256,256]{1,0:T(8,128)(2,1)S(1)}, u32[]{:S(2)}, u32[]{:S(2)}) collective-permute-start(bf16[256,256]{1,0:T(8,128)(2,1)S(1)} %get-tuple-element.659), channel_id=1, source_target_pairs={{0,64},{32,96},{1,65},{33,97},{2,66},{34,98},{3,67},{35,99},{4,68}... | collective-permute-start | bytes 393224 | tf_op jit(solution)/shard_map/while/body/eval_jaxpr/cond/branch_1_fun/ppermute | solution.py:332
  93.8 8.0 %collective-permute-start.12 = (bf16[256,256]{1,0:T(8,128)(2,1)S(1)}, bf16[256,256]{1,0:T(8,128)(2,1)S(1)}, u32[]{:S(2)}, u32[]{:S(2)}) collective-permute-start(bf16[256,256]{1,0:T(8,128)(2,1)S(1)} %get-tuple-element.660), channel_id=1, source_target_pairs={{0,128},{32,160},{1,129},{33,161},{2,130},{34,162},{3,131},{35,163... | collective-permute-start | bytes 393224 | tf_op jit(solution)/shard_map/while/body/eval_jaxpr/cond/branch_1_fun/ppermute | solution.py:332
  94.5 12.0 %collective-permute-start.7 = (bf16[256,256]{1,0:T(8,128)(2,1)}, bf16[256,256]{1,0:T(8,128)(2,1)S(1)}, u32[]{:S(2)}, u32[]{:S(2)}) collective-permute-start(bf16[256,256]{1,0:T(8,128)(2,1)} %get-tuple-element.654), channel_id=1, source_target_pairs={{0,192},{32,224},{1,193},{33,225},{2,194},{34,226},{3,195},{35,227... | collective-permute-start | bytes 393224 | tf_op jit(solution)/shard_map/while/body/eval_jaxpr/cond/branch_1_fun/ppermute | solution.py:332
  95.2 12.3 %collective-permute-start.8 = (bf16[256,256]{1,0:T(8,128)(2,1)S(1)}, bf16[256,256]{1,0:T(8,128)(2,1)S(1)}, u32[]{:S(2)}, u32[]{:S(2)}) collective-permute-start(bf16[256,256]{1,0:T(8,128)(2,1)S(1)} %get-tuple-element.655), channel_id=1, source_target_pairs={{0,64},{32,96},{1,65},{33,97},{2,66},{34,98},{3,67},{35,99},{4,68}... | collective-permute-start | bytes 393224 | tf_op jit(solution)/shard_map/while/body/eval_jaxpr/cond/branch_1_fun/ppermute | solution.py:332
  96.5 11.0 %collective-permute-start.9 = (bf16[256,256]{1,0:T(8,128)(2,1)S(1)}, bf16[256,256]{1,0:T(8,128)(2,1)S(1)}, u32[]{:S(2)}, u32[]{:S(2)}) collective-permute-start(bf16[256,256]{1,0:T(8,128)(2,1)S(1)} %get-tuple-element.656), channel_id=1, source_target_pairs={{0,128},{32,160},{1,129},{33,161},{2,130},{34,162},{3,131},{35,163... | collective-permute-start | bytes 393224 | tf_op jit(solution)/shard_map/while/body/eval_jaxpr/cond/branch_1_fun/ppermute | solution.py:332
  101.9 10.2 %collective-permute-start.13 = (bf16[256,256]{1,0:T(8,128)(2,1)S(1)}, bf16[256,256]{1,0:T(8,128)(2,1)S(1)}, u32[]{:S(2)}, u32[]{:S(2)}) collective-permute-start(bf16[256,256]{1,0:T(8,128)(2,1)S(1)} %select_select_fusion.1), channel_id=1, source_target_pairs={{32,24},{33,25},{34,26},{35,27},{36,28},{37,29},{38,30},{39,31},{4... | collective-permute-start | bytes 393224 | tf_op jit(solution)/shard_map/while/body/eval_jaxpr/cond/branch_1_fun/ppermute | solution.py:345
  112.9 5.5 %copy-start.8 = (bf16[4,512,128]{2,1,0:T(8,128)(2,1)S(1)}, bf16[4,512,128]{2,1,0:T(8,128)(2,1)}, u32[]{:S(2)}) copy-start(bf16[4,512,128]{2,1,0:T(8,128)(2,1)} %get-tuple-element.1108.edge_ref) | copy-start | bytes 1572868 | tf_op jit(solution)/shard_map/while
  112.9 5.5 %copy-start.12 = (s32[1,2048]{1,0:T(1,128)S(1)}, s32[1,2048]{1,0:T(1,128)}, u32[]{:S(2)}) copy-start(s32[1,2048]{1,0:T(1,128)} %get-tuple-element.1107.node_time_ref) | copy-start | bytes 24580 | tf_op jit(solution)/shard_map/while
  112.9 21.8 %all-to-all-start = ((bf16[32,32,256]{2,1,0:T(8,128)(2,1)}), bf16[32,32,256]{2,1,0:T(8,128)(2,1)S(1)}, u32[]{:S(2)}, u32[]{:S(2)}) async-start(bf16[32,32,256]{2,1,0:T(8,128)(2,1)} %get-tuple-element.1121._), calls=%async_computation | async-start | bytes 1048576 | tf_op jit(solution)/shard_map/while/body/eval_jaxpr/all_to_all | solution.py:447
  118.4 0.7 copy-start.14
  144.7 4.0 %collective-permute-start.52 = (bf16[256,256]{1,0:T(8,128)(2,1)S(1)}, bf16[256,256]{1,0:T(8,128)(2,1)S(1)}, u32[]{:S(2)}, u32[]{:S(2)}) collective-permute-start(bf16[256,256]{1,0:T(8,128)(2,1)S(1)} %get-tuple-element.718), channel_id=1, source_target_pairs={{192,128},{224,160},{193,129},{225,161},{194,130},{226,162},{195,1... | collective-permute-start | bytes 393224 | tf_op jit(solution)/shard_map/while/body/eval_jaxpr/cond/branch_7_fun/ppermute | solution.py:332
  145.4 4.7 %collective-permute-start.53 = (bf16[256,256]{1,0:T(8,128)(2,1)S(1)}, bf16[256,256]{1,0:T(8,128)(2,1)S(1)}, u32[]{:S(2)}, u32[]{:S(2)}) collective-permute-start(bf16[256,256]{1,0:T(8,128)(2,1)S(1)} %get-tuple-element.719), channel_id=1, source_target_pairs={{192,0},{224,32},{193,1},{225,33},{194,2},{226,34},{195,3},{227,35... | collective-permute-start | bytes 393224 | tf_op jit(solution)/shard_map/while/body/eval_jaxpr/cond/branch_7_fun/ppermute | solution.py:332
  146.1 12.4 %collective-permute-start.54 = (bf16[256,256]{1,0:T(8,128)(2,1)S(1)}, bf16[256,256]{1,0:T(8,128)(2,1)S(1)}, u32[]{:S(2)}, u32[]{:S(2)}) collective-permute-start(bf16[256,256]{1,0:T(8,128)(2,1)S(1)} %get-tuple-element.720), channel_id=1, source_target_pairs={{192,64},{224,96},{193,65},{225,97},{194,66},{226,98},{195,67},{22... | collective-permute-start | bytes 393224 | tf_op jit(solution)/shard_map/while/body/eval_jaxpr/cond/branch_7_fun/ppermute | solution.py:332
  147.4 15.8 %collective-permute-start.49 = (bf16[256,256]{1,0:T(8,128)(2,1)S(1)}, bf16[256,256]{1,0:T(8,128)(2,1)S(1)}, u32[]{:S(2)}, u32[]{:S(2)}) collective-permute-start(bf16[256,256]{1,0:T(8,128)(2,1)S(1)} %get-tuple-element.714), channel_id=1, source_target_pairs={{192,128},{224,160},{193,129},{225,161},{194,130},{226,162},{195,1... | collective-permute-start | bytes 393224 | tf_op jit(solution)/shard_map/while/body/eval_jaxpr/cond/branch_7_fun/ppermute | solution.py:332
  148.1 15.1 %collective-permute-start.50 = (bf16[256,256]{1,0:T(8,128)(2,1)S(1)}, bf16[256,256]{1,0:T(8,128)(2,1)S(1)}, u32[]{:S(2)}, u32[]{:S(2)}) collective-permute-start(bf16[256,256]{1,0:T(8,128)(2,1)S(1)} %get-tuple-element.715), channel_id=1, source_target_pairs={{192,0},{224,32},{193,1},{225,33},{194,2},{226,34},{195,3},{227,35... | collective-permute-start | bytes 393224 | tf_op jit(solution)/shard_map/while/body/eval_jaxpr/cond/branch_7_fun/ppermute | solution.py:332
  148.8 15.3 %collective-permute-start.51 = (bf16[256,256]{1,0:T(8,128)(2,1)S(1)}, bf16[256,256]{1,0:T(8,128)(2,1)S(1)}, u32[]{:S(2)}, u32[]{:S(2)}) collective-permute-start(bf16[256,256]{1,0:T(8,128)(2,1)S(1)} %get-tuple-element.716), channel_id=1, source_target_pairs={{192,64},{224,96},{193,65},{225,97},{194,66},{226,98},{195,67},{22... | collective-permute-start | bytes 393224 | tf_op jit(solution)/shard_map/while/body/eval_jaxpr/cond/branch_7_fun/ppermute | solution.py:332
  158.6 10.2 %collective-permute-start.55 = (bf16[256,256]{1,0:T(8,128)(2,1)S(1)}, bf16[256,256]{1,0:T(8,128)(2,1)S(1)}, u32[]{:S(2)}, u32[]{:S(2)}) collective-permute-start(bf16[256,256]{1,0:T(8,128)(2,1)S(1)} %select_select_fusion.7), channel_id=1, source_target_pairs={{32,24},{33,25},{34,26},{35,27},{36,28},{37,29},{38,30},{39,31},{4... | collective-permute-start | bytes 393224 | tf_op jit(solution)/shard_map/while/body/eval_jaxpr/cond/branch_7_fun/ppermute | solution.py:345
  169.6 5.7 %copy-start.8 = (bf16[4,512,128]{2,1,0:T(8,128)(2,1)S(1)}, bf16[4,512,128]{2,1,0:T(8,128)(2,1)}, u32[]{:S(2)}) copy-start(bf16[4,512,128]{2,1,0:T(8,128)(2,1)} %get-tuple-element.1108.edge_ref) | copy-start | bytes 1572868 | tf_op jit(solution)/shard_map/while
  169.6 5.7 %copy-start.12 = (s32[1,2048]{1,0:T(1,128)S(1)}, s32[1,2048]{1,0:T(1,128)}, u32[]{:S(2)}) copy-start(s32[1,2048]{1,0:T(1,128)} %get-tuple-element.1107.node_time_ref) | copy-start | bytes 24580 | tf_op jit(solution)/shard_map/while
  169.6 22.0 %all-to-all-start = ((bf16[32,32,256]{2,1,0:T(8,128)(2,1)}), bf16[32,32,256]{2,1,0:T(8,128)(2,1)S(1)}, u32[]{:S(2)}, u32[]{:S(2)}) async-start(bf16[32,32,256]{2,1,0:T(8,128)(2,1)} %get-tuple-element.1121._), calls=%async_computation | async-start | bytes 1048576 | tf_op jit(solution)/shard_map/while/body/eval_jaxpr/all_to_all | solution.py:447
  175.2 0.7 copy-start.14
  201.5 4.6 %collective-permute-start.3 = (bf16[256,256]{1,0:T(8,128)(2,1)}, bf16[256,256]{1,0:T(8,128)(2,1)S(1)}, u32[]{:S(2)}, u32[]{:S(2)}) collective-permute-start(bf16[256,256]{1,0:T(8,128)(2,1)} %get-tuple-element.648), channel_id=1, source_target_pairs={{0,192},{32,224},{1,193},{33,225},{2,194},{34,226},{3,195},{35,227... | collective-permute-start | bytes 393224 | tf_op jit(solution)/shard_map/while/body/eval_jaxpr/cond/branch_0_fun/ppermute | solution.py:332
  202.2 9.1 %collective-permute-start.4 = (bf16[256,256]{1,0:T(8,128)(2,1)S(1)}, bf16[256,256]{1,0:T(8,128)(2,1)S(1)}, u32[]{:S(2)}, u32[]{:S(2)}) collective-permute-start(bf16[256,256]{1,0:T(8,128)(2,1)S(1)} %get-tuple-element.649), channel_id=1, source_target_pairs={{0,64},{32,96},{1,65},{33,97},{2,66},{34,98},{3,67},{35,99},{4,68}... | collective-permute-start | bytes 393224 | tf_op jit(solution)/shard_map/while/body/eval_jaxpr/cond/branch_0_fun/ppermute | solution.py:332
  203.5 7.8 %collective-permute-start.5 = (bf16[256,256]{1,0:T(8,128)(2,1)S(1)}, bf16[256,256]{1,0:T(8,128)(2,1)S(1)}, u32[]{:S(2)}, u32[]{:S(2)}) collective-permute-start(bf16[256,256]{1,0:T(8,128)(2,1)S(1)} %get-tuple-element.650), channel_id=1, source_target_pairs={{0,128},{32,160},{1,129},{33,161},{2,130},{34,162},{3,131},{35,163... | collective-permute-start | bytes 393224 | tf_op jit(solution)/shard_map/while/body/eval_jaxpr/cond/branch_0_fun/ppermute | solution.py:332
  204.2 11.7 %collective-permute-start = (bf16[256,256]{1,0:T(8,128)(2,1)}, bf16[256,256]{1,0:T(8,128)(2,1)S(1)}, u32[]{:S(2)}, u32[]{:S(2)}) collective-permute-start(bf16[256,256]{1,0:T(8,128)(2,1)} %get-tuple-element.644), channel_id=1, source_target_pairs={{0,192},{32,224},{1,193},{33,225},{2,194},{34,226},{3,195},{35,227... | collective-permute-start | bytes 393224 | tf_op jit(solution)/shard_map/while/body/eval_jaxpr/cond/branch_0_fun/ppermute | solution.py:332
  204.9 12.0 %collective-permute-start.1 = (bf16[256,256]{1,0:T(8,128)(2,1)S(1)}, bf16[256,256]{1,0:T(8,128)(2,1)S(1)}, u32[]{:S(2)}, u32[]{:S(2)}) collective-permute-start(bf16[256,256]{1,0:T(8,128)(2,1)S(1)} %get-tuple-element.645), channel_id=1, source_target_pairs={{0,64},{32,96},{1,65},{33,97},{2,66},{34,98},{3,67},{35,99},{4,68}... | collective-permute-start | bytes 393224 | tf_op jit(solution)/shard_map/while/body/eval_jaxpr/cond/branch_0_fun/ppermute | solution.py:332
  206.2 10.7 %collective-permute-start.2 = (bf16[256,256]{1,0:T(8,128)(2,1)S(1)}, bf16[256,256]{1,0:T(8,128)(2,1)S(1)}, u32[]{:S(2)}, u32[]{:S(2)}) collective-permute-start(bf16[256,256]{1,0:T(8,128)(2,1)S(1)} %get-tuple-element.646), channel_id=1, source_target_pairs={{0,128},{32,160},{1,129},{33,161},{2,130},{34,162},{3,131},{35,163... | collective-permute-start | bytes 393224 | tf_op jit(solution)/shard_map/while/body/eval_jaxpr/cond/branch_0_fun/ppermute | solution.py:332
  211.3 6.8 %collective-permute-start.6 = (bf16[256,256]{1,0:T(8,128)(2,1)S(1)}, bf16[256,256]{1,0:T(8,128)(2,1)S(1)}, u32[]{:S(2)}, u32[]{:S(2)}) collective-permute-start(bf16[256,256]{1,0:T(8,128)(2,1)S(1)} %select_select_fusion), channel_id=1, source_target_pairs={{0,56},{1,57},{2,58},{3,59},{4,60},{5,61},{6,62},{7,63},{8,48},{9,... | collective-permute-start | bytes 393224 | tf_op jit(solution)/shard_map/while/body/eval_jaxpr/cond/branch_0_fun/ppermute | solution.py:345
  218.9 5.2 %copy-start.8 = (bf16[4,512,128]{2,1,0:T(8,128)(2,1)S(1)}, bf16[4,512,128]{2,1,0:T(8,128)(2,1)}, u32[]{:S(2)}) copy-start(bf16[4,512,128]{2,1,0:T(8,128)(2,1)} %get-tuple-element.1108.edge_ref) | copy-start | bytes 1572868 | tf_op jit(solution)/shard_map/while
  218.9 5.2 %copy-start.12 = (s32[1,2048]{1,0:T(1,128)S(1)}, s32[1,2048]{1,0:T(1,128)}, u32[]{:S(2)}) copy-start(s32[1,2048]{1,0:T(1,128)} %get-tuple-element.1107.node_time_ref) | copy-start | bytes 24580 | tf_op jit(solution)/shard_map/while
  218.9 21.5 %all-to-all-start = ((bf16[32,32,256]{2,1,0:T(8,128)(2,1)}), bf16[32,32,256]{2,1,0:T(8,128)(2,1)S(1)}, u32[]{:S(2)}, u32[]{:S(2)}) async-start(bf16[32,32,256]{2,1,0:T(8,128)(2,1)} %get-tuple-element.1121._), calls=%async_computation | async-start | bytes 1048576 | tf_op jit(solution)/shard_map/while/body/eval_jaxpr/all_to_all | solution.py:447
  224.1 0.7 copy-start.14
  (18 other events, 12.5 us)
